TPU v7x, 128 devices: a whole 4x4x4 slice. The times are simulated.
128 devices in a mesh: sec: 4 (over x), row: 32 (over y, z, core).
Axes of the slice: x: 4, y: 4, z: 4, core: 2. Of those that a mesh axis runs over, the one named last changes fastest.
Arguments:
- index_slices: float32 [4, 1024, 1024], P('sec', 'row'), may hold values from -6 to 6
- core_mask: int32 [1024, 1024], P('row'), may hold values 0 or 1
- illum_amp: float32 [1024, 1024], P('row'), may hold values from 0.5 to 1.5
- measured: float32 [8, 1024, 2, 1024], P(None, 'row'), may hold values from -6 to 6
- wave_ids: int32 [8], replicated, may hold values from 0 to 63
- angle_ids: int32 [8], replicated, may hold values from 0 to 63
Outputs:
- index_grad: float32 [4, 1024, 1024], P('sec', 'row')
All inputs are finite; a program needn't handle non-finite values. No bound on the sum of `core_mask` on one device may be relied on, other than what follows from the above.
Results may differ from a plain program's by a relative error of at most 0.0003.
Values sent between devices are 32-bit elements; how exact they have to be, the bound alone decides.
No kernel may reach another device: no remote copies, remote signals or barrier semaphores. Data moves between devices by JAX's collectives and lax.ppermute only.
A program may use at most 256 MiB of HBM per device.

v0:
```python
import math

import jax
import jax.numpy as jnp
from jax import lax
from jax.sharding import PartitionSpec as P

FA = 8


ratio_base = 0.75
ratio_step = 1.0 / 128.0
prop_scale = 150.0
core_step = 0.8
tilt_step = 8
angle_side = 8
precise = lax.Precision.HIGHEST


def contract(form, left_op, right_op):
    return jnp.einsum(
        form, left_op, right_op, precision=precise, preferred_element_type=jnp.float32
    )


def dft_pair(length, sign):
    counter = jnp.arange(length, dtype=jnp.int32)
    product = counter[:, None] * counter[None, :] % length
    angle = sign * 2.0 * math.pi / length * product.astype(jnp.float32)
    return (jnp.cos(angle), jnp.sin(angle))


def twiddle_pair(outer_len, inner_len, sign):
    total = outer_len * inner_len
    product = (
        jnp.arange(outer_len, dtype=jnp.int32)[:, None]
        * jnp.arange(inner_len, dtype=jnp.int32)[None, :]
        % total
    )
    angle = sign * 2.0 * math.pi / total * product.astype(jnp.float32)
    return (jnp.cos(angle), jnp.sin(angle))


def turn_rows(values):
    return jnp.concatenate([-values[:, :, 1:], values[:, :, :1]], axis=2)


def turn_cols(values):
    middle = values.shape[-1] // 2
    return jnp.concatenate([-values[..., middle:], values[..., :middle]], axis=-1)


def rows_forward(wave_field):
    batches, height, channels, breadth = wave_field.shape
    inner_len = breadth // FA
    outer_re, outer_im = dft_pair(FA, -1.0)
    twist_re, twist_im = twiddle_pair(FA, inner_len, -1.0)
    inner_re, inner_im = dft_pair(inner_len, -1.0)
    segmented = wave_field.reshape(batches, height, channels, FA, inner_len)
    segmented = contract("kn,bycnm->byckm", outer_re, segmented) + contract(
        "kn,bycnm->byckm", outer_im, turn_rows(segmented)
    )
    segmented = segmented * twist_re + turn_rows(segmented) * twist_im
    segmented = contract("bycnm,ml->bycnl", segmented, inner_re) + contract(
        "bycnm,ml->bycnl", turn_rows(segmented), inner_im
    )
    return segmented.reshape(batches, height, channels, breadth)


def rows_inverse(spectrum):
    batches, height, channels, breadth = spectrum.shape
    inner_len = breadth // FA
    outer_re, outer_im = dft_pair(FA, 1.0)
    twist_re, twist_im = twiddle_pair(FA, inner_len, 1.0)
    inner_re, inner_im = dft_pair(inner_len, 1.0)
    segmented = spectrum.reshape(batches, height, channels, FA, inner_len)
    segmented = contract("bycnm,ml->bycnl", segmented, inner_re) + contract(
        "bycnm,ml->bycnl", turn_rows(segmented), inner_im
    )
    segmented = segmented * twist_re + turn_rows(segmented) * twist_im
    segmented = contract("kn,bycnm->byckm", outer_re, segmented) + contract(
        "kn,bycnm->byckm", outer_im, turn_rows(segmented)
    )
    return segmented.reshape(batches, height, channels, breadth) * (1.0 / breadth)


def cols_forward(merged):
    batches, height, lanes = merged.shape
    inner_len = height // FA
    outer_re, outer_im = dft_pair(FA, -1.0)
    twist_re, twist_im = twiddle_pair(FA, inner_len, -1.0)
    inner_re, inner_im = dft_pair(inner_len, -1.0)
    segmented = merged.reshape(batches, FA, inner_len, lanes)
    segmented = contract("kn,bnmc->bkmc", outer_re, segmented) + contract(
        "kn,bnmc->bkmc", outer_im, turn_cols(segmented)
    )
    segmented = segmented * twist_re[:, :, None] + turn_cols(segmented) * twist_im[:, :, None]
    segmented = contract("bknc,nl->bklc", segmented, inner_re) + contract(
        "bknc,nl->bklc", turn_cols(segmented), inner_im
    )
    return segmented.reshape(batches, height, lanes)


def cols_inverse(merged):
    batches, height, lanes = merged.shape
    inner_len = height // FA
    outer_re, outer_im = dft_pair(FA, 1.0)
    twist_re, twist_im = twiddle_pair(FA, inner_len, 1.0)
    inner_re, inner_im = dft_pair(inner_len, 1.0)
    segmented = merged.reshape(batches, FA, inner_len, lanes)
    segmented = contract("bknc,nl->bklc", segmented, inner_re) + contract(
        "bknc,nl->bklc", turn_cols(segmented), inner_im
    )
    segmented = segmented * twist_re[:, :, None] + turn_cols(segmented) * twist_im[:, :, None]
    segmented = contract("kn,bnmc->bkmc", outer_re, segmented) + contract(
        "kn,bnmc->bkmc", outer_im, turn_cols(segmented)
    )
    return segmented.reshape(batches, height, lanes) * (1.0 / height)


def freq_square(positions, grid_size):
    inner_len = grid_size // FA
    natural = positions // inner_len + FA * (positions % inner_len)
    signed = jnp.where(natural < grid_size // 2, natural, natural - grid_size)
    scaled = signed.astype(jnp.float32) / (grid_size // 2)
    return scaled * scaled


def propagate(wave_field, ratios_now, sign, freq_grid):
    spectrum = rows_forward(wave_field)
    columns = lax.all_to_all(spectrum, "row", split_axis=3, concat_axis=1, tiled=True)
    batches, height, channels, narrow = columns.shape
    merged = cols_forward(columns.reshape(batches, height, channels * narrow))
    scale_now = -prop_scale * ratios_now
    angle = scale_now[:, None, None] * freq_grid[None]
    cos_part = jnp.cos(angle)
    sin_part = sign * jnp.sin(angle)
    cos_both = jnp.concatenate([cos_part, cos_part], axis=-1)
    sin_both = jnp.concatenate([sin_part, sin_part], axis=-1)
    merged = merged * cos_both + turn_cols(merged) * sin_both
    merged = cols_inverse(merged)
    returned = lax.all_to_all(
        merged.reshape(batches, height, channels, narrow),
        "row",
        split_axis=1,
        concat_axis=3,
        tiled=True,
    )
    return rows_inverse(returned)


def screen(wave_field, layer_slice, mask_float, ratios_now, sign):
    phase = (core_step * mask_float + layer_slice)[None] / ratios_now[:, None, None]
    cos_part = jnp.cos(phase)[:, :, None, :]
    sin_part = (sign * jnp.sin(phase))[:, :, None, :]
    return wave_field * cos_part + turn_rows(wave_field) * sin_part


def forward_pass(wave_field, ratios_now, slices, mask_float, freq_grid):
    kept_fields = []
    depth_now = slices.shape[0]
    for layer_index in range(depth_now):
        wave_field = propagate(wave_field, ratios_now, 1.0, freq_grid)
        wave_field = screen(wave_field, slices[layer_index], mask_float, ratios_now, 1.0)
        kept_fields.append(wave_field)
    return (wave_field, kept_fields)


def adjoint_pass(adjoint, ratios_now, slices, mask_float, freq_grid, kept_fields):
    depth_now = slices.shape[0]
    grad_terms = [None] * depth_now
    for layer_index in reversed(range(depth_now)):
        forward_now = kept_fields[layer_index]
        product = adjoint[:, :, 1] * forward_now[:, :, 0] - adjoint[:, :, 0] * forward_now[:, :, 1]
        grad_terms[layer_index] = jnp.sum(product / ratios_now[:, None, None], axis=0)
        adjoint = screen(adjoint, slices[layer_index], mask_float, ratios_now, -1.0)
        adjoint = propagate(adjoint, ratios_now, -1.0, freq_grid)
    return (adjoint, grad_terms)


def rows_of_grads(grad_terms):
    return jnp.stack(grad_terms, axis=0)


def illuminate(amplitude, angle_pick, row_pos):
    row_count, grid_size = amplitude.shape
    y_coord = row_pos * row_count + jnp.arange(row_count, dtype=jnp.int32)
    x_coord = jnp.arange(grid_size, dtype=jnp.int32)
    tilt_x = (angle_pick % angle_side - angle_side // 2) * tilt_step
    tilt_y = (angle_pick // angle_side - angle_side // 2) * tilt_step
    product = (
        tilt_x[:, None, None] * x_coord[None, None, :]
        + tilt_y[:, None, None] * y_coord[None, :, None]
    ) % grid_size
    phase = 2.0 * math.pi / grid_size * product.astype(jnp.float32)
    return jnp.stack([amplitude * jnp.cos(phase), amplitude * jnp.sin(phase)], axis=2)


def body(index_slices, core_mask, illum_amp, measured, wave_ids, angle_ids):
    row_count, grid_size = core_mask.shape
    wave_total = wave_ids.shape[0]
    row_pos = lax.axis_index("row")
    sec_pos = lax.axis_index("sec")
    sec_count = lax.axis_size("sec")
    narrow = grid_size // lax.axis_size("row")
    mask_float = core_mask.astype(jnp.float32)
    ratios = ratio_base + ratio_step * wave_ids.astype(jnp.float32)
    all_rows = freq_square(jnp.arange(grid_size, dtype=jnp.int32), grid_size)
    own_cols = freq_square(row_pos * narrow + jnp.arange(narrow, dtype=jnp.int32), grid_size)
    freq_grid = all_rows[:, None] + own_cols[None, :]
    every_slice = lax.all_gather(index_slices, "sec", axis=0, tiled=True)
    share = wave_total // sec_count
    first_wave = sec_pos * share
    ratio_pick = lax.dynamic_slice_in_dim(ratios, first_wave, share)
    launch = illuminate(illum_amp, lax.dynamic_slice_in_dim(angle_ids, first_wave, share), row_pos)
    wave_field, kept_fields = forward_pass(launch, ratio_pick, every_slice, mask_float, freq_grid)
    target = lax.dynamic_slice_in_dim(measured, first_wave, share, 0)
    adjoint, grad_terms = adjoint_pass(
        wave_field - target, ratio_pick, every_slice, mask_float, freq_grid, kept_fields
    )
    partial_grad = rows_of_grads(grad_terms)
    return lax.psum_scatter(partial_grad, "sec", scatter_dimension=0, tiled=True)


def solution(mesh):
    in_specs = (
        P("sec", "row", None),
        P("row", None),
        P("row", None),
        P(None, "row", None, None),
        P(),
        P(),
    )
    out_specs = P("sec", "row", None)
    return jax.shard_map(body, mesh=mesh, in_specs=in_specs, out_specs=out_specs, check_vma=False)
```

profile of v0, /device:TPU:1, one launch (start us, length us, event | category | flops | bytes accessed | tf_op | source)
XLA Modules:
  0.0 618.3 jit_solution(2100157458710681504)
XLA Ops:
  15.3 4.3 reshape.650
  19.6 9.6 %all-to-all-start = ((f32[32,1,4096]{2,1,0:T(1,128)}), f32[32,1,4096]{2,1,0:T(1,128)S(1)}, u32[]{:S(2)}, u32[]{:S(2)}) async-start(f32[32,1,4096]{2,1,0:T(1,128)} %reshape.650), calls=%async_computation | async-start | bytes 1048576 | tf_op jit(solution)/shard_map/all_to_all | solution.py:131
  29.9 11.8 %all_gather.3 = f32[4,32,1024]{2,1,0:T(8,128)} all-gather(f32[1,32,1024]{2,1,0:T(8,128)S(1)} %copy-done.44), channel_id=1, replica_groups=mesh['sec'=4,'row'=32] {'sec'}, dimensions={0}, use_global_device_ids=true | all-gather | bytes 655360 | tf_op jit(solution)/shard_map/all_gather | solution.py:211
  44.2 2.8 reduce
  47.0 3.1 reshape.651
  50.1 4.2 copy.534
  68.3 4.3 reshape.652
  72.6 10.2 %all-to-all-start.1 = ((f32[32,1,4096]{2,1,0:T(1,128)}), f32[32,1,4096]{2,1,0:T(1,128)}, u32[]{:S(2)}, u32[]{:S(2)}) async-start(f32[32,1,4096]{2,1,0:T(1,128)} %reshape.652), calls=%async_computation.1 | async-start | bytes 1048576 | tf_op jit(solution)/shard_map/all_to_all | solution.py:142
  85.2 4.7 broadcast_multiply_fusion.2
  89.9 4.4 all-to-all-done.1
  94.3 2.8 reduce.1
  97.1 3.2 reshape.653
  100.3 4.2 copy.533
  117.8 3.6 reshape.654
  121.5 15.6 %all_to_all.210 = f32[32,1,4096]{2,1,0:T(1,128)} all-to-all(f32[32,1,4096]{2,1,0:T(1,128)S(1)} %reshape.654), channel_id=1, replica_groups=mesh['sec'=4,'row'=32] {'row'}, dimensions={0} | all-to-all | bytes 1048576 | tf_op jit(solution)/shard_map/all_to_all | solution.py:131
  137.0 2.8 reduce.2
  139.9 3.2 reshape.655
  143.0 4.2 copy.532
  160.8 3.8 reshape.656
  164.6 15.2 %all_to_all.211 = f32[32,1,4096]{2,1,0:T(1,128)} all-to-all(f32[32,1,4096]{2,1,0:T(1,128)S(1)} %reshape.656), channel_id=1, replica_groups=mesh['sec'=4,'row'=32] {'row'}, dimensions={0} | all-to-all | bytes 1048576 | tf_op jit(solution)/shard_map/all_to_all | solution.py:142
  179.7 2.8 reduce.3
  182.5 3.2 reshape.657
  185.7 4.2 copy.531
  203.2 4.0 reshape.658
  207.3 15.2 %all_to_all.212 = f32[32,1,4096]{2,1,0:T(1,128)} all-to-all(f32[32,1,4096]{2,1,0:T(1,128)S(1)} %reshape.658), channel_id=1, replica_groups=mesh['sec'=4,'row'=32] {'row'}, dimensions={0} | all-to-all | bytes 1048576 | tf_op jit(solution)/shard_map/all_to_all | solution.py:131
  222.4 2.8 reduce.4
  225.3 3.2 reshape.659
  228.4 4.2 copy.530
  246.2 3.8 reshape.660
  250.0 15.2 %all_to_all.213 = f32[32,1,4096]{2,1,0:T(1,128)} all-to-all(f32[32,1,4096]{2,1,0:T(1,128)S(1)} %reshape.660), channel_id=1, replica_groups=mesh['sec'=4,'row'=32] {'row'}, dimensions={0} | all-to-all | bytes 1048576 | tf_op jit(solution)/shard_map/all_to_all | solution.py:142
  265.1 2.8 reduce.5
  268.0 3.2 reshape.661
  271.1 4.2 copy.529
  288.6 4.0 reshape.662
  292.6 15.2 %all_to_all.214 = f32[32,1,4096]{2,1,0:T(1,128)} all-to-all(f32[32,1,4096]{2,1,0:T(1,128)S(1)} %reshape.662), channel_id=1, replica_groups=mesh['sec'=4,'row'=32] {'row'}, dimensions={0} | all-to-all | bytes 1048576 | tf_op jit(solution)/shard_map/all_to_all | solution.py:131
  307.8 2.8 reduce.6
  310.6 3.1 reshape.663
  313.8 4.2 copy.528
  328.2 3.9 copy.287
  332.1 4.4 reshape.664
  336.5 4.4 all-to-all-start.7
  341.8 4.9 cosine_multiply_fusion
  346.8 5.5 all-to-all-done.7
  352.3 2.8 reduce.7
  373.9 2.9 reshape.666
  376.7 15.7 %all_to_all.215 = f32[32,1,4096]{2,1,0:T(1,128)S(1)} all-to-all(f32[32,1,4096]{2,1,0:T(1,128)} %reshape.666), channel_id=1, replica_groups=mesh['sec'=4,'row'=32] {'row'}, dimensions={0} | all-to-all | bytes 1048576 | tf_op jit(solution)/shard_map/all_to_all | solution.py:131
  392.4 2.7 reduce.8
  395.1 2.8 reshape.667
  410.6 3.0 copy.302
  413.5 2.9 reshape.668
  416.4 15.2 %all_to_all.216 = f32[32,1,4096]{2,1,0:T(1,128)S(1)} all-to-all(f32[32,1,4096]{2,1,0:T(1,128)} %reshape.668), channel_id=1, replica_groups=mesh['sec'=4,'row'=32] {'row'}, dimensions={0} | all-to-all | bytes 1048576 | tf_op jit(solution)/shard_map/all_to_all | solution.py:142
  431.7 2.7 reduce.9
  434.4 2.8 reshape.669
  453.2 2.8 reshape.670
  456.1 15.2 %all_to_all.217 = f32[32,1,4096]{2,1,0:T(1,128)S(1)} all-to-all(f32[32,1,4096]{2,1,0:T(1,128)} %reshape.670), channel_id=1, replica_groups=mesh['sec'=4,'row'=32] {'row'}, dimensions={0} | all-to-all | bytes 1048576 | tf_op jit(solution)/shard_map/all_to_all | solution.py:131
  474.0 2.8 reshape.671
  492.2 15.0 %all_to_all.218 = f32[32,1,4096]{2,1,0:T(1,128)S(1)} all-to-all(f32[32,1,4096]{2,1,0:T(1,128)S(1)} %reshape.672), channel_id=1, replica_groups=mesh['sec'=4,'row'=32] {'row'}, dimensions={0} | all-to-all | bytes 1048576 | tf_op jit(solution)/shard_map/all_to_all | solution.py:142
  525.5 2.9 reshape.674
  528.4 3.7 all-to-all-start.12
  534.3 9.3 %all-to-all-done.12 = f32[32,1,4096]{2,1,0:T(1,128)S(1)} async-done(((f32[32,1,4096]{2,1,0:T(1,128)}), f32[32,1,4096]{2,1,0:T(1,128)S(1)}, u32[]{:S(2)}, u32[]{:S(2)}) %all-to-all-start.12) | async-done | bytes 524320 | tf_op jit(solution)/shard_map/all_to_all | solution.py:131
  560.9 2.8 reshape.676
  563.8 3.8 all-to-all-start.13
  571.1 8.1 %all-to-all-done.13 = f32[32,1,4096]{2,1,0:T(1,128)S(1)} async-done(((f32[32,1,4096]{2,1,0:T(1,128)}), f32[32,1,4096]{2,1,0:T(1,128)S(1)}, u32[]{:S(2)}, u32[]{:S(2)}) %all-to-all-start.13) | async-done | bytes 524320 | tf_op jit(solution)/shard_map/all_to_all | solution.py:142
  594.6 16.7 %reduce-scatter.2.cloned.1.call-done = f32[1,32,1024]{2,1,0:T(8,128)} async-done(((f32[4,32,1024]{2,1,0:T(8,128)}), f32[1,32,1024]{2,1,0:T(8,128)}) %reduce-scatter.2.cloned.1.call-update) | async-done | bytes 131088 | tf_op jit(solution)/shard_map/reduce_scatter | solution.py:222
  (484 shorter events, 225.8 us)
Async XLA Ops:
  6.5 334.4 %copy-start = (f32[8,32,2,1024]{3,2,1,0:T(2,128)S(1)}, f32[8,32,2,1024]{3,2,1,0:T(2,128)}, u32[]{:S(2)}) copy-start(f32[8,32,2,1024]{3,2,1,0:T(2,128)} %param.9) | copy-start | bytes 6291460
  15.2 14.0 %copy-start.47 = (s32[8]{0:T(128)S(1)}, s32[8]{0:T(128)}, u32[]{:S(2)}) copy-start(s32[8]{0:T(128)} %param.10) | copy-start | bytes 100
  15.2 14.7 %copy-start.44 = (f32[1,32,1024]{2,1,0:T(8,128)S(1)}, f32[1,32,1024]{2,1,0:T(8,128)}, u32[]{:S(2)}) copy-start(f32[1,32,1024]{2,1,0:T(8,128)} %param.6) | copy-start | bytes 393220
  19.6 23.3 %all-to-all-start = ((f32[32,1,4096]{2,1,0:T(1,128)}), f32[32,1,4096]{2,1,0:T(1,128)S(1)}, u32[]{:S(2)}, u32[]{:S(2)}) async-start(f32[32,1,4096]{2,1,0:T(1,128)} %reshape.650), calls=%async_computation | async-start | bytes 1048576 | tf_op jit(solution)/shard_map/all_to_all | solution.py:131
  42.9 441.8 %copy-start.5 = (f32[2,8,128,32]{2,3,1,0:T(8,128)}, f32[2,8,128,32]{2,3,1,0:T(8,128)S(1)}, u32[]{:S(2)}) copy-start(f32[2,8,128,32]{2,3,1,0:T(8,128)S(1)} %get-tuple-element.234) | copy-start | bytes 786436
  42.9 0.8 copy-start.28
  68.3 14.5 %copy-start.27 = (f32[4,32,1024]{2,1,0:T(8,128)S(1)}, f32[4,32,1024]{2,1,0:T(8,128)}, u32[]{:S(2)}) copy-start(f32[4,32,1024]{2,1,0:T(8,128)} %all_gather.3) | copy-start | bytes 1572868
  72.6 21.6 %all-to-all-start.1 = ((f32[32,1,4096]{2,1,0:T(1,128)}), f32[32,1,4096]{2,1,0:T(1,128)}, u32[]{:S(2)}, u32[]{:S(2)}) async-start(f32[32,1,4096]{2,1,0:T(1,128)} %reshape.652), calls=%async_computation.1 | async-start | bytes 1048576 | tf_op jit(solution)/shard_map/all_to_all | solution.py:142
  84.4 0.6 copy-start.30
  84.4 0.7 copy-start.32
  110.7 2.2 copy-start.41
  110.7 2.2 copy-start.42
  112.0 0.7 copy-start.14
  112.0 0.8 copy-start.15
  196.1 2.2 copy-start.23
  196.1 2.2 copy-start.38
  197.4 0.7 copy-start.16
  197.4 0.8 copy-start.18
  281.5 2.1 copy-start.25
  281.5 2.1 copy-start.37
  282.9 0.7 copy-start.19
  282.9 0.8 copy-start.21
  332.1 9.8 %copy-start.31 = (f32[32,1024]{1,0:T(8,128)S(1)}, f32[32,1024]{1,0:T(8,128)}, u32[]{:S(2)}) copy-start(f32[32,1024]{1,0:T(8,128)} %copy-done.30) | copy-start | bytes 393220
  332.1 9.8 %copy-start.33 = (f32[32,1024]{1,0:T(8,128)S(1)}, f32[32,1024]{1,0:T(8,128)}, u32[]{:S(2)}) copy-start(f32[32,1024]{1,0:T(8,128)} %copy-done.32) | copy-start | bytes 393220
  332.1 9.8 %copy-start.43 = (f32[32,1024]{1,0:T(8,128)S(1)}, f32[32,1024]{1,0:T(8,128)}, u32[]{:S(2)}) copy-start(f32[32,1024]{1,0:T(8,128)} %get-tuple-element.16) | copy-start | bytes 393220
  332.1 9.8 %copy-start.45 = (f32[2]{0:T(128)S(1)}, f32[2]{0:T(128)}, u32[]{:S(2)}) copy-start(f32[2]{0:T(128)} %get-tuple-element.14) | copy-start | bytes 28
  336.5 15.8 %all-to-all-start.7 = ((f32[32,1,4096]{2,1,0:T(1,128)}), f32[32,1,4096]{2,1,0:T(1,128)}, u32[]{:S(2)}, u32[]{:S(2)}) async-start(f32[32,1,4096]{2,1,0:T(1,128)} %reshape.664), calls=%async_computation.7 | async-start | bytes 1048576 | tf_op jit(solution)/shard_map/all_to_all | solution.py:142
  364.2 1.2 copy-start.29
  364.2 1.2 copy-start.34
  365.3 2.3 copy-start.39
  365.3 2.3 copy-start.40
  444.8 1.0 copy-start.26
  445.6 1.9 copy-start.7
  445.6 1.9 copy-start.11
  518.6 1.4 copy-start.24
  519.3 0.7 copy-start.9
  519.3 2.3 copy-start.13
  525.5 6.6 %copy-start.2 = (f32[2,32,2,1024]{3,2,1,0:T(2,128)S(1)}, f32[2,32,2,1024]{3,2,1,0:T(2,128)}, u32[]{:S(2)}) copy-start(f32[2,32,2,1024]{3,2,1,0:T(2,128)} %reshape.610) | copy-start | bytes 1572868
  528.4 15.3 %all-to-all-start.12 = ((f32[32,1,4096]{2,1,0:T(1,128)}), f32[32,1,4096]{2,1,0:T(1,128)S(1)}, u32[]{:S(2)}, u32[]{:S(2)}) async-start(f32[32,1,4096]{2,1,0:T(1,128)} %reshape.674), calls=%async_computation.12 | async-start | bytes 1048576 | tf_op jit(solution)/shard_map/all_to_all | solution.py:131
  554.6 1.0 copy-start.6
  560.9 6.9 %copy-start.3 = (f32[2,32,2,1024]{3,2,1,0:T(2,128)S(1)}, f32[2,32,2,1024]{3,2,1,0:T(2,128)}, u32[]{:S(2)}) copy-start(f32[2,32,2,1024]{3,2,1,0:T(2,128)} %reshape.614) | copy-start | bytes 1572868
  560.9 6.9 %copy-start.17 = (f32[2,32,1,1024]{3,1,0,2:T(8,128)S(1)}, f32[2,32,1,1024]{3,1,0,2:T(8,128)}, u32[]{:S(2)}) copy-start(f32[2,32,1,1024]{3,1,0,2:T(8,128)} %copy-done.16) | copy-start | bytes 786436
  563.8 6.3 %copy-start.4 = (f32[2,32,2,1024]{3,2,1,0:T(2,128)S(1)}, f32[2,32,2,1024]{3,2,1,0:T(2,128)}, u32[]{:S(2)}) copy-start(f32[2,32,2,1024]{3,2,1,0:T(2,128)} %reshape.618) | copy-start | bytes 1572868
  563.8 6.3 %copy-start.20 = (f32[2,32,1,1024]{3,1,0,2:T(8,128)S(1)}, f32[2,32,1,1024]{3,1,0,2:T(8,128)}, u32[]{:S(2)}) copy-start(f32[2,32,1,1024]{3,1,0,2:T(8,128)} %copy-done.19) | copy-start | bytes 786436
  563.8 6.3 %copy-start.22 = (f32[2,32,1,1024]{3,1,0,2:T(8,128)S(1)}, f32[2,32,1,1024]{3,1,0,2:T(8,128)}, u32[]{:S(2)}) copy-start(f32[2,32,1,1024]{3,1,0,2:T(8,128)} %copy-done.21) | copy-start | bytes 786436
  563.8 6.3 %copy-start.35 = (f32[2,32,1024]{2,1,0:T(8,128)S(1)}, f32[2,32,1024]{2,1,0:T(8,128)}, u32[]{:S(2)}) copy-start(f32[2,32,1024]{2,1,0:T(8,128)} %get-tuple-element.218) | copy-start | bytes 786436
  563.8 6.3 %copy-start.36 = (f32[2,32,1024]{2,1,0:T(8,128)S(1)}, f32[2,32,1024]{2,1,0:T(8,128)}, u32[]{:S(2)}) copy-start(f32[2,32,1024]{2,1,0:T(8,128)} %get-tuple-element.219) | copy-start | bytes 786436
  563.8 15.4 %all-to-all-start.13 = ((f32[32,1,4096]{2,1,0:T(1,128)}), f32[32,1,4096]{2,1,0:T(1,128)S(1)}, u32[]{:S(2)}, u32[]{:S(2)}) async-start(f32[32,1,4096]{2,1,0:T(1,128)} %reshape.676), calls=%async_computation.13 | async-start | bytes 1048576 | tf_op jit(solution)/shard_map/all_to_all | solution.py:142
  567.6 43.7 %reduce-scatter.2.cloned.1.call-start = ((), (), s32[]{:S(2)}) async-start(), calls=%async_computation.15 | async-start | bytes 655360 | tf_op jit(solution)/shard_map/reduce_scatter | solution.py:222
  589.8 1.4 copy-start.8
  589.8 1.4 copy-start.10
  589.8 1.4 copy-start.12
  589.8 1.4 copy-start.46
  591.2 20.2 %copy-start.1 = (f32[8,32,2,1024]{3,2,1,0:T(2,128)S(1)}, f32[8,32,2,1024]{3,2,1,0:T(2,128)}, u32[]{:S(2)}) copy-start(f32[8,32,2,1024]{3,2,1,0:T(2,128)} %param.9) | copy-start | bytes 6291460
Sparse Core Ops, SparseCore 0:
  594.7 16.5 reduce-scatter.1
where the time goes:
time: 628 us; the launch traced here: 618 us
  local copies, waits for them, and re-layouts  212 us (34%)
  blocking collectives  149 us (24%)
  matrix products  87.6 us (14%)
  other arithmetic  77.3 us (12%)
  waiting for transfers between devices  44 us (7%)
  starting transfers between devices  31.9 us (5%)
  between operations  16.7 us (3%)
    unnamed x137, local copies, waits for them, and re-layouts  92 us
    dot_general x112, matrix products, contract(): jnp.einsum(form, left_op, right_op, precision=precise, preferred_element_...  87.6 us
    all_to_all x5, blocking collectives, propagate(): lax.all_to_all(spectrum, 'row', split_axis=3, concat_axis=1, tiled=True)  76.8 us
    all_to_all x4, blocking collectives, propagate(): lax.all_to_all(merged.reshape(batches, height, channels, narrow), 'row',...  60.6 us
    all_to_all x8, local copies, waits for them, and re-layouts, propagate(): lax.all_to_all(spectrum, 'row', split_axis=3, concat_axis=1, tiled=True)  25 us
    all_to_all x7, local copies, waits for them, and re-layouts, propagate(): lax.all_to_all(merged.reshape(batches, height, channels, narrow), 'row',...  22.8 us
    mul x14, local copies, waits for them, and re-layouts, cols_inverse(): return segmented.reshape(batches, height, lanes) * (1.0 / height)  22.1 us
    all_to_all x7, other arithmetic, propagate(): lax.all_to_all(spectrum, 'row', split_axis=3, concat_axis=1, tiled=True)  18.5 us
  transfers between devices with their start and end apart: 6, of which 5 were waited for; matrix products, arithmetic and copies ran while one was open for 3% of the time, Pallas kernels for 0%

commit v1 on v0

v1 whole, which is shorter than its diff:
```python
import functools
import math

import jax
import jax.numpy as jnp
import numpy as np
from jax import lax
from jax.experimental import pallas as pl
from jax.experimental.pallas import tpu as pltpu
from jax.sharding import PartitionSpec as P

ratio_base = 0.75
ratio_step = 1.0 / 128.0
prop_scale = 150.0
core_step = 0.8
tilt_step = 8
angle_side = 8

LANES = 128
GROUPS = 8
GRID = GROUPS * LANES
WIDE = 32
PEERS = GRID // WIDE
SHARE = 2
FOLD = LANES // WIDE
VMEM_LIMIT = 48 * 1024 * 1024


def dft_tables():
    counter = np.arange(LANES)
    angle = -2.0 * np.pi / LANES * (counter[:, None] * counter[None, :] % LANES)
    real, imag = np.cos(angle), np.sin(angle)
    full = np.block([[real, imag], [-imag, real]]).astype(np.float32)
    high = full.astype(jnp.bfloat16)
    low = (full - high.astype(np.float32)).astype(jnp.bfloat16)
    turn = -2.0 * np.pi / GRID * (np.arange(GROUPS)[:, None] * counter[None, :])
    twist = np.stack([np.cos(turn), np.sin(turn)]).astype(np.float32)
    return high, low, twist


def cos_sin(angle):
    turns = jnp.floor(angle * (2.0 / math.pi) + 0.5)
    rest = angle - turns * 1.5703125
    rest = rest - turns * 4.837512969970703e-4
    rest = rest - turns * 7.549789948768648e-8
    square = rest * rest
    sine = rest + rest * square * (
        -1.6666654611e-1 + square * (8.3321608736e-3 + square * -1.9515295891e-4)
    )
    cosine = (1.0 - 0.5 * square) + square * square * (
        4.166664568298827e-2 + square * (-1.388731625493765e-3 + square * 2.443315711809948e-5)
    )
    quarter = turns.astype(jnp.int32)
    swap = (quarter & 1) != 0
    cos_part = jnp.where(swap, sine, cosine)
    sin_part = jnp.where(swap, cosine, sine)
    cos_part = jnp.where(((quarter + 1) & 2) != 0, -cos_part, cos_part)
    sin_part = jnp.where((quarter & 2) != 0, -sin_part, sin_part)
    return cos_part, sin_part


def times(left, right):
    return (
        left[0] * right[0] - left[1] * right[1],
        left[0] * right[1] + left[1] * right[0],
    )


def times_conj(left, right):
    return (
        left[0] * right[0] + left[1] * right[1],
        left[1] * right[0] - left[0] * right[1],
    )


def plus(left, right):
    return (left[0] + right[0], left[1] + right[1])


def minus(left, right):
    return (left[0] - right[0], left[1] - right[1])


def quarter_turn(value, sign):
    if sign > 0:
        return (-value[1], value[0])
    return (value[1], -value[0])


def dft4(items, sign):
    even, odd = plus(items[0], items[2]), minus(items[0], items[2])
    other, rest = plus(items[1], items[3]), minus(items[1], items[3])
    rest = quarter_turn(rest, sign)
    return [plus(even, other), plus(odd, rest), minus(even, other), minus(odd, rest)]


def dft8(items, sign):
    even, odd = dft4(items[0::2], sign), dft4(items[1::2], sign)
    half = math.sqrt(0.5)
    first, third = odd[1], odd[3]
    if sign > 0:
        first = ((first[0] - first[1]) * half, (first[0] + first[1]) * half)
        third = ((-third[0] - third[1]) * half, (third[0] - third[1]) * half)
    else:
        first = ((first[0] + first[1]) * half, (first[1] - first[0]) * half)
        third = ((third[1] - third[0]) * half, (-third[0] - third[1]) * half)
    odd = [odd[0], first, quarter_turn(odd[2], sign), third]
    return [plus(e, o) for e, o in zip(even, odd)] + [minus(e, o) for e, o in zip(even, odd)]


def matmul_pair(left, right, high, low):
    both = jnp.concatenate([left, right], axis=1)
    upper = both.astype(jnp.bfloat16)
    lower = (both - upper.astype(jnp.float32)).astype(jnp.bfloat16)
    product = functools.partial(jnp.dot, preferred_element_type=jnp.float32)
    result = product(upper, high) + (product(lower, high) + product(upper, low))
    return result[:, :LANES], result[:, LANES:]


def line_filter(field, filters, twist, high, low, sign):
    stacked = []
    for wave in field:
        parts = dft8(wave, -1)
        stacked += [parts[0]] + [times(parts[k], twist[k]) for k in range(1, GROUPS)]
    real, imag = matmul_pair(
        jnp.concatenate([s[0] for s in stacked], axis=0),
        jnp.concatenate([s[1] for s in stacked], axis=0),
        high,
        low,
    )
    scaled = []
    for index in range(len(stacked)):
        rows = slice(index * WIDE, (index + 1) * WIDE)
        value, pick = (real[rows], imag[rows]), filters[index // GROUPS][index % GROUPS]
        scaled.append(times(value, pick) if sign > 0 else times_conj(value, pick))
    imag, real = matmul_pair(
        jnp.concatenate([s[1] for s in scaled], axis=0),
        jnp.concatenate([s[0] for s in scaled], axis=0),
        high,
        low,
    )
    result = []
    for wave in range(len(field)):
        parts = []
        for k in range(GROUPS):
            rows = slice((wave * GROUPS + k) * WIDE, (wave * GROUPS + k + 1) * WIDE)
            value = (real[rows], imag[rows])
            parts.append(value if k == 0 else times_conj(value, twist[k]))
        result.append(dft8(parts, 1))
    return result


def exchange_blocks(items):
    lane = lax.broadcasted_iota(jnp.int32, items[0].shape, items[0].ndim - 1)
    axis = items[0].ndim - 1
    low_half, even = (lane & 64) == 0, (lane & 32) == 0
    halves = [None] * 4
    for i in range(2):
        halves[i] = jnp.where(low_half, items[i], pltpu.roll(items[i + 2], 64, axis))
        halves[i + 2] = jnp.where(low_half, pltpu.roll(items[i], 64, axis), items[i + 2])
    result = [None] * 4
    for i in (0, 2):
        result[i] = jnp.where(even, halves[i], pltpu.roll(halves[i + 1], 32, axis))
        result[i + 1] = jnp.where(even, pltpu.roll(halves[i], LANES - 32, axis), halves[i + 1])
    return result


def load_field(blocks_ref):
    field = [[None] * GROUPS for _ in range(SHARE)]
    for group in range(GROUPS):
        items = exchange_blocks([blocks_ref[FOLD * group + i, :WIDE] for i in range(FOLD)])
        for wave in range(SHARE):
            field[wave][group] = (items[wave], items[SHARE + wave])
    return field


def store_field(blocks_ref, field):
    for group in range(GROUPS):
        rows = [field[w][group][part] for part in range(2) for w in range(SHARE)]
        turned = jnp.concatenate(rows, axis=0).T
        for i in range(FOLD):
            blocks_ref[FOLD * group + i, :WIDE] = turned[i * WIDE : (i + 1) * WIDE]


def pack_plane(plane):
    blocks = []
    for group in range(GROUPS):
        rows = [plane[group]] + [pltpu.roll(plane[group], LANES - 8 * q, 1) for q in range(1, FOLD)]
        turned = jnp.concatenate(rows, axis=0).T
        blocks += [turned[i * WIDE : i * WIDE + 8] for i in range(FOLD)]
    return blocks


def unpack_plane(blocks):
    plane = []
    for group in range(GROUPS):
        items = exchange_blocks(blocks[FOLD * group : FOLD * (group + 1)])
        plane.append(jnp.concatenate(items, axis=0))
    return plane


def ratio_of(place_ref, waves_ref, wave):
    number = waves_ref[place_ref[0] * SHARE + wave]
    return ratio_base + ratio_step * number.astype(jnp.float32)


def filters_of(place_ref, waves_ref):
    row = lax.broadcasted_iota(jnp.int32, (GROUPS, LANES), 0)
    lane = lax.broadcasted_iota(jnp.int32, (GROUPS, LANES), 1)
    natural = row + GROUPS * lane
    signed = jnp.where(natural < GRID // 2, natural, natural - GRID)
    scaled = signed.astype(jnp.float32) * (2.0 / GRID)
    squares = scaled * scaled
    filters = []
    for wave in range(SHARE):
        real, imag = cos_sin((-prop_scale * ratio_of(place_ref, waves_ref, wave)) * squares)
        real, imag = real * (1.0 / GRID), imag * (1.0 / GRID)
        filters.append([(real[k : k + 1], imag[k : k + 1]) for k in range(GROUPS)])
    return filters


def twist_of(twist_ref):
    return [(twist_ref[0, k : k + 1], twist_ref[1, k : k + 1]) for k in range(GROUPS)]


def inverse_ratio(place_ref, waves_ref, wave):
    ratio = ratio_of(place_ref, waves_ref, wave)
    return 1.0 / jnp.full((8, LANES), ratio, jnp.float32)[:1]


def launch_kernel(place_ref, waves_ref, angles_ref, illum_ref, high_ref, low_ref, twist_ref, out_ref):
    twist = twist_of(twist_ref)
    filters = filters_of(place_ref, waves_ref)
    field = []
    for wave in range(SHARE):
        pick = angles_ref[place_ref[0] * SHARE + wave]
        tilt_x = ((pick & (angle_side - 1)) - angle_side // 2) * tilt_step
        tilt_y = ((pick >> 3) - angle_side // 2) * tilt_step
        row = lax.broadcasted_iota(jnp.int32, (WIDE, LANES), 0) + place_ref[1] * WIDE

        def wheel(product):
            turned = ((product + GRID // 2) & (GRID - 1)) - GRID // 2
            return cos_sin((2.0 * math.pi / GRID) * turned.astype(jnp.float32))

        down = wheel(tilt_y * row)
        groups = []
        for group in range(GROUPS):
            column = lax.broadcasted_iota(jnp.int32, (8, LANES), 1) + group * LANES
            across = wheel(tilt_x * column)
            across = (across[0][:1], across[1][:1])
            wave_now = times(down, across)
            bright = illum_ref[:, group * LANES : (group + 1) * LANES]
            groups.append((bright * wave_now[0], bright * wave_now[1]))
        field.append(groups)
    field = line_filter(field, filters, twist, high_ref[...], low_ref[...], 1)
    store_field(out_ref, field)


def save(kept_ref, field):
    for wave in range(SHARE):
        for group in range(GROUPS):
            for part in range(2):
                kept_ref[wave, group, part] = field[wave][group][part]


def kept(kept_ref):
    return [
        [(kept_ref[wave, group, 0], kept_ref[wave, group, 1]) for group in range(GROUPS)]
        for wave in range(SHARE)
    ]


def read_base(base_ref, layer):
    if layer % 2:
        return [
            jnp.concatenate([base_ref[layer, tile * GROUPS + group] for tile in range(FOLD)], axis=0)
            for group in range(GROUPS)
        ]
    return unpack_plane([base_ref[layer, peer] for peer in range(PEERS)])


def screens(base_ref, layer, place_ref, waves_ref):
    base = read_base(base_ref, layer)
    result = []
    for wave in range(SHARE):
        scale = inverse_ratio(place_ref, waves_ref, wave)
        result.append([cos_sin(base[group] * scale) for group in range(GROUPS)])
    return result


def gradient(adjoint, field, place_ref, waves_ref):
    total = [None] * GROUPS
    for wave in range(SHARE):
        scale = inverse_ratio(place_ref, waves_ref, wave)
        for group in range(GROUPS):
            left, right = adjoint[wave][group], field[wave][group]
            term = (left[1] * right[0] - left[0] * right[1]) * scale
            total[group] = term if wave == 0 else total[group] + term
    return total


def each(function, left, right):
    return [[function(a, b) for a, b in zip(p, q)] for p, q in zip(left, right)]


def forward_kernel(
    layer, place_ref, waves_ref, in_ref, base_ref, high_ref, low_ref, twist_ref, out_ref, field_ref, screen_ref
):
    twist, high, low = twist_of(twist_ref), high_ref[...], low_ref[...]
    filters = filters_of(place_ref, waves_ref)
    field = line_filter(load_field(in_ref), filters, twist, high, low, 1)
    screen = screens(base_ref, layer, place_ref, waves_ref)
    save(screen_ref, screen)
    field = each(times, field, screen)
    save(field_ref, field)
    store_field(out_ref, line_filter(field, filters, twist, high, low, 1))


def turn_kernel(place_ref, waves_ref, in_ref, base_ref, target_ref, high_ref, low_ref, twist_ref, out_ref):
    twist, high, low = twist_of(twist_ref), high_ref[...], low_ref[...]
    filters = filters_of(place_ref, waves_ref)
    field = line_filter(load_field(in_ref), filters, twist, high, low, 1)
    screen = screens(base_ref, 3, place_ref, waves_ref)
    field = each(times, field, screen)
    adjoint = []
    for wave in range(SHARE):
        groups = []
        for group in range(GROUPS):
            lanes = slice(group * LANES, (group + 1) * LANES)
            goal = (target_ref[wave, :, 0, lanes], target_ref[wave, :, 1, lanes])
            groups.append(minus(field[wave][group], goal))
        adjoint.append(groups)
    blocks = pack_plane(gradient(adjoint, field, place_ref, waves_ref))
    for peer in range(PEERS):
        out_ref[peer, WIDE:] = blocks[peer]
    adjoint = each(times_conj, adjoint, screen)
    store_field(out_ref, line_filter(adjoint, filters, twist, high, low, -1))


def adjoint_kernel(
    with_plane, place_ref, waves_ref, in_ref, field_ref, screen_ref, high_ref, low_ref, twist_ref, out_ref, *grad_ref
):
    twist, high, low = twist_of(twist_ref), high_ref[...], low_ref[...]
    filters = filters_of(place_ref, waves_ref)
    adjoint = line_filter(load_field(in_ref), filters, twist, high, low, -1)
    grad = gradient(adjoint, kept(field_ref), place_ref, waves_ref)
    if with_plane:
        blocks = pack_plane(grad)
        for peer in range(PEERS):
            out_ref[peer, WIDE:] = blocks[peer]
    else:
        for group in range(GROUPS):
            grad_ref[0][group] = grad[group]
    adjoint = each(times_conj, adjoint, kept(screen_ref))
    store_field(out_ref, line_filter(adjoint, filters, twist, high, low, -1))


def last_kernel(
    place_ref, waves_ref, in_ref, field_ref, third_ref, second_ref, high_ref, low_ref, twist_ref, out_ref
):
    twist, high, low = twist_of(twist_ref), high_ref[...], low_ref[...]
    filters = filters_of(place_ref, waves_ref)
    adjoint = line_filter(load_field(in_ref), filters, twist, high, low, -1)
    planes = [
        gradient(adjoint, kept(field_ref), place_ref, waves_ref),
        unpack_plane([in_ref[peer, WIDE:] for peer in range(PEERS)]),
        [second_ref[group] for group in range(GROUPS)],
        unpack_plane([third_ref[peer, WIDE:] for peer in range(PEERS)]),
    ]
    for layer in range(4):
        blocks = pack_plane(planes[layer])
        for peer in range(PEERS):
            out_ref[layer * PEERS + peer] = blocks[peer]


def sum_kernel(in_ref, out_ref):
    total = [
        (in_ref[peer] + in_ref[PEERS + peer]) + (in_ref[2 * PEERS + peer] + in_ref[3 * PEERS + peer])
        for peer in range(PEERS)
    ]
    plane = unpack_plane(total)
    for group in range(GROUPS):
        out_ref[0, :, group * LANES : (group + 1) * LANES] = plane[group]


def base_kernel(slice_ref, mask_ref, rows_ref, out_ref):
    base = []
    for group in range(GROUPS):
        lanes = slice(group * LANES, (group + 1) * LANES)
        plane = core_step * mask_ref[:, lanes].astype(jnp.float32) + slice_ref[0, :, lanes]
        base.append(plane)
        for tile in range(FOLD):
            rows_ref[tile * GROUPS + group] = plane[tile * 8 : (tile + 1) * 8]
    blocks = pack_plane(base)
    for peer in range(PEERS):
        out_ref[peer] = blocks[peer]


def call(kernel, scalars, arrays, outs):
    specs = [pl.BlockSpec(memory_space=pltpu.SMEM)] * len(scalars)
    specs += [pl.BlockSpec(memory_space=pltpu.VMEM)] * len(arrays)
    return pl.pallas_call(
        kernel,
        out_shape=[jax.ShapeDtypeStruct(shape, jnp.float32) for shape in outs],
        in_specs=specs,
        out_specs=[pl.BlockSpec(memory_space=pltpu.VMEM)] * len(outs),
        compiler_params=pltpu.CompilerParams(vmem_limit_bytes=VMEM_LIMIT),
    )(*scalars, *arrays)


def body(index_slices, core_mask, illum_amp, measured, wave_ids, angle_ids):
    row_pos, sec_pos = lax.axis_index("row"), lax.axis_index("sec")
    high, low, twist = (jnp.asarray(table) for table in dft_tables())
    tables = (high, low, twist)
    place = jnp.stack([sec_pos, row_pos]).astype(jnp.int32)
    swap = functools.partial(lax.all_to_all, axis_name="row", split_axis=0, concat_axis=0, tiled=True)
    blocks, small = (PEERS, WIDE, LANES), (PEERS, 8, LANES)
    wide_blocks = (PEERS, WIDE + 8, LANES)
    saved = (SHARE, GROUPS, 2, WIDE, LANES)
    scalars = (place, wave_ids)

    base_rows, base_blocks = call(base_kernel, (), (index_slices, core_mask), (small, small))
    base_own = jnp.where(sec_pos % 2 == 0, swap(base_blocks), base_rows)
    base = lax.all_gather(base_own, "sec", axis=0)
    (sent,) = call(launch_kernel, (*scalars, angle_ids), (illum_amp, *tables), (blocks,))
    fields, screen = [], []
    for layer in range(3):
        kernel = functools.partial(forward_kernel, layer)
        sent, field_now, screen_now = call(kernel, scalars, (swap(sent), base, *tables), (blocks, saved, saved))
        fields.append(field_now)
        screen.append(screen_now)
    target = lax.dynamic_slice_in_dim(measured, sec_pos * SHARE, SHARE, 0)
    (sent,) = call(turn_kernel, scalars, (swap(sent), base, target, *tables), (wide_blocks,))
    third = swap(sent)
    kernel = functools.partial(adjoint_kernel, False)
    sent, second = call(
        kernel, scalars, (third, fields[2], screen[2], *tables), (blocks, (GROUPS, WIDE, LANES))
    )
    kernel = functools.partial(adjoint_kernel, True)
    (sent,) = call(kernel, scalars, (swap(sent), fields[1], screen[1], *tables), (wide_blocks,))
    (grads,) = call(
        last_kernel, scalars, (swap(sent), fields[0], third, second, *tables), ((4 * PEERS, 8, LANES),)
    )
    grads = lax.all_to_all(grads, ("sec", "row"), 0, 0, tiled=True)
    (result,) = call(sum_kernel, (), (grads,), ((1, WIDE, GRID),))
    return result


def solution(mesh):
    in_specs = (
        P("sec", "row", None),
        P("row", None),
        P("row", None),
        P(None, "row", None, None),
        P(),
        P(),
    )
    out_specs = P("sec", "row", None)
    return jax.shard_map(body, mesh=mesh, in_specs=in_specs, out_specs=out_specs, check_vma=False)
```

time: 628 us -> 187 us (0.30); the launches traced: 618 us -> 187 us
  local copies, waits for them, and re-layouts: 212 us -> 13.3 us
  matrix products: 87.6 us -> 0 us
  other arithmetic: 77.3 us -> 0.09 us
  blocking collectives: 149 us -> 113 us
  waiting for transfers between devices: 44 us -> 11.3 us
  Pallas kernels: 0 us -> 27.7 us
  between operations: 16.7 us -> 0.2 us
  starting transfers between devices: 31.9 us -> 20.6 us
    dot_general x112 -> x0, matrix products: 87.6 us -> none  [contract(): jnp.einsum(form, left_op, right_op, precision=precise, preferred_element_...]
    unnamed x137 -> x50, local copies, waits for them, and re-layouts: 92 us -> 12.5 us
    all_to_all x15 -> x0, local copies, waits for them, and re-layouts: 47.8 us -> none  [the longest x8 25 us: propagate(): lax.all_to_all(spectrum, 'row', split_axis=3, concat_axis=1, tiled=True)]
    all_to_all x14 -> x0, other arithmetic: 36.1 us -> none  [the longest x7 18.5 us: propagate(): lax.all_to_all(spectrum, 'row', split_axis=3, concat_axis=1, tiled=True)]
    all_to_all x9 -> x6, blocking collectives: 137 us -> 102 us  [the longest x4 66.9 us: body(): swap(sent)]
    reshape x25 -> x0, local copies, waits for them, and re-layouts: 31.4 us -> none  [the longest x7 14.5 us: rows_inverse(): segmented = spectrum.reshape(batches, height, channels, FA, inner_len)]
    pallas_call x0 -> x10, Pallas kernels: none -> 27.7 us  [call(): pl.pallas_call(kernel, out_shape=[jax.ShapeDtypeStruct(shape, jnp.float32...]
    mul x17 -> x0, local copies, waits for them, and re-layouts: 22.9 us -> none  [the longest x14 22.1 us: cols_inverse(): return segmented.reshape(batches, height, lanes) * (1.0 / height)]
  transfers between devices with their start and end apart: 6 -> 3, of which waited for: 5 -> 3; matrix products, arithmetic and copies ran while one was open for 3% -> 0% of each run, Pallas kernels for 0% -> 1%
where the time goes in v1:
time: 187 us
  blocking collectives  113 us (60%)
  Pallas kernels  27.7 us (15%)
  starting transfers between devices  20.6 us (11%)
  local copies, waits for them, and re-layouts  13.3 us (7%)
  waiting for transfers between devices  11.3 us (6%)
    all_to_all x4, blocking collectives, body(): swap(sent)  66.9 us
    pallas_call x10, Pallas kernels, call(): pl.pallas_call(kernel, out_shape=[jax.ShapeDtypeStruct(shape, jnp.float32...  27.7 us
    all_to_all x1, blocking collectives, body(): grads = lax.all_to_all(grads, ('sec', 'row'), 0, 0, tiled=True)  18.9 us
    all_to_all x1, blocking collectives, body(): third = swap(sent)  16.5 us
    unnamed x50, local copies, waits for them, and re-layouts  12.5 us
    all_to_all x2, waiting for transfers between devices, body(): swap(sent)  11.1 us
    all_to_all x2, starting transfers between devices, body(): swap(sent)  11 us
    all_gather x1, blocking collectives, body(): base = lax.all_gather(base_own, 'sec', axis=0)  11 us
  transfers between devices with their start and end apart: 3, of which 3 were waited for; matrix products, arithmetic and copies ran while one was open for 0% of the time, Pallas kernels for 1%

profile of v1, /device:TPU:1, one launch (start us, length us, event | category | flops | bytes accessed | tf_op | source)
XLA Modules:
  0.0 186.6 jit_solution(1425101033888270208)
XLA Ops:
  0.0 0.0 copy-start
  0.0 0.0 copy-start.7
  0.0 0.0 copy-start.2
  0.0 0.0 copy-start.4
  0.0 0.0 copy-start.19
  0.0 1.0 copy-done.19
  1.1 0.0 copy-start.20
  1.1 0.9 copy-done.20
  2.0 0.0 copy-start.23
  2.0 1.0 shard_map.92
  3.0 9.6 %all-to-all-start.1 = ((f32[32,8,128]{2,1,0:T(8,128)}), f32[32,8,128]{2,1,0:T(8,128)S(1)}, u32[]{:S(2)}, u32[]{:S(2)}) async-start(f32[32,8,128]{2,1,0:T(8,128)} %get-tuple-element.17), calls=%async_computation.1 | async-start | bytes 262144 | tf_op jit(solution)/shard_map/all_to_all | solution.py:423
  12.6 0.1 pad_add_fusion.place_ref
  12.7 0.0 copy-start.1
  12.7 0.9 copy-done.1
  13.6 0.0 copy-start.3
  13.6 0.9 copy-done.3
  14.5 0.0 copy-start.6
  14.5 0.7 copy-done.6
  15.2 0.9 copy-done.21
  16.1 0.7 copy-done.22
  16.7 0.7 copy-done.24
  17.4 2.7 %shard_map.91 = f32[32,32,128]{2,1,0:T(8,128)} custom-call(s32[2]{0:T(128)S(1)} %pad_add_fusion.place_ref, s32[8]{0:T(128)S(1)} %copy-done.22, s32[8]{0:T(128)S(1)} %copy-done.24, f32[32,1024]{1,0:T(8,128)S(1)} %copy-done.21, bf16[256,256]{1,0:T(8,128)(2,1)S(1)} %copy-done.3, bf16[256,256]{1,0:T(8,128)(2,1)S(1)} %copy-done.1, f32[2,8,128]{2,1,0:T(8,128)S(1)} %copy-done.6), custom_call_target="tpu_custom_call" | custom-call | tf_op jit(solution)/shard_map/pallas_call | solution.py:402
  20.1 0.2 all-to-all-done.1
  20.3 7.2 %all-to-all-start = ((f32[32,32,128]{2,1,0:T(8,128)}), f32[32,32,128]{2,1,0:T(8,128)S(1)}, u32[]{:S(2)}, u32[]{:S(2)}) async-start(f32[32,32,128]{2,1,0:T(8,128)} %shard_map.91), calls=%async_computation | async-start | bytes 1048576 | tf_op jit(solution)/shard_map/all_to_all | solution.py:429
  27.5 11.0 %all-gather = f32[128,8,128]{2,1,0:T(8,128)S(1)} all-gather(f32[32,8,128]{2,1,0:T(8,128)S(1)} %broadcast_select_fusion), channel_id=2, replica_groups=mesh['sec'=4,'row'=32] {'sec'}, dimensions={0}, use_global_device_ids=true | all-gather | bytes 655360 | tf_op jit(solution)/shard_map/all_gather | solution.py:424
  38.5 0.6 all-to-all-done.in_ref
  39.1 0.0 copy-done.7
  39.1 0.0 copy-done.2
  39.1 0.0 copy-done.4
  39.1 0.0 copy-done.23
  39.1 3.2 %shard_map.93 = (f32[32,32,128]{2,1,0:T(8,128)S(1)}, f32[2,8,2,32,128]{4,3,2,1,0:T(8,128)S(1)}, f32[2,8,2,32,128]{4,3,2,1,0:T(8,128)}) custom-call(s32[2]{0:T(128)S(1)} %pad_add_fusion.place_ref, s32[8]{0:T(128)S(1)} %copy-done.23, f32[32,32,128]{2,1,0:T(8,128)S(1)} %all-to-all-done.in_ref, f32[4,32,8,128]{3,2,1,0:T(8,128)S(1)} %bitcast.3, ...), custom_call_target="tpu_custom_call" | custom-call | tf_op jit(solution)/shard_map/pallas_call | solution.py:402
  42.3 0.0 copy-start.8
  42.3 0.8 copy-done.8
  43.1 20.4 %all_to_all.45.in_ref = f32[32,32,128]{2,1,0:T(8,128)S(1)} all-to-all(f32[32,32,128]{2,1,0:T(8,128)S(1)} %get-tuple-element.19), channel_id=1, replica_groups=mesh['sec'=4,'row'=32] {'row'}, dimensions={0} | all-to-all | bytes 1048576 | tf_op jit(solution)/shard_map/all_to_all | solution.py:429
  63.5 3.3 %shard_map.94 = (f32[32,32,128]{2,1,0:T(8,128)S(1)}, f32[2,8,2,32,128]{4,3,2,1,0:T(8,128)S(1)}, f32[2,8,2,32,128]{4,3,2,1,0:T(8,128)S(1)}) custom-call(s32[2]{0:T(128)S(1)} %pad_add_fusion.place_ref, s32[8]{0:T(128)S(1)} %copy-done.23, f32[32,32,128]{2,1,0:T(8,128)S(1)} %all_to_all.45.in_ref, f32[4,32,8,128]{3,2,1,0:T(8,128)S(1)} %bitcast.4, ...), custom_call_target="tpu_custom_call" | custom-call | tf_op jit(solution)/shard_map/pallas_call | solution.py:402
  66.8 0.0 copy-start.15
  66.8 0.8 copy-done.15
  67.6 0.8 copy-done.17
  68.4 15.0 %all_to_all.46.in_ref = f32[32,32,128]{2,1,0:T(8,128)S(1)} all-to-all(f32[32,32,128]{2,1,0:T(8,128)S(1)} %get-tuple-element.20), channel_id=1, replica_groups=mesh['sec'=4,'row'=32] {'row'}, dimensions={0} | all-to-all | bytes 1048576 | tf_op jit(solution)/shard_map/all_to_all | solution.py:429
  83.4 3.2 %shard_map.95 = (f32[32,32,128]{2,1,0:T(8,128)S(1)}, f32[2,8,2,32,128]{4,3,2,1,0:T(8,128)S(1)}, f32[2,8,2,32,128]{4,3,2,1,0:T(8,128)S(1)}) custom-call(s32[2]{0:T(128)S(1)} %pad_add_fusion.place_ref, s32[8]{0:T(128)S(1)} %copy-done.23, f32[32,32,128]{2,1,0:T(8,128)S(1)} %all_to_all.46.in_ref, f32[4,32,8,128]{3,2,1,0:T(8,128)S(1)} %bitcast.5, ...), custom_call_target="tpu_custom_call" | custom-call | tf_op jit(solution)/shard_map/pallas_call | solution.py:402
  86.6 0.0 copy-start.10
  86.6 0.8 copy-done.10
  87.4 0.8 copy-done.12
  88.2 0.8 copy-done.14
  89.0 3.9 %all-to-all-start.4 = ((f32[32,32,128]{2,1,0:T(8,128)}), f32[32,32,128]{2,1,0:T(8,128)S(1)}, u32[]{:S(2)}, u32[]{:S(2)}) async-start(f32[32,32,128]{2,1,0:T(8,128)} %copy-done.14), calls=%async_computation.4 | async-start | bytes 1048576 | tf_op jit(solution)/shard_map/all_to_all | solution.py:433
  92.9 0.0 copy-done
  92.9 0.8 constant_dynamic-slice_fusion.target_ref
  93.7 10.6 %all-to-all-done.4.in_ref = f32[32,32,128]{2,1,0:T(8,128)S(1)} async-done(((f32[32,32,128]{2,1,0:T(8,128)}), f32[32,32,128]{2,1,0:T(8,128)S(1)}, u32[]{:S(2)}, u32[]{:S(2)}) %all-to-all-start.4) | async-done | bytes 524320 | tf_op jit(solution)/shard_map/all_to_all | solution.py:433
  104.3 1.0 copy-done.5
  105.3 3.9 %shard_map.96 = f32[32,40,128]{2,1,0:T(8,128)S(1)} custom-call(s32[2]{0:T(128)S(1)} %pad_add_fusion.place_ref, s32[8]{0:T(128)S(1)} %copy-done.23, f32[32,32,128]{2,1,0:T(8,128)S(1)} %all-to-all-done.4.in_ref, f32[4,32,8,128]{3,2,1,0:T(8,128)S(1)} %bitcast.6, f32[2,32,2,1024]{3,2,1,0:T(2,128)S(1)} %copy-done.5, bf16[256,256]{1,0:T(8,128)(2,1)S(1)} %copy-done.4, ...), custom_call_target="tpu_custom_call" | custom-call | tf_op jit(solution)/shard_map/pallas_call | solution.py:402
  109.2 0.0 copy-start.18
  109.2 16.5 %all_to_all.47.in_ref.third_ref = f32[32,40,128]{2,1,0:T(8,128)S(1)} all-to-all(f32[32,40,128]{2,1,0:T(8,128)S(1)} %shard_map.96), channel_id=1, replica_groups=mesh['sec'=4,'row'=32] {'row'}, dimensions={0} | all-to-all | bytes 1310720 | tf_op jit(solution)/shard_map/all_to_all | solution.py:434
  125.7 0.0 copy-done.11
  125.7 0.0 copy-done.13
  125.7 3.0 %shard_map.97 = (f32[32,32,128]{2,1,0:T(8,128)S(1)}, f32[8,32,128]{2,1,0:T(8,128)S(1)}) custom-call(s32[2]{0:T(128)S(1)} %pad_add_fusion.place_ref, s32[8]{0:T(128)S(1)} %copy-done.23, f32[32,40,128]{2,1,0:T(8,128)S(1)} %all_to_all.47.in_ref.third_ref, f32[2,8,2,32,128]{4,3,2,1,0:T(8,128)S(1)} %copy-done.11, f32[2,8,2,32,128]{4,3,2,1,0:T(8,128)S(1)} %copy-done.13, ...), custom_call_target="tpu_custom_call" | custom-call | tf_op jit(solution)/shard_map/pallas_call | solution.py:402
  128.7 15.1 %all_to_all.48.in_ref = f32[32,32,128]{2,1,0:T(8,128)S(1)} all-to-all(f32[32,32,128]{2,1,0:T(8,128)S(1)} %get-tuple-element.24), channel_id=1, replica_groups=mesh['sec'=4,'row'=32] {'row'}, dimensions={0} | all-to-all | bytes 1048576 | tf_op jit(solution)/shard_map/all_to_all | solution.py:440
  143.9 0.0 copy-done.16
  143.9 0.0 copy-done.18
  143.9 3.0 %shard_map.98 = f32[32,40,128]{2,1,0:T(8,128)S(1)} custom-call(s32[2]{0:T(128)S(1)} %pad_add_fusion.place_ref, s32[8]{0:T(128)S(1)} %copy-done.23, f32[32,32,128]{2,1,0:T(8,128)S(1)} %all_to_all.48.in_ref, f32[2,8,2,32,128]{4,3,2,1,0:T(8,128)S(1)} %copy-done.16, f32[2,8,2,32,128]{4,3,2,1,0:T(8,128)S(1)} %copy-done.18, bf16[256,256]{1,0:T(8,128)(2,1)S(1)} %copy-done.4, ...), custom_call_target="tpu_custom_call" | custom-call | tf_op jit(solution)/shard_map/pallas_call | solution.py:402
  146.9 16.4 %all_to_all.49.in_ref = f32[32,40,128]{2,1,0:T(8,128)S(1)} all-to-all(f32[32,40,128]{2,1,0:T(8,128)S(1)} %shard_map.98), channel_id=1, replica_groups=mesh['sec'=4,'row'=32] {'row'}, dimensions={0} | all-to-all | bytes 1310720 | tf_op jit(solution)/shard_map/all_to_all | solution.py:442
  163.3 0.0 copy-done.9
  163.3 3.5 %shard_map.99 = f32[128,8,128]{2,1,0:T(8,128)S(1)} custom-call(s32[2]{0:T(128)S(1)} %pad_add_fusion.place_ref, s32[8]{0:T(128)S(1)} %copy-done.23, f32[32,40,128]{2,1,0:T(8,128)S(1)} %all_to_all.49.in_ref, f32[2,8,2,32,128]{4,3,2,1,0:T(8,128)S(1)} %copy-done.9, f32[32,40,128]{2,1,0:T(8,128)S(1)} %all_to_all.47.in_ref.third_ref, ...), custom_call_target="tpu_custom_call" | custom-call | tf_op jit(solution)/shard_map/pallas_call | solution.py:402
  166.8 18.9 %all_to_all.50.in_ref = f32[128,8,128]{2,1,0:T(8,128)S(1)} all-to-all(f32[128,8,128]{2,1,0:T(8,128)S(1)} %shard_map.99), channel_id=1, replica_groups=mesh['sec'=4,'row'=32] {'sec','row'}, dimensions={0} | all-to-all | bytes 1048576 | tf_op jit(solution)/shard_map/all_to_all | solution.py:444
  185.7 0.8 shard_map.100
  (12 shorter events, 0.0 us)
Async XLA Ops:
  0.0 92.9 %copy-start = (f32[8,32,2,1024]{3,2,1,0:T(2,128)S(1)}, f32[8,32,2,1024]{3,2,1,0:T(2,128)}, u32[]{:S(2)}) copy-start(f32[8,32,2,1024]{3,2,1,0:T(2,128)} %param.12) | copy-start | bytes 6291460
  0.0 39.1 %copy-start.7 = (f32[2,8,128]{2,1,0:T(8,128)S(1)}, f32[2,8,128]{2,1,0:T(8,128)}, u32[]{:S(2)}) copy-start(f32[2,8,128]{2,1,0:T(8,128)} %constant.33.clone.twist_ref) | copy-start | bytes 24580
  0.0 39.1 %copy-start.2 = (bf16[256,256]{1,0:T(8,128)(2,1)S(1)}, bf16[256,256]{1,0:T(8,128)(2,1)}, u32[]{:S(2)}) copy-start(bf16[256,256]{1,0:T(8,128)(2,1)} %constant.32.clone.low_ref) | copy-start | bytes 393220
  0.0 39.1 %copy-start.4 = (bf16[256,256]{1,0:T(8,128)(2,1)S(1)}, bf16[256,256]{1,0:T(8,128)(2,1)}, u32[]{:S(2)}) copy-start(bf16[256,256]{1,0:T(8,128)(2,1)} %constant.31.clone.high_ref) | copy-start | bytes 393220
  0.0 1.1 copy-start.19
  1.1 0.9 copy-start.20
  2.0 37.1 %copy-start.23 = (s32[8]{0:T(128)S(1)}, s32[8]{0:T(128)}, u32[]{:S(2)}) copy-start(s32[8]{0:T(128)} %waves_ref.15) | copy-start | bytes 100
  3.0 17.3 %all-to-all-start.1 = ((f32[32,8,128]{2,1,0:T(8,128)}), f32[32,8,128]{2,1,0:T(8,128)S(1)}, u32[]{:S(2)}, u32[]{:S(2)}) async-start(f32[32,8,128]{2,1,0:T(8,128)} %get-tuple-element.17), calls=%async_computation.1 | async-start | bytes 262144 | tf_op jit(solution)/shard_map/all_to_all | solution.py:423
  12.7 0.9 copy-start.1
  13.6 0.9 copy-start.3
  14.5 0.7 copy-start.6
  15.2 0.9 copy-start.21
  16.1 0.7 copy-start.22
  16.7 0.7 copy-start.24
  20.3 18.8 %all-to-all-start = ((f32[32,32,128]{2,1,0:T(8,128)}), f32[32,32,128]{2,1,0:T(8,128)S(1)}, u32[]{:S(2)}, u32[]{:S(2)}) async-start(f32[32,32,128]{2,1,0:T(8,128)} %shard_map.91), calls=%async_computation | async-start | bytes 1048576 | tf_op jit(solution)/shard_map/all_to_all | solution.py:429
  42.3 0.8 copy-start.8
  66.8 0.8 copy-start.15
  67.6 0.8 copy-start.17
  86.6 0.8 copy-start.10
  87.4 0.8 copy-start.12
  88.2 0.8 copy-start.14
  89.0 15.3 %all-to-all-start.4 = ((f32[32,32,128]{2,1,0:T(8,128)}), f32[32,32,128]{2,1,0:T(8,128)S(1)}, u32[]{:S(2)}, u32[]{:S(2)}) async-start(f32[32,32,128]{2,1,0:T(8,128)} %copy-done.14), calls=%async_computation.4 | async-start | bytes 1048576 | tf_op jit(solution)/shard_map/all_to_all | solution.py:433
  104.3 1.0 copy-start.5
  105.3 20.4 %copy-start.11 = (f32[2,8,2,32,128]{4,3,2,1,0:T(8,128)S(1)}, f32[2,8,2,32,128]{4,3,2,1,0:T(8,128)}, u32[]{:S(2)}) copy-start(f32[2,8,2,32,128]{4,3,2,1,0:T(8,128)} %copy-done.10) | copy-start | bytes 1572868
  105.3 20.4 %copy-start.13 = (f32[2,8,2,32,128]{4,3,2,1,0:T(8,128)S(1)}, f32[2,8,2,32,128]{4,3,2,1,0:T(8,128)}, u32[]{:S(2)}) copy-start(f32[2,8,2,32,128]{4,3,2,1,0:T(8,128)} %copy-done.12) | copy-start | bytes 1572868
  109.2 34.7 %copy-start.16 = (f32[2,8,2,32,128]{4,3,2,1,0:T(8,128)S(1)}, f32[2,8,2,32,128]{4,3,2,1,0:T(8,128)}, u32[]{:S(2)}) copy-start(f32[2,8,2,32,128]{4,3,2,1,0:T(8,128)} %copy-done.15) | copy-start | bytes 1572868
  109.2 34.7 %copy-start.18 = (f32[2,8,2,32,128]{4,3,2,1,0:T(8,128)S(1)}, f32[2,8,2,32,128]{4,3,2,1,0:T(8,128)}, u32[]{:S(2)}) copy-start(f32[2,8,2,32,128]{4,3,2,1,0:T(8,128)} %copy-done.17) | copy-start | bytes 1572868
  143.9 19.4 %copy-start.9 = (f32[2,8,2,32,128]{4,3,2,1,0:T(8,128)S(1)}, f32[2,8,2,32,128]{4,3,2,1,0:T(8,128)}, u32[]{:S(2)}) copy-start(f32[2,8,2,32,128]{4,3,2,1,0:T(8,128)} %copy-done.8) | copy-start | bytes 1572868

commit v2 on v1

v2 whole, which is shorter than its diff:
```python
import functools
import math

import jax
import jax.numpy as jnp
import numpy as np
from jax import lax
from jax.experimental import pallas as pl
from jax.experimental.pallas import tpu as pltpu
from jax.sharding import PartitionSpec as P

ratio_base = 0.75
ratio_step = 1.0 / 128.0
prop_scale = 150.0
core_step = 0.8
tilt_step = 8
angle_side = 8

LANES = 128
GROUPS = 8
GRID = GROUPS * LANES
WIDE = 32
PEERS = GRID // WIDE
SHARE = 2
FOLD = LANES // WIDE
CHUNK = 16
VMEM_LIMIT = 48 * 1024 * 1024


def dft_tables():
    counter = np.arange(LANES)
    angle = -2.0 * np.pi / LANES * (counter[:, None] * counter[None, :] % LANES)
    real, imag = np.cos(angle), np.sin(angle)
    full = np.block([[real, imag], [-imag, real]]).astype(np.float32)
    high = full.astype(jnp.bfloat16)
    low = (full - high.astype(np.float32)).astype(jnp.bfloat16)
    return high, low


def cos_sin(angle):
    turns = jnp.floor(angle * (2.0 / math.pi) + 0.5)
    rest = angle - turns * 1.5703125
    rest = rest - turns * 4.837512969970703e-4
    rest = rest - turns * 7.549789948768648e-8
    square = rest * rest
    sine = rest + rest * square * (
        -1.6666654611e-1 + square * (8.3321608736e-3 + square * -1.9515295891e-4)
    )
    cosine = (1.0 - 0.5 * square) + square * square * (
        4.166664568298827e-2 + square * (-1.388731625493765e-3 + square * 2.443315711809948e-5)
    )
    quarter = turns.astype(jnp.int32)
    swap = (quarter & 1) != 0
    cos_part = jnp.where(swap, sine, cosine)
    sin_part = jnp.where(swap, cosine, sine)
    cos_part = jnp.where(((quarter + 1) & 2) != 0, -cos_part, cos_part)
    sin_part = jnp.where((quarter & 2) != 0, -sin_part, sin_part)
    return cos_part, sin_part


def times(left, right):
    return (
        left[0] * right[0] - left[1] * right[1],
        left[0] * right[1] + left[1] * right[0],
    )


def times_conj(left, right):
    return (
        left[0] * right[0] + left[1] * right[1],
        left[1] * right[0] - left[0] * right[1],
    )


def plus(left, right):
    return (left[0] + right[0], left[1] + right[1])


def minus(left, right):
    return (left[0] - right[0], left[1] - right[1])


def quarter_turn(value, sign):
    if sign > 0:
        return (-value[1], value[0])
    return (value[1], -value[0])


def dft4(items, sign):
    even, odd = plus(items[0], items[2]), minus(items[0], items[2])
    other, rest = plus(items[1], items[3]), minus(items[1], items[3])
    rest = quarter_turn(rest, sign)
    return [plus(even, other), plus(odd, rest), minus(even, other), minus(odd, rest)]


def dft8(items, sign):
    even, odd = dft4(items[0::2], sign), dft4(items[1::2], sign)
    half = math.sqrt(0.5)
    first, third = odd[1], odd[3]
    if sign > 0:
        first = ((first[0] - first[1]) * half, (first[0] + first[1]) * half)
        third = ((-third[0] - third[1]) * half, (third[0] - third[1]) * half)
    else:
        first = ((first[0] + first[1]) * half, (first[1] - first[0]) * half)
        third = ((third[1] - third[0]) * half, (-third[0] - third[1]) * half)
    odd = [odd[0], first, quarter_turn(odd[2], sign), third]
    return [plus(e, o) for e, o in zip(even, odd)] + [minus(e, o) for e, o in zip(even, odd)]


def matmul_pair(left, right, high, low):
    both = jnp.concatenate([left, right], axis=1)
    upper = both.astype(jnp.bfloat16)
    lower = (both - upper.astype(jnp.float32)).astype(jnp.bfloat16)
    product = functools.partial(jnp.dot, preferred_element_type=jnp.float32)
    result = product(upper, high) + (product(lower, high) + product(upper, low))
    return result[:, :LANES], result[:, LANES:]


def filter_lines(wave, picks, twist, high, low, sign):
    rows = wave[0][0].shape[0]

    def stack(items, part):
        return jnp.concatenate([item[part] for item in items], axis=0)

    def pieces(real, imag):
        return [(real[k * rows : (k + 1) * rows], imag[k * rows : (k + 1) * rows]) for k in range(GROUPS)]

    parts = dft8(wave, -1)
    parts = [parts[0]] + [times(parts[k], twist[k]) for k in range(1, GROUPS)]
    spectrum = pieces(*matmul_pair(stack(parts, 0), stack(parts, 1), high, low))
    multiply = times if sign > 0 else times_conj
    spectrum = [multiply(value, pick) for value, pick in zip(spectrum, picks)]
    imag, real = matmul_pair(stack(spectrum, 1), stack(spectrum, 0), high, low)
    parts = pieces(real, imag)
    parts = [parts[0]] + [times_conj(parts[k], twist[k]) for k in range(1, GROUPS)]
    return dft8(parts, 1)


def line_filter(field, filters, twist, high, low, sign):
    result = []
    for wave, picks in zip(field, filters):
        chunks = []
        for first in range(0, WIDE, CHUNK):
            part = [(real[first : first + CHUNK], imag[first : first + CHUNK]) for real, imag in wave]
            chunks.append(filter_lines(part, picks, twist, high, low, sign))
        result.append(
            [
                tuple(jnp.concatenate([chunk[group][part] for chunk in chunks], axis=0) for part in range(2))
                for group in range(GROUPS)
            ]
        )
    return result


def exchange_blocks(items):
    lane = lax.broadcasted_iota(jnp.int32, items[0].shape, items[0].ndim - 1)
    axis = items[0].ndim - 1
    low_half, even = (lane & 64) == 0, (lane & 32) == 0
    halves = [None] * 4
    for i in range(2):
        halves[i] = jnp.where(low_half, items[i], pltpu.roll(items[i + 2], 64, axis))
        halves[i + 2] = jnp.where(low_half, pltpu.roll(items[i], 64, axis), items[i + 2])
    result = [None] * 4
    for i in (0, 2):
        result[i] = jnp.where(even, halves[i], pltpu.roll(halves[i + 1], 32, axis))
        result[i + 1] = jnp.where(even, pltpu.roll(halves[i], LANES - 32, axis), halves[i + 1])
    return result


def load_field(blocks_ref):
    turned = [
        jnp.concatenate([blocks_ref[GROUPS * i + j, :WIDE] for i in range(FOLD)], axis=0).T
        for j in range(GROUPS)
    ]
    field = [[[None, None] for _ in range(GROUPS)] for _ in range(SHARE)]
    for part in range(2):
        for wave in range(SHARE):
            first = (part * SHARE + wave) * WIDE
            for half in range(GROUPS // FOLD):
                rows = [turned[half * FOLD + i][first : first + WIDE] for i in range(FOLD)]
                points = jnp.concatenate(rows, axis=0).T
                for i in range(FOLD):
                    group = i * (GROUPS // FOLD) + half
                    field[wave][group][part] = points[i * WIDE : (i + 1) * WIDE]
    return field


def store_field(blocks_ref, field):
    for group in range(GROUPS):
        rows = [field[w][group][part] for part in range(2) for w in range(SHARE)]
        turned = jnp.concatenate(rows, axis=0).T
        for i in range(FOLD):
            blocks_ref[FOLD * group + i, :WIDE] = turned[i * WIDE : (i + 1) * WIDE]


def pack_plane(plane):
    blocks = []
    for group in range(GROUPS):
        rows = [plane[group]] + [pltpu.roll(plane[group], LANES - 8 * q, 1) for q in range(1, FOLD)]
        turned = jnp.concatenate(rows, axis=0).T
        blocks += [turned[i * WIDE : i * WIDE + 8] for i in range(FOLD)]
    return blocks


def unpack_plane(blocks):
    plane = []
    for group in range(GROUPS):
        items = exchange_blocks(blocks[FOLD * group : FOLD * (group + 1)])
        plane.append(jnp.concatenate(items, axis=0))
    return plane


def ratio_of(place_ref, wave):
    number = place_ref[2 + place_ref[0] * SHARE + wave]
    return ratio_base + ratio_step * number.astype(jnp.float32)


def filters_of(place_ref):
    row = lax.broadcasted_iota(jnp.int32, (GROUPS, LANES), 0)
    lane = lax.broadcasted_iota(jnp.int32, (GROUPS, LANES), 1)
    natural = row + GROUPS * lane
    signed = jnp.where(natural < GRID // 2, natural, natural - GRID)
    scaled = signed.astype(jnp.float32) * (2.0 / GRID)
    squares = scaled * scaled
    filters = []
    for wave in range(SHARE):
        real, imag = cos_sin((-prop_scale * ratio_of(place_ref, wave)) * squares)
        real, imag = real * (1.0 / GRID), imag * (1.0 / GRID)
        filters.append([(real[k : k + 1], imag[k : k + 1]) for k in range(GROUPS)])
    return filters


def twists():
    row = lax.broadcasted_iota(jnp.int32, (GROUPS, LANES), 0)
    lane = lax.broadcasted_iota(jnp.int32, (GROUPS, LANES), 1)
    real, imag = cos_sin((-2.0 * math.pi / GRID) * (row * lane).astype(jnp.float32))
    return [(real[k : k + 1], imag[k : k + 1]) for k in range(GROUPS)]


def inverse_ratio(place_ref, wave):
    ratio = ratio_of(place_ref, wave)
    return 1.0 / jnp.full((8, LANES), ratio, jnp.float32)[:1]


def copies(pairs, sems):
    return [pltpu.make_async_copy(source, target, sems.at[i]) for i, (source, target) in enumerate(pairs)]


def start(moves):
    for move in moves:
        move.start()


def wait(moves):
    for move in moves:
        move.wait()


def launch_kernel(
    waves,
    place_ref,
    illum_hbm,
    high_hbm,
    low_hbm,
    measured_hbm,
    out_ref,
    target_ref,
    illum_ref,
    high_ref,
    low_ref,
    measured_ref,
    sems,
):
    own = measured_hbm.at[pl.ds(place_ref[0] * SHARE, SHARE)]
    moves = copies(
        [(illum_hbm, illum_ref), (high_hbm, high_ref), (low_hbm, low_ref), (own, measured_ref)], sems
    )
    start(moves)
    twist = twists()
    filters = filters_of(place_ref)
    tilted = []
    for wave in range(SHARE):
        pick = place_ref[2 + waves + place_ref[0] * SHARE + wave]
        tilt_x = ((pick & (angle_side - 1)) - angle_side // 2) * tilt_step
        tilt_y = ((pick >> 3) - angle_side // 2) * tilt_step
        row = lax.broadcasted_iota(jnp.int32, (WIDE, LANES), 0) + place_ref[1] * WIDE

        def wheel(product):
            turned = ((product + GRID // 2) & (GRID - 1)) - GRID // 2
            return cos_sin((2.0 * math.pi / GRID) * turned.astype(jnp.float32))

        down = wheel(tilt_y * row)
        groups = []
        for group in range(GROUPS):
            column = lax.broadcasted_iota(jnp.int32, (8, LANES), 1) + group * LANES
            across = wheel(tilt_x * column)
            groups.append(times(down, (across[0][:1], across[1][:1])))
        tilted.append(groups)
    wait(moves[:3])
    field = []
    for wave in range(SHARE):
        groups = []
        for group in range(GROUPS):
            bright = illum_ref[:, group * LANES : (group + 1) * LANES]
            groups.append((bright * tilted[wave][group][0], bright * tilted[wave][group][1]))
        field.append(groups)
    field = line_filter(field, filters, twist, high_ref[...], low_ref[...], 1)
    store_field(out_ref, field)
    wait(moves[3:])
    for wave in range(SHARE):
        for part in range(2):
            target_ref[wave, part] = measured_ref[wave, :, part]


def save(kept_ref, field):
    for wave in range(SHARE):
        for group in range(GROUPS):
            for part in range(2):
                kept_ref[wave, group, part] = field[wave][group][part]


def kept(kept_ref):
    return [
        [(kept_ref[wave, group, 0], kept_ref[wave, group, 1]) for group in range(GROUPS)]
        for wave in range(SHARE)
    ]


def read_base(base_refs, layer, place_ref):
    slot = (place_ref[0] - layer) & 3

    def block(index):
        value = base_refs[0][index]
        for shift in range(1, len(base_refs)):
            value = jnp.where(slot == shift, base_refs[shift][index], value)
        return value

    if layer % 2:
        return [
            jnp.concatenate([block(tile * GROUPS + group) for tile in range(FOLD)], axis=0)
            for group in range(GROUPS)
        ]
    return unpack_plane([block(peer) for peer in range(PEERS)])


def screens(base_refs, layer, place_ref):
    base = read_base(base_refs, layer, place_ref)
    result = []
    for wave in range(SHARE):
        scale = inverse_ratio(place_ref, wave)
        result.append([cos_sin(base[group] * scale) for group in range(GROUPS)])
    return result


def gradient(adjoint, field, place_ref):
    total = [None] * GROUPS
    for wave in range(SHARE):
        scale = inverse_ratio(place_ref, wave)
        for group in range(GROUPS):
            left, right = adjoint[wave][group], field[wave][group]
            term = (left[1] * right[0] - left[0] * right[1]) * scale
            total[group] = term if wave == 0 else total[group] + term
    return total


def each(function, left, right):
    return [[function(a, b) for a, b in zip(p, q)] for p, q in zip(left, right)]


def forward_kernel(
    layer, place_ref, in_ref, high_ref, low_ref, base_0, base_1, base_2, base_3, out_ref, field_ref, *screen_ref
):
    high, low, twist = high_ref[...], low_ref[...], twists()
    filters = filters_of(place_ref)
    field = line_filter(load_field(in_ref), filters, twist, high, low, 1)
    screen = screens((base_0, base_1, base_2, base_3), layer, place_ref)
    if layer:
        save(screen_ref[0], screen)
    field = each(times, field, screen)
    save(field_ref, field)
    store_field(out_ref, line_filter(field, filters, twist, high, low, 1))


def turn_kernel(
    place_ref, in_ref, high_ref, low_ref, base_0, base_1, base_2, base_3, target_ref, out_ref
):
    high, low, twist = high_ref[...], low_ref[...], twists()
    filters = filters_of(place_ref)
    field = line_filter(load_field(in_ref), filters, twist, high, low, 1)
    screen = screens((base_0, base_1, base_2, base_3), 3, place_ref)
    field = each(times, field, screen)
    adjoint = []
    for wave in range(SHARE):
        groups = []
        for group in range(GROUPS):
            lanes = slice(group * LANES, (group + 1) * LANES)
            goal = (target_ref[wave, 0, :, lanes], target_ref[wave, 1, :, lanes])
            groups.append(minus(field[wave][group], goal))
        adjoint.append(groups)
    blocks = pack_plane(gradient(adjoint, field, place_ref))
    for peer in range(PEERS):
        out_ref[peer, WIDE:] = blocks[peer]
    adjoint = each(times_conj, adjoint, screen)
    store_field(out_ref, line_filter(adjoint, filters, twist, high, low, -1))


def adjoint_kernel(
    with_plane, place_ref, in_ref, high_ref, low_ref, field_ref, screen_ref, out_ref, *grad_ref
):
    high, low, twist = high_ref[...], low_ref[...], twists()
    filters = filters_of(place_ref)
    adjoint = line_filter(load_field(in_ref), filters, twist, high, low, -1)
    grad = gradient(adjoint, kept(field_ref), place_ref)
    if with_plane:
        blocks = pack_plane(grad)
        for peer in range(PEERS):
            out_ref[peer, WIDE:] = blocks[peer]
    else:
        for group in range(GROUPS):
            grad_ref[0][group] = grad[group]
    adjoint = each(times_conj, adjoint, kept(screen_ref))
    store_field(out_ref, line_filter(adjoint, filters, twist, high, low, -1))


def last_kernel(place_ref, in_ref, high_ref, low_ref, third_ref, second_ref, field_ref, out_ref):
    high, low, twist = high_ref[...], low_ref[...], twists()
    filters = filters_of(place_ref)
    adjoint = line_filter(load_field(in_ref), filters, twist, high, low, -1)
    planes = [
        gradient(adjoint, kept(field_ref), place_ref),
        unpack_plane([in_ref[peer, WIDE:] for peer in range(PEERS)]),
        [second_ref[group] for group in range(GROUPS)],
        unpack_plane([third_ref[peer, WIDE:] for peer in range(PEERS)]),
    ]
    for group in range(GROUPS):
        turned = jnp.concatenate([plane[group] for plane in planes], axis=0).T
        for i in range(FOLD):
            rows = [turned[i * WIDE + 8 * q : i * WIDE + 8 * (q + 1)] for q in range(FOLD)]
            for layer, block in enumerate(exchange_blocks(rows)):
                out_ref[layer * PEERS + group * FOLD + i] = block


def sum_kernel(in_ref, out_ref):
    total = [
        (in_ref[peer] + in_ref[PEERS + peer]) + (in_ref[2 * PEERS + peer] + in_ref[3 * PEERS + peer])
        for peer in range(PEERS)
    ]
    plane = unpack_plane(total)
    for group in range(GROUPS):
        out_ref[0, :, group * LANES : (group + 1) * LANES] = plane[group]


def base_kernel(slice_hbm, mask_hbm, rows_ref, out_ref, slice_ref, mask_ref, sems):
    moves = copies([(slice_hbm, slice_ref), (mask_hbm, mask_ref)], sems)
    start(moves)
    wait(moves)
    base = []
    for group in range(GROUPS):
        lanes = slice(group * LANES, (group + 1) * LANES)
        plane = core_step * mask_ref[:, lanes].astype(jnp.float32) + slice_ref[0, :, lanes]
        base.append(plane)
        for tile in range(FOLD):
            rows_ref[tile * GROUPS + group] = plane[tile * 8 : (tile + 1) * 8]
    blocks = pack_plane(base)
    for peer in range(PEERS):
        out_ref[peer] = blocks[peer]


def call(kernel, scalars, near, far, outs, scratch=(), moves=1):
    specs = [pl.BlockSpec(memory_space=pltpu.SMEM)] * len(scalars)
    specs += [pl.BlockSpec(memory_space=pltpu.VMEM)] * len(near)
    specs += [pl.BlockSpec(memory_space=pltpu.HBM)] * len(far)
    scratch = [pltpu.VMEM(shape, dtype) for shape, dtype in scratch]
    if scratch:
        scratch.append(pltpu.SemaphoreType.DMA((moves,)))
    return pl.pallas_call(
        kernel,
        out_shape=[place(shape, jnp.float32) for shape, place in outs],
        in_specs=specs,
        out_specs=[pl.BlockSpec(memory_space=pltpu.VMEM)] * len(outs),
        scratch_shapes=scratch,
        compiler_params=pltpu.CompilerParams(vmem_limit_bytes=VMEM_LIMIT),
    )(*scalars, *near, *far)


def near(shape):
    return (shape, pltpu.VMEM)


def free(shape):
    return (shape, jax.ShapeDtypeStruct)


def in_hbm(*arrays):
    return tuple(pltpu.with_memory_space_constraint(array, pltpu.HBM) for array in arrays)


def body(index_slices, core_mask, illum_amp, measured, wave_ids, angle_ids):
    row_pos, sec_pos = lax.axis_index("row"), lax.axis_index("sec")
    sec_count, waves = lax.axis_size("sec"), wave_ids.shape[0]
    tables = tuple(jnp.asarray(table) for table in dft_tables())
    place = jnp.concatenate([sec_pos[None], row_pos[None], wave_ids, angle_ids]).astype(jnp.int32)
    swap = functools.partial(lax.all_to_all, axis_name="row", split_axis=0, concat_axis=0, tiled=True)
    blocks, small = (PEERS, WIDE, LANES), (PEERS, 8, LANES)
    wide_blocks = (PEERS, WIDE + 8, LANES)
    saved = (SHARE, GROUPS, 2, WIDE, LANES)
    table = ((2 * LANES, 2 * LANES), jnp.bfloat16)
    base_rows, base_blocks = call(
        base_kernel,
        (),
        (),
        in_hbm(index_slices, core_mask),
        (free(small), free(small)),
        scratch=((index_slices.shape, jnp.float32), (core_mask.shape, jnp.int32)),
        moves=2,
    )
    sent, target = call(
        functools.partial(launch_kernel, waves),
        (place,),
        (),
        in_hbm(illum_amp, *tables, measured),
        (free(blocks), near((SHARE, 2, WIDE, GRID))),
        scratch=(
            (illum_amp.shape, jnp.float32),
            table,
            table,
            ((SHARE, *measured.shape[1:]), jnp.float32),
        ),
        moves=4,
    )
    base_own = jnp.where(sec_pos % 2 == 0, swap(base_blocks), base_rows)
    base = [base_own]
    for shift in range(1, sec_count):
        base.append(lax.ppermute(base_own, "sec", [(i, (i + shift) % sec_count) for i in range(sec_count)]))
    fields, screen = [], []
    for layer in range(3):
        sent, field_now, *screen_now = call(
            functools.partial(forward_kernel, layer),
            (place,),
            (swap(sent), *tables, *base),
            (),
            (free(blocks),) + (near(saved),) * (2 if layer else 1),
        )
        fields.append(field_now)
        screen += screen_now
    (sent,) = call(
        turn_kernel,
        (place,),
        (swap(sent), *tables, *base, target),
        (),
        (free(wide_blocks),),
    )
    third = swap(sent)
    sent, second = call(
        functools.partial(adjoint_kernel, False),
        (place,),
        (third, *tables, fields[2], screen[1]),
        (),
        (free(blocks), near((GROUPS, WIDE, LANES))),
    )
    (sent,) = call(
        functools.partial(adjoint_kernel, True),
        (place,),
        (swap(sent), *tables, fields[1], screen[0]),
        (),
        (free(wide_blocks),),
    )
    (grads,) = call(
        last_kernel,
        (place,),
        (swap(sent), *tables, third, second, fields[0]),
        (),
        (free((4 * PEERS, 8, LANES)),),
    )
    grads = lax.all_to_all(grads, ("sec", "row"), 0, 0, tiled=True)
    (result,) = call(sum_kernel, (), (grads,), (), (free((1, WIDE, GRID)),))
    return result


def solution(mesh):
    in_specs = (
        P("sec", "row", None),
        P("row", None),
        P("row", None),
        P(None, "row", None, None),
        P(),
        P(),
    )
    out_specs = P("sec", "row", None)
    return jax.shard_map(body, mesh=mesh, in_specs=in_specs, out_specs=out_specs, check_vma=False)
```

time: 187 us -> 169 us (0.904)
  local copies, waits for them, and re-layouts: 13.3 us -> 0.01 us
  Pallas kernels: 27.7 us -> 24.3 us
  starting transfers between devices: 20.6 us -> 17.4 us
    all_to_all x4 -> x5, blocking collectives: 66.9 us -> 80.6 us  [body(): swap(sent)]
    unnamed x50 -> x4, local copies, waits for them, and re-layouts: 12.5 us -> 0.01 us
    all_to_all x2 -> x1, waiting for transfers between devices: 11.1 us -> 0.01 us  [body(): swap(sent)]
    all_gather x1 -> x0, blocking collectives: 11 us -> none  [body(): base = lax.all_gather(base_own, 'sec', axis=0)]
    ppermute x0 -> x3, waiting for transfers between devices: none -> 8.6 us  [body(): lax.ppermute(base_own, 'sec', [(i, (i + shift) % sec_count) for i in rang...]
    all_to_all x2 -> x1, starting transfers between devices: 11 us -> 3.94 us  [body(): swap(sent)]
    ppermute x0 -> x3, starting transfers between devices: none -> 3.67 us  [body(): lax.ppermute(base_own, 'sec', [(i, (i + shift) % sec_count) for i in rang...]
    all_to_all x1, waiting for transfers between devices: 0.2 us -> 3.58 us  [body(): base_own = jnp.where(sec_pos % 2 == 0, swap(base_blocks), base_rows)]
  transfers between devices with their start and end apart: 3 -> 5, of which waited for: 3 -> 4; matrix products, arithmetic and copies ran while one was open for 0% -> 0% of each run, Pallas kernels for 1% -> 2%
where the time goes in v2:
time: 169 us
  blocking collectives  114 us (67%)
  Pallas kernels  24.3 us (14%)
  starting transfers between devices  17.4 us (10%)
  waiting for transfers between devices  12.2 us (7%)
    all_to_all x5, blocking collectives, body(): swap(sent)  80.6 us
    pallas_call x10, Pallas kernels, call(): pl.pallas_call(kernel, out_shape=[place(shape, jnp.float32) for shape, pl...  24.3 us
    all_to_all x1, blocking collectives, body(): grads = lax.all_to_all(grads, ('sec', 'row'), 0, 0, tiled=True)  16.9 us
    all_to_all x1, blocking collectives, body(): third = swap(sent)  16.4 us
    all_to_all x1, starting transfers between devices, body(): base_own = jnp.where(sec_pos % 2 == 0, swap(base_blocks), base_rows)  9.74 us
    ppermute x3, waiting for transfers between devices, body(): lax.ppermute(base_own, 'sec', [(i, (i + shift) % sec_count) for i in rang...  8.6 us
    all_to_all x1, starting transfers between devices, body(): swap(sent)  3.94 us
    ppermute x3, starting transfers between devices, body(): lax.ppermute(base_own, 'sec', [(i, (i + shift) % sec_count) for i in rang...  3.67 us
  transfers between devices with their start and end apart: 5, of which 4 were waited for; matrix products, arithmetic and copies ran while one was open for 0% of the time, Pallas kernels for 2%

profile of v2, /device:TPU:1, one launch (start us, length us, event | category | flops | bytes accessed | tf_op | source)
XLA Modules:
  0.0 168.7 jit_solution(6386134694751815197)
XLA Ops:
  0.0 2.0 %shard_map.83 = (f32[32,8,128]{2,1,0:T(8,128)S(1)}, f32[32,8,128]{2,1,0:T(8,128)}) custom-call(f32[1,32,1024]{2,1,0:T(8,128)} %slice_hbm.1, s32[32,1024]{1,0:T(8,128)} %mask_hbm.1), custom_call_target="tpu_custom_call" | custom-call | tf_op jit(solution)/shard_map/pallas_call | solution.py:476
  2.0 0.0 copy-start
  2.0 0.0 copy-start.1
  2.0 9.7 %all-to-all-start.1 = ((f32[32,8,128]{2,1,0:T(8,128)}), f32[32,8,128]{2,1,0:T(8,128)S(1)}, u32[]{:S(2)}, u32[]{:S(2)}) async-start(f32[32,8,128]{2,1,0:T(8,128)} %get-tuple-element.20), calls=%async_computation.1 | async-start | bytes 262144 | tf_op jit(solution)/shard_map/all_to_all | solution.py:531
  11.7 0.8 pad_add_fusion.place_ref
  12.5 3.4 %shard_map.82 = (f32[32,32,128]{2,1,0:T(8,128)}, f32[2,2,32,1024]{3,2,1,0:T(8,128)S(1)}) custom-call(s32[18]{0:T(128)S(1)} %pad_add_fusion.place_ref, f32[32,1024]{1,0:T(8,128)} %illum_hbm.1, bf16[256,256]{1,0:T(8,128)(2,1)} %constant.27.clone.high_hbm.high_ref, bf16[256,256]{1,0:T(8,128)(2,1)} %constant.28.clone.low_hbm.low_ref, f32[8,32,2,1024]{3,2,1,0:T(2,128)} %measured_hbm.1), custom_call_target="tpu_custom_call" | custom-call | tf_op jit(solution)/shard_map/pallas_call | solution.py:476
  15.9 3.6 %all-to-all-done.1 = f32[32,8,128]{2,1,0:T(8,128)S(1)} async-done(((f32[32,8,128]{2,1,0:T(8,128)}), f32[32,8,128]{2,1,0:T(8,128)S(1)}, u32[]{:S(2)}, u32[]{:S(2)}) %all-to-all-start.1) | async-done | bytes 131104 | tf_op jit(solution)/shard_map/all_to_all | solution.py:531
  19.4 3.9 %all-to-all-start = ((f32[32,32,128]{2,1,0:T(8,128)}), f32[32,32,128]{2,1,0:T(8,128)S(1)}, u32[]{:S(2)}, u32[]{:S(2)}) async-start(f32[32,32,128]{2,1,0:T(8,128)} %get-tuple-element.19), calls=%async_computation | async-start | bytes 1048576 | tf_op jit(solution)/shard_map/all_to_all | solution.py:540
  23.4 2.5 %collective-permute-start.2 = (f32[32,8,128]{2,1,0:T(8,128)S(1)}, f32[32,8,128]{2,1,0:T(8,128)S(1)}, u32[]{:S(2)}, u32[]{:S(2)}) collective-permute-start(f32[32,8,128]{2,1,0:T(8,128)S(1)} %broadcast_select_fusion.base_0), channel_id=1, source_target_pairs={{0,96},{32,0},{64,32},{96,64},{1,97},{33,1},{65,33},{97,65},{2,98}... | collective-permute-start | bytes 393224 | tf_op jit(solution)/shard_map/ppermute | solution.py:534
  26.0 0.5 collective-permute-start.1
  26.5 0.6 collective-permute-start
  27.1 4.1 %collective-permute-done.2.base_3 = f32[32,8,128]{2,1,0:T(8,128)S(1)} collective-permute-done((f32[32,8,128]{2,1,0:T(8,128)S(1)}, f32[32,8,128]{2,1,0:T(8,128)S(1)}, u32[]{:S(2)}, u32[]{:S(2)}) %collective-permute-start.2) | collective-permute-done | bytes 131104 | tf_op jit(solution)/shard_map/ppermute | solution.py:534
  31.2 0.7 collective-permute-done.1.base_2
  31.9 3.8 %collective-permute-done.base_1 = f32[32,8,128]{2,1,0:T(8,128)S(1)} collective-permute-done((f32[32,8,128]{2,1,0:T(8,128)S(1)}, f32[32,8,128]{2,1,0:T(8,128)S(1)}, u32[]{:S(2)}, u32[]{:S(2)}) %collective-permute-start) | collective-permute-done | bytes 131104 | tf_op jit(solution)/shard_map/ppermute | solution.py:534
  35.7 0.0 all-to-all-done.in_ref
  35.7 0.0 copy-done
  35.7 0.0 copy-done.1
  35.7 2.6 %shard_map.84 = (f32[32,32,128]{2,1,0:T(8,128)S(1)}, f32[2,8,2,32,128]{4,3,2,1,0:T(8,128)S(1)}) custom-call(s32[18]{0:T(128)S(1)} %pad_add_fusion.place_ref, f32[32,32,128]{2,1,0:T(8,128)S(1)} %all-to-all-done.in_ref, bf16[256,256]{1,0:T(8,128)(2,1)S(1)} %copy-done.1, bf16[256,256]{1,0:T(8,128)(2,1)S(1)} %copy-done, ...), custom_call_target="tpu_custom_call" | custom-call | tf_op jit(solution)/shard_map/pallas_call | solution.py:476
  38.3 19.0 %all_to_all.45.in_ref = f32[32,32,128]{2,1,0:T(8,128)S(1)} all-to-all(f32[32,32,128]{2,1,0:T(8,128)S(1)} %get-tuple-element.22), channel_id=1, replica_groups=mesh['sec'=4,'row'=32] {'row'}, dimensions={0} | all-to-all | bytes 1048576 | tf_op jit(solution)/shard_map/all_to_all | solution.py:540
  57.4 2.7 %shard_map.85 = (f32[32,32,128]{2,1,0:T(8,128)S(1)}, f32[2,8,2,32,128]{4,3,2,1,0:T(8,128)S(1)}, f32[2,8,2,32,128]{4,3,2,1,0:T(8,128)S(1)}) custom-call(s32[18]{0:T(128)S(1)} %pad_add_fusion.place_ref, f32[32,32,128]{2,1,0:T(8,128)S(1)} %all_to_all.45.in_ref, bf16[256,256]{1,0:T(8,128)(2,1)S(1)} %copy-done.1, bf16[256,256]{1,0:T(8,128)(2,1)S(1)} %copy-done, ...), custom_call_target="tpu_custom_call" | custom-call | tf_op jit(solution)/shard_map/pallas_call | solution.py:476
  60.1 15.0 %all_to_all.46.in_ref = f32[32,32,128]{2,1,0:T(8,128)S(1)} all-to-all(f32[32,32,128]{2,1,0:T(8,128)S(1)} %get-tuple-element.23), channel_id=1, replica_groups=mesh['sec'=4,'row'=32] {'row'}, dimensions={0} | all-to-all | bytes 1048576 | tf_op jit(solution)/shard_map/all_to_all | solution.py:540
  75.2 2.6 %shard_map.86 = (f32[32,32,128]{2,1,0:T(8,128)S(1)}, f32[2,8,2,32,128]{4,3,2,1,0:T(8,128)S(1)}, f32[2,8,2,32,128]{4,3,2,1,0:T(8,128)S(1)}) custom-call(s32[18]{0:T(128)S(1)} %pad_add_fusion.place_ref, f32[32,32,128]{2,1,0:T(8,128)S(1)} %all_to_all.46.in_ref, bf16[256,256]{1,0:T(8,128)(2,1)S(1)} %copy-done.1, bf16[256,256]{1,0:T(8,128)(2,1)S(1)} %copy-done, ...), custom_call_target="tpu_custom_call" | custom-call | tf_op jit(solution)/shard_map/pallas_call | solution.py:476
  77.8 15.0 %all_to_all.47.in_ref = f32[32,32,128]{2,1,0:T(8,128)S(1)} all-to-all(f32[32,32,128]{2,1,0:T(8,128)S(1)} %get-tuple-element.24), channel_id=1, replica_groups=mesh['sec'=4,'row'=32] {'row'}, dimensions={0} | all-to-all | bytes 1048576 | tf_op jit(solution)/shard_map/all_to_all | solution.py:549
  92.8 2.8 %shard_map.87 = f32[32,40,128]{2,1,0:T(8,128)S(1)} custom-call(s32[18]{0:T(128)S(1)} %pad_add_fusion.place_ref, f32[32,32,128]{2,1,0:T(8,128)S(1)} %all_to_all.47.in_ref, bf16[256,256]{1,0:T(8,128)(2,1)S(1)} %copy-done.1, bf16[256,256]{1,0:T(8,128)(2,1)S(1)} %copy-done, f32[32,8,128]{2,1,0:T(8,128)S(1)} %broadcast_select_fusion.base_0, ...), custom_call_target="tpu_custom_call" | custom-call | tf_op jit(solution)/shard_map/pallas_call | solution.py:476
  95.6 16.4 %all_to_all.48.in_ref.third_ref = f32[32,40,128]{2,1,0:T(8,128)S(1)} all-to-all(f32[32,40,128]{2,1,0:T(8,128)S(1)} %shard_map.87), channel_id=1, replica_groups=mesh['sec'=4,'row'=32] {'row'}, dimensions={0} | all-to-all | bytes 1310720 | tf_op jit(solution)/shard_map/all_to_all | solution.py:553
  112.0 2.4 %shard_map.88 = (f32[32,32,128]{2,1,0:T(8,128)S(1)}, f32[8,32,128]{2,1,0:T(8,128)S(1)}) custom-call(s32[18]{0:T(128)S(1)} %pad_add_fusion.place_ref, f32[32,40,128]{2,1,0:T(8,128)S(1)} %all_to_all.48.in_ref.third_ref, bf16[256,256]{1,0:T(8,128)(2,1)S(1)} %copy-done.1, bf16[256,256]{1,0:T(8,128)(2,1)S(1)} %copy-done, ...), custom_call_target="tpu_custom_call" | custom-call | tf_op jit(solution)/shard_map/pallas_call | solution.py:476
  114.4 15.1 %all_to_all.49.in_ref = f32[32,32,128]{2,1,0:T(8,128)S(1)} all-to-all(f32[32,32,128]{2,1,0:T(8,128)S(1)} %get-tuple-element.28), channel_id=1, replica_groups=mesh['sec'=4,'row'=32] {'row'}, dimensions={0} | all-to-all | bytes 1048576 | tf_op jit(solution)/shard_map/all_to_all | solution.py:564
  129.5 2.4 %shard_map.89 = f32[32,40,128]{2,1,0:T(8,128)S(1)} custom-call(s32[18]{0:T(128)S(1)} %pad_add_fusion.place_ref, f32[32,32,128]{2,1,0:T(8,128)S(1)} %all_to_all.49.in_ref, bf16[256,256]{1,0:T(8,128)(2,1)S(1)} %copy-done.1, bf16[256,256]{1,0:T(8,128)(2,1)S(1)} %copy-done, f32[2,8,2,32,128]{4,3,2,1,0:T(8,128)S(1)} %get-tuple-element.29.field_ref, ...), custom_call_target="tpu_custom_call" | custom-call | tf_op jit(solution)/shard_map/pallas_call | solution.py:476
  132.0 16.4 %all_to_all.50.in_ref = f32[32,40,128]{2,1,0:T(8,128)S(1)} all-to-all(f32[32,40,128]{2,1,0:T(8,128)S(1)} %shard_map.89), channel_id=1, replica_groups=mesh['sec'=4,'row'=32] {'row'}, dimensions={0} | all-to-all | bytes 1310720 | tf_op jit(solution)/shard_map/all_to_all | solution.py:571
  148.3 2.6 %shard_map.90 = f32[128,8,128]{2,1,0:T(8,128)S(1)} custom-call(s32[18]{0:T(128)S(1)} %pad_add_fusion.place_ref, f32[32,40,128]{2,1,0:T(8,128)S(1)} %all_to_all.50.in_ref, bf16[256,256]{1,0:T(8,128)(2,1)S(1)} %copy-done.1, bf16[256,256]{1,0:T(8,128)(2,1)S(1)} %copy-done, f32[32,40,128]{2,1,0:T(8,128)S(1)} %all_to_all.48.in_ref.third_ref, ...), custom_call_target="tpu_custom_call" | custom-call | tf_op jit(solution)/shard_map/pallas_call | solution.py:476
  151.0 16.9 %all_to_all.51.in_ref = f32[128,8,128]{2,1,0:T(8,128)S(1)} all-to-all(f32[128,8,128]{2,1,0:T(8,128)S(1)} %shard_map.90), channel_id=1, replica_groups=mesh['sec'=4,'row'=32] {'sec','row'}, dimensions={0} | all-to-all | bytes 1048576 | tf_op jit(solution)/shard_map/all_to_all | solution.py:575
  167.8 0.8 shard_map.91
  (1 shorter events, 0.0 us)
Async XLA Ops:
  2.0 33.7 %copy-start = (bf16[256,256]{1,0:T(8,128)(2,1)S(1)}, bf16[256,256]{1,0:T(8,128)(2,1)}, u32[]{:S(2)}) copy-start(bf16[256,256]{1,0:T(8,128)(2,1)} %constant.28.clone.low_hbm.low_ref) | copy-start | bytes 393220
  2.0 33.7 %copy-start.1 = (bf16[256,256]{1,0:T(8,128)(2,1)S(1)}, bf16[256,256]{1,0:T(8,128)(2,1)}, u32[]{:S(2)}) copy-start(bf16[256,256]{1,0:T(8,128)(2,1)} %constant.27.clone.high_hbm.high_ref) | copy-start | bytes 393220
  2.0 17.5 %all-to-all-start.1 = ((f32[32,8,128]{2,1,0:T(8,128)}), f32[32,8,128]{2,1,0:T(8,128)S(1)}, u32[]{:S(2)}, u32[]{:S(2)}) async-start(f32[32,8,128]{2,1,0:T(8,128)} %get-tuple-element.20), calls=%async_computation.1 | async-start | bytes 262144 | tf_op jit(solution)/shard_map/all_to_all | solution.py:531
  19.4 16.3 %all-to-all-start = ((f32[32,32,128]{2,1,0:T(8,128)}), f32[32,32,128]{2,1,0:T(8,128)S(1)}, u32[]{:S(2)}, u32[]{:S(2)}) async-start(f32[32,32,128]{2,1,0:T(8,128)} %get-tuple-element.19), calls=%async_computation | async-start | bytes 1048576 | tf_op jit(solution)/shard_map/all_to_all | solution.py:540
  23.4 7.7 %collective-permute-start.2 = (f32[32,8,128]{2,1,0:T(8,128)S(1)}, f32[32,8,128]{2,1,0:T(8,128)S(1)}, u32[]{:S(2)}, u32[]{:S(2)}) collective-permute-start(f32[32,8,128]{2,1,0:T(8,128)S(1)} %broadcast_select_fusion.base_0), channel_id=1, source_target_pairs={{0,96},{32,0},{64,32},{96,64},{1,97},{33,1},{65,33},{97,65},{2,98}... | collective-permute-start | bytes 393224 | tf_op jit(solution)/shard_map/ppermute | solution.py:534
  26.0 5.9 %collective-permute-start.1 = (f32[32,8,128]{2,1,0:T(8,128)S(1)}, f32[32,8,128]{2,1,0:T(8,128)S(1)}, u32[]{:S(2)}, u32[]{:S(2)}) collective-permute-start(f32[32,8,128]{2,1,0:T(8,128)S(1)} %broadcast_select_fusion.base_0), channel_id=1, source_target_pairs={{0,64},{32,96},{64,0},{96,32},{1,65},{33,97},{65,1},{97,33},{2,66}... | collective-permute-start | bytes 393224 | tf_op jit(solution)/shard_map/ppermute | solution.py:534
  26.5 9.2 %collective-permute-start = (f32[32,8,128]{2,1,0:T(8,128)S(1)}, f32[32,8,128]{2,1,0:T(8,128)S(1)}, u32[]{:S(2)}, u32[]{:S(2)}) collective-permute-start(f32[32,8,128]{2,1,0:T(8,128)S(1)} %broadcast_select_fusion.base_0), channel_id=1, source_target_pairs={{0,32},{32,64},{64,96},{96,0},{1,33},{33,65},{65,97},{97,1},{2,34}... | collective-permute-start | bytes 393224 | tf_op jit(solution)/shard_map/ppermute | solution.py:534

commit v3 on v2

--- a/solution.py
+++ b/solution.py
@@ -167,9 +167,9 @@
     return result
 
 
-def load_field(blocks_ref):
+def load_field(blocks_ref, start):
     turned = [
-        jnp.concatenate([blocks_ref[GROUPS * i + j, :WIDE] for i in range(FOLD)], axis=0).T
+        jnp.concatenate([blocks_ref[GROUPS * i + j, start : start + WIDE] for i in range(FOLD)], axis=0).T
         for j in range(GROUPS)
     ]
     field = [[[None, None] for _ in range(GROUPS)] for _ in range(SHARE)]
@@ -185,12 +185,12 @@
     return field
 
 
-def store_field(blocks_ref, field):
+def store_field(blocks_ref, start, field):
     for group in range(GROUPS):
         rows = [field[w][group][part] for part in range(2) for w in range(SHARE)]
         turned = jnp.concatenate(rows, axis=0).T
         for i in range(FOLD):
-            blocks_ref[FOLD * group + i, :WIDE] = turned[i * WIDE : (i + 1) * WIDE]
+            blocks_ref[FOLD * group + i, start : start + WIDE] = turned[i * WIDE : (i + 1) * WIDE]
 
 
 def pack_plane(plane):
@@ -200,6 +200,16 @@
         turned = jnp.concatenate(rows, axis=0).T
         blocks += [turned[i * WIDE : i * WIDE + 8] for i in range(FOLD)]
     return blocks
+
+
+def store_plane(blocks_ref, start, plane):
+    blocks = pack_plane(plane)
+    for peer in range(PEERS):
+        blocks_ref[peer, start : start + 8] = blocks[peer]
+
+
+def load_plane(blocks_ref, start):
+    return unpack_plane([blocks_ref[peer, start : start + 8] for peer in range(PEERS)])
 
 
 def unpack_plane(blocks):
@@ -305,7 +315,7 @@
             groups.append((bright * tilted[wave][group][0], bright * tilted[wave][group][1]))
         field.append(groups)
     field = line_filter(field, filters, twist, high_ref[...], low_ref[...], 1)
-    store_field(out_ref, field)
+    store_field(out_ref, 0, field)
     wait(moves[3:])
     for wave in range(SHARE):
         for part in range(2):
@@ -326,144 +336,127 @@
     ]
 
 
-def read_base(base_refs, layer, place_ref):
-    slot = (place_ref[0] - layer) & 3
-
-    def block(index):
-        value = base_refs[0][index]
-        for shift in range(1, len(base_refs)):
-            value = jnp.where(slot == shift, base_refs[shift][index], value)
-        return value
-
-    if layer % 2:
-        return [
-            jnp.concatenate([block(tile * GROUPS + group) for tile in range(FOLD)], axis=0)
-            for group in range(GROUPS)
-        ]
-    return unpack_plane([block(peer) for peer in range(PEERS)])
-
-
-def screens(base_refs, layer, place_ref):
-    base = read_base(base_refs, layer, place_ref)
+def screens(base, place_ref):
     result = []
     for wave in range(SHARE):
         scale = inverse_ratio(place_ref, wave)
-        result.append([cos_sin(base[group] * scale) for group in range(GROUPS)])
+        result.append([cos_sin(plane * scale) for plane in base])
     return result
 
 
-def gradient(adjoint, field, place_ref):
+def gradient(target, field, place_ref):
     total = [None] * GROUPS
     for wave in range(SHARE):
         scale = inverse_ratio(place_ref, wave)
         for group in range(GROUPS):
-            left, right = adjoint[wave][group], field[wave][group]
-            term = (left[1] * right[0] - left[0] * right[1]) * scale
+            left, right = target[wave][group], field[wave][group]
+            term = (left[0] * right[1] - left[1] * right[0]) * scale
             total[group] = term if wave == 0 else total[group] + term
     return total
 
 
+def lanes_of(group):
+    return slice(group * LANES, (group + 1) * LANES)
+
+
+def planes_of(ref):
+    return [ref[:, lanes_of(group)] for group in range(GROUPS)]
+
+
+def target_of(target_ref):
+    return [
+        [(target_ref[wave, 0, :, lanes_of(group)], target_ref[wave, 1, :, lanes_of(group)]) for group in range(GROUPS)]
+        for wave in range(SHARE)
+    ]
+
+
 def each(function, left, right):
     return [[function(a, b) for a, b in zip(p, q)] for p, q in zip(left, right)]
 
 
-def forward_kernel(
-    layer, place_ref, in_ref, high_ref, low_ref, base_0, base_1, base_2, base_3, out_ref, field_ref, *screen_ref
+def begin_kernel(
+    place_ref, launched_ref, slices_ref, mask_ref, target_ref, high_ref, low_ref, out_ref, base_ref, screen_ref
 ):
     high, low, twist = high_ref[...], low_ref[...], twists()
     filters = filters_of(place_ref)
-    field = line_filter(load_field(in_ref), filters, twist, high, low, 1)
-    screen = screens((base_0, base_1, base_2, base_3), layer, place_ref)
-    if layer:
-        save(screen_ref[0], screen)
-    field = each(times, field, screen)
-    save(field_ref, field)
-    store_field(out_ref, line_filter(field, filters, twist, high, low, 1))
-
-
-def turn_kernel(
-    place_ref, in_ref, high_ref, low_ref, base_0, base_1, base_2, base_3, target_ref, out_ref
-):
+    mask = [core_step * mask_ref[:, lanes_of(group)].astype(jnp.float32) for group in range(GROUPS)]
+
+    def base_of(layer):
+        return [mask[group] + slices_ref[layer, :, lanes_of(group)] for group in range(GROUPS)]
+
+    for peer in range(PEERS):
+        out_ref[peer, :WIDE] = launched_ref[peer]
+    store_plane(out_ref, 2 * WIDE, base_of(0))
+    store_plane(out_ref, 2 * WIDE + 8, base_of(2))
+    for group, plane in enumerate(base_of(1)):
+        base_ref[:, lanes_of(group)] = plane
+    screen = screens(base_of(3), place_ref)
+    save(screen_ref, screen)
+    target = each(times_conj, target_of(target_ref), screen)
+    store_field(out_ref, WIDE, line_filter(target, filters, twist, high, low, -1))
+
+
+def first_kernel(place_ref, in_ref, high_ref, low_ref, out_ref, field_ref, target_ref, screen_ref):
     high, low, twist = high_ref[...], low_ref[...], twists()
     filters = filters_of(place_ref)
-    field = line_filter(load_field(in_ref), filters, twist, high, low, 1)
-    screen = screens((base_0, base_1, base_2, base_3), 3, place_ref)
-    field = each(times, field, screen)
-    adjoint = []
-    for wave in range(SHARE):
-        groups = []
-        for group in range(GROUPS):
-            lanes = slice(group * LANES, (group + 1) * LANES)
-            goal = (target_ref[wave, 0, :, lanes], target_ref[wave, 1, :, lanes])
-            groups.append(minus(field[wave][group], goal))
-        adjoint.append(groups)
-    blocks = pack_plane(gradient(adjoint, field, place_ref))
-    for peer in range(PEERS):
-        out_ref[peer, WIDE:] = blocks[peer]
-    adjoint = each(times_conj, adjoint, screen)
-    store_field(out_ref, line_filter(adjoint, filters, twist, high, low, -1))
-
-
-def adjoint_kernel(
-    with_plane, place_ref, in_ref, high_ref, low_ref, field_ref, screen_ref, out_ref, *grad_ref
-):
+    field = line_filter(load_field(in_ref, 0), filters, twist, high, low, 1)
+    field = each(times, field, screens(load_plane(in_ref, 2 * WIDE), place_ref))
+    save(field_ref, field)
+    store_field(out_ref, 0, line_filter(field, filters, twist, high, low, 1))
+    target = line_filter(load_field(in_ref, WIDE), filters, twist, high, low, -1)
+    save(target_ref, target)
+    screen = screens(load_plane(in_ref, 2 * WIDE + 8), place_ref)
+    save(screen_ref, screen)
+    target = each(times_conj, target, screen)
+    store_field(out_ref, WIDE, line_filter(target, filters, twist, high, low, -1))
+
+
+def second_kernel(place_ref, in_ref, high_ref, low_ref, base_ref, out_ref, grad_ref):
     high, low, twist = high_ref[...], low_ref[...], twists()
     filters = filters_of(place_ref)
-    adjoint = line_filter(load_field(in_ref), filters, twist, high, low, -1)
-    grad = gradient(adjoint, kept(field_ref), place_ref)
-    if with_plane:
-        blocks = pack_plane(grad)
-        for peer in range(PEERS):
-            out_ref[peer, WIDE:] = blocks[peer]
-    else:
-        for group in range(GROUPS):
-            grad_ref[0][group] = grad[group]
-    adjoint = each(times_conj, adjoint, kept(screen_ref))
-    store_field(out_ref, line_filter(adjoint, filters, twist, high, low, -1))
-
-
-def last_kernel(place_ref, in_ref, high_ref, low_ref, third_ref, second_ref, field_ref, out_ref):
+    screen = screens(planes_of(base_ref), place_ref)
+    field = line_filter(load_field(in_ref, 0), filters, twist, high, low, 1)
+    field = each(times, field, screen)
+    target = line_filter(load_field(in_ref, WIDE), filters, twist, high, low, -1)
+    for group, plane in enumerate(gradient(target, field, place_ref)):
+        grad_ref[:, lanes_of(group)] = plane
+    store_field(out_ref, 0, line_filter(field, filters, twist, high, low, 1))
+    target = each(times_conj, target, screen)
+    store_field(out_ref, WIDE, line_filter(target, filters, twist, high, low, -1))
+
+
+def third_kernel(place_ref, in_ref, high_ref, low_ref, field_ref, target_ref, screen_ref, out_ref):
     high, low, twist = high_ref[...], low_ref[...], twists()
     filters = filters_of(place_ref)
-    adjoint = line_filter(load_field(in_ref), filters, twist, high, low, -1)
+    field = line_filter(load_field(in_ref, 0), filters, twist, high, low, 1)
+    field = each(times, field, kept(screen_ref))
+    store_plane(out_ref, WIDE + 8, gradient(kept(target_ref), field, place_ref))
+    store_field(out_ref, 0, line_filter(field, filters, twist, high, low, 1))
+    target = line_filter(load_field(in_ref, WIDE), filters, twist, high, low, -1)
+    store_plane(out_ref, WIDE, gradient(target, kept(field_ref), place_ref))
+
+
+def last_kernel(place_ref, in_ref, high_ref, low_ref, screen_ref, target_ref, first_ref, out_ref):
+    high, low, twist = high_ref[...], low_ref[...], twists()
+    filters = filters_of(place_ref)
+    field = line_filter(load_field(in_ref, 0), filters, twist, high, low, 1)
+    field = each(times, field, kept(screen_ref))
     planes = [
-        gradient(adjoint, kept(field_ref), place_ref),
-        unpack_plane([in_ref[peer, WIDE:] for peer in range(PEERS)]),
-        [second_ref[group] for group in range(GROUPS)],
-        unpack_plane([third_ref[peer, WIDE:] for peer in range(PEERS)]),
+        load_plane(in_ref, WIDE),
+        planes_of(first_ref),
+        load_plane(in_ref, WIDE + 8),
+        gradient(target_of(target_ref), field, place_ref),
     ]
-    for group in range(GROUPS):
-        turned = jnp.concatenate([plane[group] for plane in planes], axis=0).T
-        for i in range(FOLD):
-            rows = [turned[i * WIDE + 8 * q : i * WIDE + 8 * (q + 1)] for q in range(FOLD)]
-            for layer, block in enumerate(exchange_blocks(rows)):
-                out_ref[layer * PEERS + group * FOLD + i] = block
+    for layer, plane in enumerate(planes):
+        for group in range(GROUPS):
+            out_ref[layer, :, lanes_of(group)] = plane[group]
 
 
 def sum_kernel(in_ref, out_ref):
-    total = [
-        (in_ref[peer] + in_ref[PEERS + peer]) + (in_ref[2 * PEERS + peer] + in_ref[3 * PEERS + peer])
-        for peer in range(PEERS)
-    ]
-    plane = unpack_plane(total)
-    for group in range(GROUPS):
-        out_ref[0, :, group * LANES : (group + 1) * LANES] = plane[group]
-
-
-def base_kernel(slice_hbm, mask_hbm, rows_ref, out_ref, slice_ref, mask_ref, sems):
-    moves = copies([(slice_hbm, slice_ref), (mask_hbm, mask_ref)], sems)
-    start(moves)
-    wait(moves)
-    base = []
-    for group in range(GROUPS):
-        lanes = slice(group * LANES, (group + 1) * LANES)
-        plane = core_step * mask_ref[:, lanes].astype(jnp.float32) + slice_ref[0, :, lanes]
-        base.append(plane)
-        for tile in range(FOLD):
-            rows_ref[tile * GROUPS + group] = plane[tile * 8 : (tile + 1) * 8]
-    blocks = pack_plane(base)
-    for peer in range(PEERS):
-        out_ref[peer] = blocks[peer]
+    total = in_ref[0]
+    for section in range(1, in_ref.shape[0]):
+        total = total + in_ref[section]
+    out_ref[0] = total
 
 
 def call(kernel, scalars, near, far, outs, scratch=(), moves=1):
@@ -500,80 +493,51 @@
     sec_count, waves = lax.axis_size("sec"), wave_ids.shape[0]
     tables = tuple(jnp.asarray(table) for table in dft_tables())
     place = jnp.concatenate([sec_pos[None], row_pos[None], wave_ids, angle_ids]).astype(jnp.int32)
-    swap = functools.partial(lax.all_to_all, axis_name="row", split_axis=0, concat_axis=0, tiled=True)
-    blocks, small = (PEERS, WIDE, LANES), (PEERS, 8, LANES)
-    wide_blocks = (PEERS, WIDE + 8, LANES)
-    saved = (SHARE, GROUPS, 2, WIDE, LANES)
+    swap = functools.partial(lax.all_to_all, split_axis=0, concat_axis=0, tiled=True)
+    plane, saved = (WIDE, GRID), (SHARE, GROUPS, 2, WIDE, LANES)
     table = ((2 * LANES, 2 * LANES), jnp.bfloat16)
-    base_rows, base_blocks = call(
-        base_kernel,
-        (),
-        (),
-        in_hbm(index_slices, core_mask),
-        (free(small), free(small)),
-        scratch=((index_slices.shape, jnp.float32), (core_mask.shape, jnp.int32)),
-        moves=2,
-    )
-    sent, target = call(
+
+    def blocks(rows):
+        return free((PEERS, rows, LANES))
+
+    slices = swap(jnp.broadcast_to(index_slices, (sec_count, *plane)), "sec")
+    launched, target = call(
         functools.partial(launch_kernel, waves),
         (place,),
         (),
         in_hbm(illum_amp, *tables, measured),
-        (free(blocks), near((SHARE, 2, WIDE, GRID))),
-        scratch=(
-            (illum_amp.shape, jnp.float32),
-            table,
-            table,
-            ((SHARE, *measured.shape[1:]), jnp.float32),
-        ),
+        (near((PEERS, WIDE, LANES)), near((SHARE, 2, *plane))),
+        scratch=((plane, jnp.float32), table, table, ((SHARE, *measured.shape[1:]), jnp.float32)),
         moves=4,
     )
-    base_own = jnp.where(sec_pos % 2 == 0, swap(base_blocks), base_rows)
-    base = [base_own]
-    for shift in range(1, sec_count):
-        base.append(lax.ppermute(base_own, "sec", [(i, (i + shift) % sec_count) for i in range(sec_count)]))
-    fields, screen = [], []
-    for layer in range(3):
-        sent, field_now, *screen_now = call(
-            functools.partial(forward_kernel, layer),
-            (place,),
-            (swap(sent), *tables, *base),
-            (),
-            (free(blocks),) + (near(saved),) * (2 if layer else 1),
-        )
-        fields.append(field_now)
-        screen += screen_now
+    sent, base, screen_3 = call(
+        begin_kernel,
+        (place,),
+        (launched, slices, core_mask, target, *tables),
+        (),
+        (blocks(2 * WIDE + 16), near(plane), near(saved)),
+    )
+    sent, field_0, target_2, screen_2 = call(
+        first_kernel, (place,), (swap(sent, "row"), *tables), (), (blocks(2 * WIDE),) + (near(saved),) * 3
+    )
+    sent, grad_1 = call(
+        second_kernel, (place,), (swap(sent, "row"), *tables, base), (), (blocks(2 * WIDE), near(plane))
+    )
     (sent,) = call(
-        turn_kernel,
+        third_kernel,
         (place,),
-        (swap(sent), *tables, *base, target),
+        (swap(sent, "row"), *tables, field_0, target_2, screen_2),
         (),
-        (free(wide_blocks),),
-    )
-    third = swap(sent)
-    sent, second = call(
-        functools.partial(adjoint_kernel, False),
-        (place,),
-        (third, *tables, fields[2], screen[1]),
-        (),
-        (free(blocks), near((GROUPS, WIDE, LANES))),
-    )
-    (sent,) = call(
-        functools.partial(adjoint_kernel, True),
-        (place,),
-        (swap(sent), *tables, fields[1], screen[0]),
-        (),
-        (free(wide_blocks),),
+        (blocks(WIDE + 16),),
     )
     (grads,) = call(
         last_kernel,
         (place,),
-        (swap(sent), *tables, third, second, fields[0]),
+        (swap(sent, "row"), *tables, screen_3, target, grad_1),
         (),
-        (free((4 * PEERS, 8, LANES)),),
-    )
-    grads = lax.all_to_all(grads, ("sec", "row"), 0, 0, tiled=True)
-    (result,) = call(sum_kernel, (), (grads,), (), (free((1, WIDE, GRID)),))
+        (free((sec_count, *plane)),),
+    )
+    (result,) = call(sum_kernel, (), (swap(grads, "sec"),), (), (free((1, *plane)),))
     return result
 
 

time: 169 us -> 132 us (0.78)
  blocking collectives: 114 us -> 101 us
  starting transfers between devices: 17.4 us -> 4.84 us
  waiting for transfers between devices: 12.2 us -> 5.49 us
  Pallas kernels: 24.3 us -> 18 us
  local copies, waits for them, and re-layouts: 0.01 us -> 1.79 us
    all_to_all x7 -> x5, blocking collectives: 114 us -> 101 us  [the longest x4 89.3 us: body(): swap(sent, 'row')]
    all_to_all x2 -> x1, starting transfers between devices: 13.7 us -> 4.84 us  [body(): slices = swap(jnp.broadcast_to(index_slices, (sec_count, *plane)), 'sec')]
    ppermute x3 -> x0, waiting for transfers between devices: 8.6 us -> none  [body(): lax.ppermute(base_own, 'sec', [(i, (i + shift) % sec_count) for i in rang...]
    pallas_call x10 -> x7, Pallas kernels: 24.3 us -> 18 us  [call(): pl.pallas_call(kernel, out_shape=[place(shape, jnp.float32) for shape, pl...]
    ppermute x3 -> x0, starting transfers between devices: 3.67 us -> none  [body(): lax.ppermute(base_own, 'sec', [(i, (i + shift) % sec_count) for i in rang...]
    all_to_all x2 -> x1, waiting for transfers between devices: 3.58 us -> 5.49 us  [body(): slices = swap(jnp.broadcast_to(index_slices, (sec_count, *plane)), 'sec')]
    broadcast_in_dim x0 -> x1, local copies, waits for them, and re-layouts: none -> 1.77 us  [body(): slices = swap(jnp.broadcast_to(index_slices, (sec_count, *plane)), 'sec')]
  transfers between devices with their start and end apart: 5 -> 1, of which waited for: 4 -> 1; matrix products, arithmetic and copies ran while one was open for 0% -> 0% of each run, Pallas kernels for 2% -> 2%
where the time goes in v3:
time: 132 us
  blocking collectives  101 us (77%)
  Pallas kernels  18 us (14%)
  waiting for transfers between devices  5.49 us (4%)
  starting transfers between devices  4.84 us (4%)
  local copies, waits for them, and re-layouts  1.79 us (1%)
    all_to_all x4, blocking collectives, body(): swap(sent, 'row')  89.3 us
    pallas_call x7, Pallas kernels, call(): pl.pallas_call(kernel, out_shape=[place(shape, jnp.float32) for shape, pl...  18 us
    all_to_all x1, blocking collectives, body(): swap(grads, 'sec')  12.1 us
    all_to_all x1, waiting for transfers between devices, body(): slices = swap(jnp.broadcast_to(index_slices, (sec_count, *plane)), 'sec')  5.49 us
    all_to_all x1, starting transfers between devices, body(): slices = swap(jnp.broadcast_to(index_slices, (sec_count, *plane)), 'sec')  4.84 us
  transfers between devices with their start and end apart: 1, of which 1 were waited for; matrix products, arithmetic and copies ran while one was open for 0% of the time, Pallas kernels for 2%

profile of v3, /device:TPU:1, one launch (start us, length us, event | category | flops | bytes accessed | tf_op | source)
XLA Modules:
  0.0 131.7 jit_solution(10250233193886697299)
XLA Ops:
  0.0 0.0 copy-start.3
  0.0 0.0 copy-start.4
  0.0 1.8 %broadcast_in_dim.16 = f32[4,32,1024]{2,1,0:T(8,128)} broadcast(f32[32,1024]{1,0:T(8,128)} %bitcast.3), dimensions={1,2} | broadcast | bytes 655360 | tf_op jit(solution)/shard_map/broadcast_in_dim | solution.py:503
  1.8 4.8 %all-to-all-start = ((f32[4,32,1024]{2,1,0:T(8,128)}), f32[4,32,1024]{2,1,0:T(8,128)S(1)}, u32[]{:S(2)}, u32[]{:S(2)}) async-start(f32[4,32,1024]{2,1,0:T(8,128)} %broadcast_in_dim.16), calls=%async_computation | async-start | bytes 1048576 | tf_op jit(solution)/shard_map/all_to_all | solution.py:503
  6.6 0.0 copy-start
  6.6 0.0 copy-start.1
  6.6 0.0 copy-start.2
  6.6 0.0 copy-done.3
  6.6 0.0 copy-done.4
  6.7 0.1 pad_add_fusion.place_ref
  6.7 2.7 %shard_map.82 = (f32[32,32,128]{2,1,0:T(8,128)S(1)}, f32[2,2,32,1024]{3,2,1,0:T(8,128)S(1)}) custom-call(s32[18]{0:T(128)S(1)} %pad_add_fusion.place_ref, f32[32,1024]{1,0:T(8,128)} %illum_hbm.1, bf16[256,256]{1,0:T(8,128)(2,1)} %constant.13.clone.high_hbm.high_ref, bf16[256,256]{1,0:T(8,128)(2,1)} %constant.14.clone.low_hbm.low_ref, ...), custom_call_target="tpu_custom_call" | custom-call | tf_op jit(solution)/shard_map/pallas_call | solution.py:469
  9.4 5.5 %all-to-all-done.slices_ref = f32[4,32,1024]{2,1,0:T(8,128)S(1)} async-done(((f32[4,32,1024]{2,1,0:T(8,128)}), f32[4,32,1024]{2,1,0:T(8,128)S(1)}, u32[]{:S(2)}, u32[]{:S(2)}) %all-to-all-start) | async-done | bytes 524320 | tf_op jit(solution)/shard_map/all_to_all | solution.py:503
  14.9 0.0 copy-done
  14.9 0.0 copy-done.1
  14.9 0.0 copy-done.2
  14.9 1.9 %shard_map.83 = (f32[32,80,128]{2,1,0:T(8,128)S(1)}, f32[32,1024]{1,0:T(8,128)S(1)}, f32[2,8,2,32,128]{4,3,2,1,0:T(8,128)S(1)}) custom-call(s32[18]{0:T(128)S(1)} %pad_add_fusion.place_ref, f32[32,32,128]{2,1,0:T(8,128)S(1)} %get-tuple-element.16.launched_ref, f32[4,32,1024]{2,1,0:T(8,128)S(1)} %all-to-all-done.slices_ref, s32[32,1024]{1,0:T(8,128)S(1)} %copy-done.2, ...), custom_call_target="tpu_custom_call" | custom-call | tf_op jit(solution)/shard_map/pallas_call | solution.py:469
  16.8 30.3 %all_to_all.30.in_ref = f32[32,80,128]{2,1,0:T(8,128)S(1)} all-to-all(f32[32,80,128]{2,1,0:T(8,128)S(1)} %get-tuple-element.18), channel_id=1, replica_groups=mesh['sec'=4,'row'=32] {'row'}, dimensions={0} | all-to-all | bytes 2621440 | tf_op jit(solution)/shard_map/all_to_all | solution.py:521
  47.1 4.2 %shard_map.84 = (f32[32,64,128]{2,1,0:T(8,128)S(1)}, f32[2,8,2,32,128]{4,3,2,1,0:T(8,128)S(1)}, f32[2,8,2,32,128]{4,3,2,1,0:T(8,128)S(1)}, f32[2,8,2,32,128]{4,3,2,1,0:T(8,128)S(1)}) custom-call(s32[18]{0:T(128)S(1)} %pad_add_fusion.place_ref, f32[32,80,128]{2,1,0:T(8,128)S(1)} %all_to_all.30.in_ref, bf16[256,256]{1,0:T(8,128)(2,1)S(1)} %copy-done.1, ...), custom_call_target="tpu_custom_call" | custom-call | tf_op jit(solution)/shard_map/pallas_call | solution.py:469
  51.3 20.4 %all_to_all.31.in_ref = f32[32,64,128]{2,1,0:T(8,128)S(1)} all-to-all(f32[32,64,128]{2,1,0:T(8,128)S(1)} %get-tuple-element.19), channel_id=1, replica_groups=mesh['sec'=4,'row'=32] {'row'}, dimensions={0} | all-to-all | bytes 2097152 | tf_op jit(solution)/shard_map/all_to_all | solution.py:524
  71.7 3.8 %shard_map.85 = (f32[32,64,128]{2,1,0:T(8,128)S(1)}, f32[32,1024]{1,0:T(8,128)S(1)}) custom-call(s32[18]{0:T(128)S(1)} %pad_add_fusion.place_ref, f32[32,64,128]{2,1,0:T(8,128)S(1)} %all_to_all.31.in_ref, bf16[256,256]{1,0:T(8,128)(2,1)S(1)} %copy-done.1, bf16[256,256]{1,0:T(8,128)(2,1)S(1)} %copy-done, f32[32,1024]{1,0:T(8,128)S(1)} %get-tuple-element.20.base_ref), custom_call_target="tpu_custom_call" | custom-call | tf_op jit(solution)/shard_map/pallas_call | solution.py:469
  75.5 20.7 %all_to_all.32.in_ref = f32[32,64,128]{2,1,0:T(8,128)S(1)} all-to-all(f32[32,64,128]{2,1,0:T(8,128)S(1)} %get-tuple-element.21), channel_id=1, replica_groups=mesh['sec'=4,'row'=32] {'row'}, dimensions={0} | all-to-all | bytes 2097152 | tf_op jit(solution)/shard_map/all_to_all | solution.py:529
  96.1 3.1 %shard_map.86 = f32[32,48,128]{2,1,0:T(8,128)S(1)} custom-call(s32[18]{0:T(128)S(1)} %pad_add_fusion.place_ref, f32[32,64,128]{2,1,0:T(8,128)S(1)} %all_to_all.32.in_ref, bf16[256,256]{1,0:T(8,128)(2,1)S(1)} %copy-done.1, bf16[256,256]{1,0:T(8,128)(2,1)S(1)} %copy-done, f32[2,8,2,32,128]{4,3,2,1,0:T(8,128)S(1)} %get-tuple-element.22.field_ref, ...), custom_call_target="tpu_custom_call" | custom-call | tf_op jit(solution)/shard_map/pallas_call | solution.py:469
  99.3 18.0 %all_to_all.33.in_ref = f32[32,48,128]{2,1,0:T(8,128)S(1)} all-to-all(f32[32,48,128]{2,1,0:T(8,128)S(1)} %shard_map.86), channel_id=1, replica_groups=mesh['sec'=4,'row'=32] {'row'}, dimensions={0} | all-to-all | bytes 1572864 | tf_op jit(solution)/shard_map/all_to_all | solution.py:536
  117.3 1.7 %shard_map.87 = f32[4,32,1024]{2,1,0:T(8,128)S(1)} custom-call(s32[18]{0:T(128)S(1)} %pad_add_fusion.place_ref, f32[32,48,128]{2,1,0:T(8,128)S(1)} %all_to_all.33.in_ref, bf16[256,256]{1,0:T(8,128)(2,1)S(1)} %copy-done.1, bf16[256,256]{1,0:T(8,128)(2,1)S(1)} %copy-done, f32[2,8,2,32,128]{4,3,2,1,0:T(8,128)S(1)} %get-tuple-element.25.screen_ref, ...), custom_call_target="tpu_custom_call" | custom-call | tf_op jit(solution)/shard_map/pallas_call | solution.py:469
  118.9 12.1 %all_to_all.34.in_ref = f32[4,32,1024]{2,1,0:T(8,128)S(1)} all-to-all(f32[4,32,1024]{2,1,0:T(8,128)S(1)} %shard_map.87), channel_id=1, replica_groups=mesh['sec'=4,'row'=32] {'sec'}, dimensions={0} | all-to-all | bytes 1048576 | tf_op jit(solution)/shard_map/all_to_all | solution.py:540
  131.1 0.7 shard_map.88
Async XLA Ops:
  0.0 6.6 %copy-start.3 = (s32[8]{0:T(128)S(1)}, s32[8]{0:T(128)}, u32[]{:S(2)}) copy-start(s32[8]{0:T(128)} %param.13) | copy-start | bytes 100
  0.0 6.6 %copy-start.4 = (s32[8]{0:T(128)S(1)}, s32[8]{0:T(128)}, u32[]{:S(2)}) copy-start(s32[8]{0:T(128)} %param.12) | copy-start | bytes 100
  1.8 13.1 %all-to-all-start = ((f32[4,32,1024]{2,1,0:T(8,128)}), f32[4,32,1024]{2,1,0:T(8,128)S(1)}, u32[]{:S(2)}, u32[]{:S(2)}) async-start(f32[4,32,1024]{2,1,0:T(8,128)} %broadcast_in_dim.16), calls=%async_computation | async-start | bytes 1048576 | tf_op jit(solution)/shard_map/all_to_all | solution.py:503
  6.6 8.3 %copy-start = (bf16[256,256]{1,0:T(8,128)(2,1)S(1)}, bf16[256,256]{1,0:T(8,128)(2,1)}, u32[]{:S(2)}) copy-start(bf16[256,256]{1,0:T(8,128)(2,1)} %constant.14.clone.low_hbm.low_ref) | copy-start | bytes 393220
  6.6 8.3 %copy-start.1 = (bf16[256,256]{1,0:T(8,128)(2,1)S(1)}, bf16[256,256]{1,0:T(8,128)(2,1)}, u32[]{:S(2)}) copy-start(bf16[256,256]{1,0:T(8,128)(2,1)} %constant.13.clone.high_hbm.high_ref) | copy-start | bytes 393220
  6.6 8.3 %copy-start.2 = (s32[32,1024]{1,0:T(8,128)S(1)}, s32[32,1024]{1,0:T(8,128)}, u32[]{:S(2)}) copy-start(s32[32,1024]{1,0:T(8,128)} %mask_ref.1) | copy-start | bytes 393220

commit v4 on v3

--- a/solution.py
+++ b/solution.py
@@ -42,6 +42,15 @@
     rest = angle - turns * 1.5703125
     rest = rest - turns * 4.837512969970703e-4
     rest = rest - turns * 7.549789948768648e-8
+    return in_quarter(turns, rest)
+
+
+def cos_sin_quarters(quarters):
+    turns = jnp.floor(quarters + 0.5)
+    return in_quarter(turns, (quarters - turns) * (0.5 * math.pi))
+
+
+def in_quarter(turns, rest):
     square = rest * rest
     sine = rest + rest * square * (
         -1.6666654611e-1 + square * (8.3321608736e-3 + square * -1.9515295891e-4)
@@ -116,54 +125,40 @@
     return result[:, :LANES], result[:, LANES:]
 
 
-def filter_lines(wave, picks, twist, high, low, sign):
-    rows = wave[0][0].shape[0]
-
+def line_filter(field, filters, twist, high, low, sign):
     def stack(items, part):
         return jnp.concatenate([item[part] for item in items], axis=0)
 
     def pieces(real, imag):
-        return [(real[k * rows : (k + 1) * rows], imag[k * rows : (k + 1) * rows]) for k in range(GROUPS)]
-
-    parts = dft8(wave, -1)
-    parts = [parts[0]] + [times(parts[k], twist[k]) for k in range(1, GROUPS)]
-    spectrum = pieces(*matmul_pair(stack(parts, 0), stack(parts, 1), high, low))
+        return [(real[k * CHUNK : (k + 1) * CHUNK], imag[k * CHUNK : (k + 1) * CHUNK]) for k in range(GROUPS)]
+
     multiply = times if sign > 0 else times_conj
-    spectrum = [multiply(value, pick) for value, pick in zip(spectrum, picks)]
-    imag, real = matmul_pair(stack(spectrum, 1), stack(spectrum, 0), high, low)
-    parts = pieces(real, imag)
-    parts = [parts[0]] + [times_conj(parts[k], twist[k]) for k in range(1, GROUPS)]
-    return dft8(parts, 1)
-
-
-def line_filter(field, filters, twist, high, low, sign):
+    products = []
+    for wave in field:
+        for first in range(0, WIDE, CHUNK):
+            parts = dft8([(real[first : first + CHUNK], imag[first : first + CHUNK]) for real, imag in wave], -1)
+            parts = [parts[0]] + [times(parts[k], twist[k]) for k in range(1, GROUPS)]
+            products.append(matmul_pair(stack(parts, 0), stack(parts, 1), high, low))
+    returned = []
+    for index, product in enumerate(products):
+        picks = filters[index // (WIDE // CHUNK)]
+        spectrum = [multiply(value, pick) for value, pick in zip(pieces(*product), picks)]
+        imag, real = matmul_pair(stack(spectrum, 1), stack(spectrum, 0), high, low)
+        returned.append((real, imag))
+    chunks = []
+    for product in returned:
+        parts = pieces(*product)
+        parts = [parts[0]] + [times_conj(parts[k], twist[k]) for k in range(1, GROUPS)]
+        chunks.append(dft8(parts, 1))
     result = []
-    for wave, picks in zip(field, filters):
-        chunks = []
-        for first in range(0, WIDE, CHUNK):
-            part = [(real[first : first + CHUNK], imag[first : first + CHUNK]) for real, imag in wave]
-            chunks.append(filter_lines(part, picks, twist, high, low, sign))
+    for wave in range(len(field)):
+        mine = chunks[wave * (WIDE // CHUNK) : (wave + 1) * (WIDE // CHUNK)]
         result.append(
             [
-                tuple(jnp.concatenate([chunk[group][part] for chunk in chunks], axis=0) for part in range(2))
+                tuple(jnp.concatenate([chunk[group][part] for chunk in mine], axis=0) for part in range(2))
                 for group in range(GROUPS)
             ]
         )
-    return result
-
-
-def exchange_blocks(items):
-    lane = lax.broadcasted_iota(jnp.int32, items[0].shape, items[0].ndim - 1)
-    axis = items[0].ndim - 1
-    low_half, even = (lane & 64) == 0, (lane & 32) == 0
-    halves = [None] * 4
-    for i in range(2):
-        halves[i] = jnp.where(low_half, items[i], pltpu.roll(items[i + 2], 64, axis))
-        halves[i + 2] = jnp.where(low_half, pltpu.roll(items[i], 64, axis), items[i + 2])
-    result = [None] * 4
-    for i in (0, 2):
-        result[i] = jnp.where(even, halves[i], pltpu.roll(halves[i + 1], 32, axis))
-        result[i + 1] = jnp.where(even, pltpu.roll(halves[i], LANES - 32, axis), halves[i + 1])
     return result
 
 
@@ -193,31 +188,34 @@
             blocks_ref[FOLD * group + i, start : start + WIDE] = turned[i * WIDE : (i + 1) * WIDE]
 
 
-def pack_plane(plane):
-    blocks = []
+def store_planes(blocks_ref, start, planes):
+    lane = lax.broadcasted_iota(jnp.int32, (16, LANES), 1)
     for group in range(GROUPS):
-        rows = [plane[group]] + [pltpu.roll(plane[group], LANES - 8 * q, 1) for q in range(1, FOLD)]
-        turned = jnp.concatenate(rows, axis=0).T
-        blocks += [turned[i * WIDE : i * WIDE + 8] for i in range(FOLD)]
-    return blocks
-
-
-def store_plane(blocks_ref, start, plane):
-    blocks = pack_plane(plane)
-    for peer in range(PEERS):
-        blocks_ref[peer, start : start + 8] = blocks[peer]
-
-
-def load_plane(blocks_ref, start):
-    return unpack_plane([blocks_ref[peer, start : start + 8] for peer in range(PEERS)])
-
-
-def unpack_plane(blocks):
-    plane = []
-    for group in range(GROUPS):
-        items = exchange_blocks(blocks[FOLD * group : FOLD * (group + 1)])
-        plane.append(jnp.concatenate(items, axis=0))
-    return plane
+        rows = [planes[0][group], planes[1][group]]
+        turned = jnp.concatenate(rows + rows, axis=0).T
+        for i in range(FOLD):
+            upper, lower = turned[i * WIDE : i * WIDE + 16], turned[i * WIDE + 16 : (i + 1) * WIDE]
+            blocks_ref[FOLD * group + i, start : start + 16] = jnp.where(lane < 64, upper, lower)
+
+
+def load_planes(blocks_ref, start):
+    turned = [
+        jnp.concatenate([blocks_ref[FOLD * i + j, start : start + 16] for i in range(GROUPS)], axis=0).T
+        for j in range(FOLD)
+    ]
+    planes = []
+    for plane in range(2):
+        halves = []
+        for half in range(2):
+            first = (half * 2 + plane) * WIDE
+            halves.append(jnp.concatenate([t[first : first + WIDE] for t in turned], axis=0).T)
+        planes.append(
+            [
+                jnp.concatenate([half[16 * group : 16 * (group + 1)] for half in halves], axis=0)
+                for group in range(GROUPS)
+            ]
+        )
+    return planes
 
 
 def ratio_of(place_ref, wave):
@@ -225,31 +223,35 @@
     return ratio_base + ratio_step * number.astype(jnp.float32)
 
 
-def filters_of(place_ref):
+def write_constants(constants_ref, place_ref):
     row = lax.broadcasted_iota(jnp.int32, (GROUPS, LANES), 0)
     lane = lax.broadcasted_iota(jnp.int32, (GROUPS, LANES), 1)
     natural = row + GROUPS * lane
     signed = jnp.where(natural < GRID // 2, natural, natural - GRID)
     scaled = signed.astype(jnp.float32) * (2.0 / GRID)
     squares = scaled * scaled
-    filters = []
-    for wave in range(SHARE):
-        real, imag = cos_sin((-prop_scale * ratio_of(place_ref, wave)) * squares)
-        real, imag = real * (1.0 / GRID), imag * (1.0 / GRID)
-        filters.append([(real[k : k + 1], imag[k : k + 1]) for k in range(GROUPS)])
-    return filters
-
-
-def twists():
-    row = lax.broadcasted_iota(jnp.int32, (GROUPS, LANES), 0)
-    lane = lax.broadcasted_iota(jnp.int32, (GROUPS, LANES), 1)
+    for wave in range(SHARE):
+        ratio = ratio_of(place_ref, wave)
+        real, imag = cos_sin((-prop_scale * ratio) * squares)
+        constants_ref[2 * wave], constants_ref[2 * wave + 1] = real * (1.0 / GRID), imag * (1.0 / GRID)
+        constants_ref[2 * SHARE + 2 + wave] = 1.0 / jnp.full((GROUPS, LANES), ratio, jnp.float32)
     real, imag = cos_sin((-2.0 * math.pi / GRID) * (row * lane).astype(jnp.float32))
-    return [(real[k : k + 1], imag[k : k + 1]) for k in range(GROUPS)]
-
-
-def inverse_ratio(place_ref, wave):
-    ratio = ratio_of(place_ref, wave)
-    return 1.0 / jnp.full((8, LANES), ratio, jnp.float32)[:1]
+    constants_ref[2 * SHARE], constants_ref[2 * SHARE + 1] = real, imag
+
+
+class Constants:
+    def __init__(self, constants_ref, high_ref, low_ref):
+        def rows(real, imag):
+            real, imag = constants_ref[real], constants_ref[imag]
+            return [(real[k : k + 1], imag[k : k + 1]) for k in range(GROUPS)]
+
+        self.filters = [rows(2 * wave, 2 * wave + 1) for wave in range(SHARE)]
+        self.twist = rows(2 * SHARE, 2 * SHARE + 1)
+        self.inverse = [constants_ref[2 * SHARE + 2 + wave][:1] for wave in range(SHARE)]
+        self.high, self.low = high_ref[...], low_ref[...]
+
+    def along(self, field, sign):
+        return line_filter(field, self.filters, self.twist, self.high, self.low, sign)
 
 
 def copies(pairs, sems):
@@ -275,6 +277,7 @@
     measured_hbm,
     out_ref,
     target_ref,
+    constants_ref,
     illum_ref,
     high_ref,
     low_ref,
@@ -286,8 +289,7 @@
         [(illum_hbm, illum_ref), (high_hbm, high_ref), (low_hbm, low_ref), (own, measured_ref)], sems
     )
     start(moves)
-    twist = twists()
-    filters = filters_of(place_ref)
+    write_constants(constants_ref, place_ref)
     tilted = []
     for wave in range(SHARE):
         pick = place_ref[2 + waves + place_ref[0] * SHARE + wave]
@@ -314,8 +316,7 @@
             bright = illum_ref[:, group * LANES : (group + 1) * LANES]
             groups.append((bright * tilted[wave][group][0], bright * tilted[wave][group][1]))
         field.append(groups)
-    field = line_filter(field, filters, twist, high_ref[...], low_ref[...], 1)
-    store_field(out_ref, 0, field)
+    store_field(out_ref, 0, Constants(constants_ref, high_ref, low_ref).along(field, 1))
     wait(moves[3:])
     for wave in range(SHARE):
         for part in range(2):
@@ -336,18 +337,18 @@
     ]
 
 
-def screens(base, place_ref):
+def screens(base, constants):
     result = []
     for wave in range(SHARE):
-        scale = inverse_ratio(place_ref, wave)
-        result.append([cos_sin(plane * scale) for plane in base])
+        scale = constants.inverse[wave] * (2.0 / math.pi)
+        result.append([cos_sin_quarters(plane * scale) for plane in base])
     return result
 
 
-def gradient(target, field, place_ref):
+def gradient(target, field, constants):
     total = [None] * GROUPS
     for wave in range(SHARE):
-        scale = inverse_ratio(place_ref, wave)
+        scale = constants.inverse[wave]
         for group in range(GROUPS):
             left, right = target[wave][group], field[wave][group]
             term = (left[0] * right[1] - left[1] * right[0]) * scale
@@ -375,10 +376,9 @@
 
 
 def begin_kernel(
-    place_ref, launched_ref, slices_ref, mask_ref, target_ref, high_ref, low_ref, out_ref, base_ref, screen_ref
+    constants_ref, launched_ref, slices_ref, mask_ref, target_ref, high_ref, low_ref, out_ref, base_ref, screen_ref
 ):
-    high, low, twist = high_ref[...], low_ref[...], twists()
-    filters = filters_of(place_ref)
+    constants = Constants(constants_ref, high_ref, low_ref)
     mask = [core_step * mask_ref[:, lanes_of(group)].astype(jnp.float32) for group in range(GROUPS)]
 
     def base_of(layer):
@@ -386,67 +386,59 @@
 
     for peer in range(PEERS):
         out_ref[peer, :WIDE] = launched_ref[peer]
-    store_plane(out_ref, 2 * WIDE, base_of(0))
-    store_plane(out_ref, 2 * WIDE + 8, base_of(2))
+    store_planes(out_ref, 2 * WIDE, (base_of(0), base_of(2)))
     for group, plane in enumerate(base_of(1)):
         base_ref[:, lanes_of(group)] = plane
-    screen = screens(base_of(3), place_ref)
+    screen = screens(base_of(3), constants)
     save(screen_ref, screen)
     target = each(times_conj, target_of(target_ref), screen)
-    store_field(out_ref, WIDE, line_filter(target, filters, twist, high, low, -1))
-
-
-def first_kernel(place_ref, in_ref, high_ref, low_ref, out_ref, field_ref, target_ref, screen_ref):
-    high, low, twist = high_ref[...], low_ref[...], twists()
-    filters = filters_of(place_ref)
-    field = line_filter(load_field(in_ref, 0), filters, twist, high, low, 1)
-    field = each(times, field, screens(load_plane(in_ref, 2 * WIDE), place_ref))
+    store_field(out_ref, WIDE, constants.along(target, -1))
+
+
+def first_kernel(constants_ref, in_ref, high_ref, low_ref, out_ref, field_ref, target_ref, screen_ref):
+    constants = Constants(constants_ref, high_ref, low_ref)
+    base_0, base_2 = load_planes(in_ref, 2 * WIDE)
+    field = constants.along(load_field(in_ref, 0), 1)
+    field = each(times, field, screens(base_0, constants))
     save(field_ref, field)
-    store_field(out_ref, 0, line_filter(field, filters, twist, high, low, 1))
-    target = line_filter(load_field(in_ref, WIDE), filters, twist, high, low, -1)
+    store_field(out_ref, 0, constants.along(field, 1))
+    target = constants.along(load_field(in_ref, WIDE), -1)
     save(target_ref, target)
-    screen = screens(load_plane(in_ref, 2 * WIDE + 8), place_ref)
+    screen = screens(base_2, constants)
     save(screen_ref, screen)
     target = each(times_conj, target, screen)
-    store_field(out_ref, WIDE, line_filter(target, filters, twist, high, low, -1))
-
-
-def second_kernel(place_ref, in_ref, high_ref, low_ref, base_ref, out_ref, grad_ref):
-    high, low, twist = high_ref[...], low_ref[...], twists()
-    filters = filters_of(place_ref)
-    screen = screens(planes_of(base_ref), place_ref)
-    field = line_filter(load_field(in_ref, 0), filters, twist, high, low, 1)
+    store_field(out_ref, WIDE, constants.along(target, -1))
+
+
+def second_kernel(constants_ref, in_ref, high_ref, low_ref, base_ref, out_ref, grad_ref):
+    constants = Constants(constants_ref, high_ref, low_ref)
+    screen = screens(planes_of(base_ref), constants)
+    field = constants.along(load_field(in_ref, 0), 1)
     field = each(times, field, screen)
-    target = line_filter(load_field(in_ref, WIDE), filters, twist, high, low, -1)
-    for group, plane in enumerate(gradient(target, field, place_ref)):
+    target = constants.along(load_field(in_ref, WIDE), -1)
+    for group, plane in enumerate(gradient(target, field, constants)):
         grad_ref[:, lanes_of(group)] = plane
-    store_field(out_ref, 0, line_filter(field, filters, twist, high, low, 1))
+    store_field(out_ref, 0, constants.along(field, 1))
     target = each(times_conj, target, screen)
-    store_field(out_ref, WIDE, line_filter(target, filters, twist, high, low, -1))
-
-
-def third_kernel(place_ref, in_ref, high_ref, low_ref, field_ref, target_ref, screen_ref, out_ref):
-    high, low, twist = high_ref[...], low_ref[...], twists()
-    filters = filters_of(place_ref)
-    field = line_filter(load_field(in_ref, 0), filters, twist, high, low, 1)
+    store_field(out_ref, WIDE, constants.along(target, -1))
+
+
+def third_kernel(constants_ref, in_ref, high_ref, low_ref, field_ref, target_ref, screen_ref, out_ref):
+    constants = Constants(constants_ref, high_ref, low_ref)
+    field = constants.along(load_field(in_ref, 0), 1)
     field = each(times, field, kept(screen_ref))
-    store_plane(out_ref, WIDE + 8, gradient(kept(target_ref), field, place_ref))
-    store_field(out_ref, 0, line_filter(field, filters, twist, high, low, 1))
-    target = line_filter(load_field(in_ref, WIDE), filters, twist, high, low, -1)
-    store_plane(out_ref, WIDE, gradient(target, kept(field_ref), place_ref))
-
-
-def last_kernel(place_ref, in_ref, high_ref, low_ref, screen_ref, target_ref, first_ref, out_ref):
-    high, low, twist = high_ref[...], low_ref[...], twists()
-    filters = filters_of(place_ref)
-    field = line_filter(load_field(in_ref, 0), filters, twist, high, low, 1)
+    grad_2 = gradient(kept(target_ref), field, constants)
+    store_field(out_ref, 0, constants.along(field, 1))
+    target = constants.along(load_field(in_ref, WIDE), -1)
+    store_planes(out_ref, WIDE, (gradient(target, kept(field_ref), constants), grad_2))
+
+
+def last_kernel(constants_ref, in_ref, high_ref, low_ref, screen_ref, target_ref, first_ref, out_ref):
+    constants = Constants(constants_ref, high_ref, low_ref)
+    field = constants.along(load_field(in_ref, 0), 1)
     field = each(times, field, kept(screen_ref))
-    planes = [
-        load_plane(in_ref, WIDE),
-        planes_of(first_ref),
-        load_plane(in_ref, WIDE + 8),
-        gradient(target_of(target_ref), field, place_ref),
-    ]
+    grad_0, grad_2 = load_planes(in_ref, WIDE)
+    planes = [grad_0, planes_of(first_ref), grad_2, gradient(target_of(target_ref), field, constants)]
     for layer, plane in enumerate(planes):
         for group in range(GROUPS):
             out_ref[layer, :, lanes_of(group)] = plane[group]
@@ -501,39 +493,39 @@
         return free((PEERS, rows, LANES))
 
     slices = swap(jnp.broadcast_to(index_slices, (sec_count, *plane)), "sec")
-    launched, target = call(
+    launched, target, constants = call(
         functools.partial(launch_kernel, waves),
         (place,),
         (),
         in_hbm(illum_amp, *tables, measured),
-        (near((PEERS, WIDE, LANES)), near((SHARE, 2, *plane))),
+        (near((PEERS, WIDE, LANES)), near((SHARE, 2, *plane)), near((3 * SHARE + 2, GROUPS, LANES))),
         scratch=((plane, jnp.float32), table, table, ((SHARE, *measured.shape[1:]), jnp.float32)),
         moves=4,
     )
     sent, base, screen_3 = call(
         begin_kernel,
-        (place,),
-        (launched, slices, core_mask, target, *tables),
+        (),
+        (constants, launched, slices, core_mask, target, *tables),
         (),
         (blocks(2 * WIDE + 16), near(plane), near(saved)),
     )
     sent, field_0, target_2, screen_2 = call(
-        first_kernel, (place,), (swap(sent, "row"), *tables), (), (blocks(2 * WIDE),) + (near(saved),) * 3
+        first_kernel, (), (constants, swap(sent, "row"), *tables), (), (blocks(2 * WIDE),) + (near(saved),) * 3
     )
     sent, grad_1 = call(
-        second_kernel, (place,), (swap(sent, "row"), *tables, base), (), (blocks(2 * WIDE), near(plane))
+        second_kernel, (), (constants, swap(sent, "row"), *tables, base), (), (blocks(2 * WIDE), near(plane))
     )
     (sent,) = call(
         third_kernel,
-        (place,),
-        (swap(sent, "row"), *tables, field_0, target_2, screen_2),
+        (),
+        (constants, swap(sent, "row"), *tables, field_0, target_2, screen_2),
         (),
         (blocks(WIDE + 16),),
     )
     (grads,) = call(
         last_kernel,
-        (place,),
-        (swap(sent, "row"), *tables, screen_3, target, grad_1),
+        (),
+        (constants, swap(sent, "row"), *tables, screen_3, target, grad_1),
         (),
         (free((sec_count, *plane)),),
     )

time: 132 us -> 129 us (0.977)
  Pallas kernels: 18 us -> 14.5 us
    pallas_call x7, Pallas kernels: 18 us -> 14.5 us  [call(): pl.pallas_call(kernel, out_shape=[place(shape, jnp.float32) for shape, pl...]
where the time goes in v4:
time: 129 us; the launch traced here: 128 us
  blocking collectives  101 us (78%)
  Pallas kernels  14.5 us (11%)
  waiting for transfers between devices  5.61 us (4%)
  starting transfers between devices  4.84 us (4%)
  local copies, waits for them, and re-layouts  1.79 us (1%)
    all_to_all x4, blocking collectives, body(): swap(sent, 'row')  89.3 us
    pallas_call x7, Pallas kernels, call(): pl.pallas_call(kernel, out_shape=[place(shape, jnp.float32) for shape, pl...  14.5 us
    all_to_all x1, blocking collectives, body(): swap(grads, 'sec')  12.1 us
    all_to_all x1, waiting for transfers between devices, body(): slices = swap(jnp.broadcast_to(index_slices, (sec_count, *plane)), 'sec')  5.61 us
    all_to_all x1, starting transfers between devices, body(): slices = swap(jnp.broadcast_to(index_slices, (sec_count, *plane)), 'sec')  4.84 us
  transfers between devices with their start and end apart: 1, of which 1 were waited for; matrix products, arithmetic and copies ran while one was open for 0% of the time, Pallas kernels for 2%

profile of v4, /device:TPU:1, one launch (start us, length us, event | category | flops | bytes accessed | tf_op | source)
XLA Modules:
  0.0 128.4 jit_solution(10189932390624344087)
XLA Ops:
  0.0 0.0 copy-start.3
  0.0 0.0 copy-start.4
  0.0 1.8 %broadcast_in_dim.16 = f32[4,32,1024]{2,1,0:T(8,128)} broadcast(f32[32,1024]{1,0:T(8,128)} %bitcast.3), dimensions={1,2} | broadcast | bytes 655360 | tf_op jit(solution)/shard_map/broadcast_in_dim | solution.py:495
  1.8 4.8 %all-to-all-start = ((f32[4,32,1024]{2,1,0:T(8,128)}), f32[4,32,1024]{2,1,0:T(8,128)S(1)}, u32[]{:S(2)}, u32[]{:S(2)}) async-start(f32[4,32,1024]{2,1,0:T(8,128)} %broadcast_in_dim.16), calls=%async_computation | async-start | bytes 1048576 | tf_op jit(solution)/shard_map/all_to_all | solution.py:495
  6.6 0.0 copy-start
  6.6 0.0 copy-start.1
  6.6 0.0 copy-start.2
  6.6 0.0 copy-done.3
  6.6 0.0 copy-done.4
  6.7 0.1 pad_add_fusion.place_ref
  6.7 2.5 %shard_map.82 = (f32[32,32,128]{2,1,0:T(8,128)S(1)}, f32[2,2,32,1024]{3,2,1,0:T(8,128)S(1)}, f32[8,8,128]{2,1,0:T(8,128)S(1)}) custom-call(s32[18]{0:T(128)S(1)} %pad_add_fusion.place_ref, f32[32,1024]{1,0:T(8,128)} %illum_hbm.1, bf16[256,256]{1,0:T(8,128)(2,1)} %constant.13.clone.high_hbm.high_ref, bf16[256,256]{1,0:T(8,128)(2,1)} %constant.14.clone.low_hbm.low_ref, ...), custom_call_target="tpu_custom_call" | custom-call | tf_op jit(solution)/shard_map/pallas_call | solution.py:461
  9.3 5.6 %all-to-all-done.slices_ref = f32[4,32,1024]{2,1,0:T(8,128)S(1)} async-done(((f32[4,32,1024]{2,1,0:T(8,128)}), f32[4,32,1024]{2,1,0:T(8,128)S(1)}, u32[]{:S(2)}, u32[]{:S(2)}) %all-to-all-start) | async-done | bytes 524320 | tf_op jit(solution)/shard_map/all_to_all | solution.py:495
  14.9 0.0 copy-done
  14.9 0.0 copy-done.1
  14.9 0.0 copy-done.2
  14.9 1.3 shard_map.83
  16.2 30.3 %all_to_all.30.in_ref = f32[32,80,128]{2,1,0:T(8,128)S(1)} all-to-all(f32[32,80,128]{2,1,0:T(8,128)S(1)} %get-tuple-element.20), channel_id=1, replica_groups=mesh['sec'=4,'row'=32] {'row'}, dimensions={0} | all-to-all | bytes 2621440 | tf_op jit(solution)/shard_map/all_to_all | solution.py:513
  46.5 3.5 %shard_map.84 = (f32[32,64,128]{2,1,0:T(8,128)S(1)}, f32[2,8,2,32,128]{4,3,2,1,0:T(8,128)S(1)}, f32[2,8,2,32,128]{4,3,2,1,0:T(8,128)S(1)}, f32[2,8,2,32,128]{4,3,2,1,0:T(8,128)S(1)}) custom-call(f32[8,8,128]{2,1,0:T(8,128)S(1)} %get-tuple-element.17.constants_ref, f32[32,80,128]{2,1,0:T(8,128)S(1)} %all_to_all.30.in_ref, bf16[256,256]{1,0:T(8,128)(2,1)S(1)} %copy-done.1, ...), custom_call_target="tpu_custom_call" | custom-call | tf_op jit(solution)/shard_map/pallas_call | solution.py:461
  50.0 20.4 %all_to_all.31.in_ref = f32[32,64,128]{2,1,0:T(8,128)S(1)} all-to-all(f32[32,64,128]{2,1,0:T(8,128)S(1)} %get-tuple-element.21), channel_id=1, replica_groups=mesh['sec'=4,'row'=32] {'row'}, dimensions={0} | all-to-all | bytes 2097152 | tf_op jit(solution)/shard_map/all_to_all | solution.py:516
  70.4 3.2 %shard_map.85 = (f32[32,64,128]{2,1,0:T(8,128)S(1)}, f32[32,1024]{1,0:T(8,128)S(1)}) custom-call(f32[8,8,128]{2,1,0:T(8,128)S(1)} %get-tuple-element.17.constants_ref, f32[32,64,128]{2,1,0:T(8,128)S(1)} %all_to_all.31.in_ref, bf16[256,256]{1,0:T(8,128)(2,1)S(1)} %copy-done.1, bf16[256,256]{1,0:T(8,128)(2,1)S(1)} %copy-done, ...), custom_call_target="tpu_custom_call" | custom-call | tf_op jit(solution)/shard_map/pallas_call | solution.py:461
  73.5 20.7 %all_to_all.32.in_ref = f32[32,64,128]{2,1,0:T(8,128)S(1)} all-to-all(f32[32,64,128]{2,1,0:T(8,128)S(1)} %get-tuple-element.23), channel_id=1, replica_groups=mesh['sec'=4,'row'=32] {'row'}, dimensions={0} | all-to-all | bytes 2097152 | tf_op jit(solution)/shard_map/all_to_all | solution.py:521
  94.2 2.4 %shard_map.86 = f32[32,48,128]{2,1,0:T(8,128)S(1)} custom-call(f32[8,8,128]{2,1,0:T(8,128)S(1)} %get-tuple-element.17.constants_ref, f32[32,64,128]{2,1,0:T(8,128)S(1)} %all_to_all.32.in_ref, bf16[256,256]{1,0:T(8,128)(2,1)S(1)} %copy-done.1, bf16[256,256]{1,0:T(8,128)(2,1)S(1)} %copy-done, f32[2,8,2,32,128]{4,3,2,1,0:T(8,128)S(1)} %get-tuple-element.24.field_ref, ...), custom_call_target="tpu_custom_call" | custom-call | tf_op jit(solution)/shard_map/pallas_call | solution.py:461
  96.6 18.0 %all_to_all.33.in_ref = f32[32,48,128]{2,1,0:T(8,128)S(1)} all-to-all(f32[32,48,128]{2,1,0:T(8,128)S(1)} %shard_map.86), channel_id=1, replica_groups=mesh['sec'=4,'row'=32] {'row'}, dimensions={0} | all-to-all | bytes 1572864 | tf_op jit(solution)/shard_map/all_to_all | solution.py:528
  114.5 1.0 shard_map.87
  115.6 12.1 %all_to_all.34.in_ref = f32[4,32,1024]{2,1,0:T(8,128)S(1)} all-to-all(f32[4,32,1024]{2,1,0:T(8,128)S(1)} %shard_map.87), channel_id=1, replica_groups=mesh['sec'=4,'row'=32] {'sec'}, dimensions={0} | all-to-all | bytes 1048576 | tf_op jit(solution)/shard_map/all_to_all | solution.py:532
  127.7 0.7 shard_map.88
Async XLA Ops:
  0.0 6.6 %copy-start.3 = (s32[8]{0:T(128)S(1)}, s32[8]{0:T(128)}, u32[]{:S(2)}) copy-start(s32[8]{0:T(128)} %param.13) | copy-start | bytes 100
  0.0 6.6 %copy-start.4 = (s32[8]{0:T(128)S(1)}, s32[8]{0:T(128)}, u32[]{:S(2)}) copy-start(s32[8]{0:T(128)} %param.12) | copy-start | bytes 100
  1.8 13.1 %all-to-all-start = ((f32[4,32,1024]{2,1,0:T(8,128)}), f32[4,32,1024]{2,1,0:T(8,128)S(1)}, u32[]{:S(2)}, u32[]{:S(2)}) async-start(f32[4,32,1024]{2,1,0:T(8,128)} %broadcast_in_dim.16), calls=%async_computation | async-start | bytes 1048576 | tf_op jit(solution)/shard_map/all_to_all | solution.py:495
  6.6 8.3 %copy-start = (bf16[256,256]{1,0:T(8,128)(2,1)S(1)}, bf16[256,256]{1,0:T(8,128)(2,1)}, u32[]{:S(2)}) copy-start(bf16[256,256]{1,0:T(8,128)(2,1)} %constant.14.clone.low_hbm.low_ref) | copy-start | bytes 393220
  6.6 8.3 %copy-start.1 = (bf16[256,256]{1,0:T(8,128)(2,1)S(1)}, bf16[256,256]{1,0:T(8,128)(2,1)}, u32[]{:S(2)}) copy-start(bf16[256,256]{1,0:T(8,128)(2,1)} %constant.13.clone.high_hbm.high_ref) | copy-start | bytes 393220
  6.6 8.3 %copy-start.2 = (s32[32,1024]{1,0:T(8,128)S(1)}, s32[32,1024]{1,0:T(8,128)}, u32[]{:S(2)}) copy-start(s32[32,1024]{1,0:T(8,128)} %mask_ref.1) | copy-start | bytes 393220

commit v5 on v4

--- a/solution.py
+++ b/solution.py
@@ -235,6 +235,7 @@
         real, imag = cos_sin((-prop_scale * ratio) * squares)
         constants_ref[2 * wave], constants_ref[2 * wave + 1] = real * (1.0 / GRID), imag * (1.0 / GRID)
         constants_ref[2 * SHARE + 2 + wave] = 1.0 / jnp.full((GROUPS, LANES), ratio, jnp.float32)
+    constants_ref[3 * SHARE + 2] = jnp.full((GROUPS, LANES), place_ref[0].astype(jnp.float32), jnp.float32)
     real, imag = cos_sin((-2.0 * math.pi / GRID) * (row * lane).astype(jnp.float32))
     constants_ref[2 * SHARE], constants_ref[2 * SHARE + 1] = real, imag
 
@@ -376,13 +377,33 @@
 
 
 def begin_kernel(
-    constants_ref, launched_ref, slices_ref, mask_ref, target_ref, high_ref, low_ref, out_ref, base_ref, screen_ref
+    constants_ref,
+    launched_ref,
+    slice_0,
+    slice_1,
+    slice_2,
+    slice_3,
+    mask_ref,
+    target_ref,
+    high_ref,
+    low_ref,
+    out_ref,
+    base_ref,
+    screen_ref,
 ):
     constants = Constants(constants_ref, high_ref, low_ref)
     mask = [core_step * mask_ref[:, lanes_of(group)].astype(jnp.float32) for group in range(GROUPS)]
 
     def base_of(layer):
-        return [mask[group] + slices_ref[layer, :, lanes_of(group)] for group in range(GROUPS)]
+        back = constants_ref[3 * SHARE + 2][:1] - float(layer)
+        back = jnp.where(back < 0.0, back + 4.0, back)
+        result = []
+        for group in range(GROUPS):
+            value = slice_0[0, :, lanes_of(group)]
+            for place, ref in enumerate((slice_1, slice_2, slice_3)):
+                value = jnp.where(back == place + 1.0, ref[0, :, lanes_of(group)], value)
+            result.append(mask[group] + value)
+        return result
 
     for peer in range(PEERS):
         out_ref[peer, :WIDE] = launched_ref[peer]
@@ -492,20 +513,23 @@
     def blocks(rows):
         return free((PEERS, rows, LANES))
 
-    slices = swap(jnp.broadcast_to(index_slices, (sec_count, *plane)), "sec")
+    slices = [index_slices]
+    for back in range(1, sec_count):
+        pairs = [(i, (i + back) % sec_count) for i in range(sec_count)]
+        slices.append(lax.ppermute(index_slices, "sec", pairs))
     launched, target, constants = call(
         functools.partial(launch_kernel, waves),
         (place,),
         (),
         in_hbm(illum_amp, *tables, measured),
-        (near((PEERS, WIDE, LANES)), near((SHARE, 2, *plane)), near((3 * SHARE + 2, GROUPS, LANES))),
+        (near((PEERS, WIDE, LANES)), near((SHARE, 2, *plane)), near((3 * SHARE + 3, GROUPS, LANES))),
         scratch=((plane, jnp.float32), table, table, ((SHARE, *measured.shape[1:]), jnp.float32)),
         moves=4,
     )
     sent, base, screen_3 = call(
         begin_kernel,
         (),
-        (constants, launched, slices, core_mask, target, *tables),
+        (constants, launched, *slices, core_mask, target, *tables),
         (),
         (blocks(2 * WIDE + 16), near(plane), near(saved)),
     )

time: 129 us -> 124 us (0.961)
  waiting for transfers between devices: 5.61 us -> 0.42 us
  local copies, waits for them, and re-layouts: 1.79 us -> 0.02 us
  starting transfers between devices: 4.84 us -> 6.33 us
    ppermute x0 -> x3, starting transfers between devices: none -> 6.33 us  [body(): slices.append(lax.ppermute(index_slices, 'sec', pairs))]
    all_to_all x1 -> x0, waiting for transfers between devices: 5.61 us -> none  [body(): slices = swap(jnp.broadcast_to(index_slices, (sec_count, *plane)), 'sec')]
    all_to_all x1 -> x0, starting transfers between devices: 4.84 us -> none  [body(): slices = swap(jnp.broadcast_to(index_slices, (sec_count, *plane)), 'sec')]
    broadcast_in_dim x1 -> x0, local copies, waits for them, and re-layouts: 1.77 us -> none  [body(): slices = swap(jnp.broadcast_to(index_slices, (sec_count, *plane)), 'sec')]
  transfers between devices with their start and end apart: 1 -> 3, of which waited for: 1 -> 1; matrix products, arithmetic and copies ran while one was open for 0% -> 1% of each run, Pallas kernels for 2% -> 2%
where the time goes in v5:
time: 124 us
  blocking collectives  102 us (82%)
  Pallas kernels  14.8 us (12%)
  starting transfers between devices  6.33 us (5%)
    all_to_all x4, blocking collectives, body(): swap(sent, 'row')  88.8 us
    pallas_call x7, Pallas kernels, call(): pl.pallas_call(kernel, out_shape=[place(shape, jnp.float32) for shape, pl...  14.8 us
    all_to_all x1, blocking collectives, body(): swap(grads, 'sec')  12.9 us
    ppermute x3, starting transfers between devices, body(): slices.append(lax.ppermute(index_slices, 'sec', pairs))  6.33 us
  transfers between devices with their start and end apart: 3, of which 1 were waited for; matrix products, arithmetic and copies ran while one was open for 1% of the time, Pallas kernels for 2%

profile of v5, /device:TPU:1, one launch (start us, length us, event | category | flops | bytes accessed | tf_op | source)
XLA Modules:
  0.0 124.0 jit_solution(677651067561469958)
XLA Ops:
  0.0 0.0 copy-start
  0.0 0.0 copy-start.1
  0.0 0.0 copy-start.2
  0.0 0.0 copy-start.3
  0.0 3.7 %collective-permute-start.1 = (f32[1,32,1024]{2,1,0:T(8,128)}, f32[1,32,1024]{2,1,0:T(8,128)S(1)}, u32[]{:S(2)}, u32[]{:S(2)}) collective-permute-start(f32[1,32,1024]{2,1,0:T(8,128)} %slice_0.1), channel_id=1, source_target_pairs={{0,64},{32,96},{64,0},{96,32},{1,65},{33,97},{65,1},{97,33},{2,66}... | collective-permute-start | bytes 393224 | tf_op jit(solution)/shard_map/ppermute | solution.py:519
  3.7 0.3 collective-permute-start
  4.0 2.4 %collective-permute-start.2 = (f32[1,32,1024]{2,1,0:T(8,128)}, f32[1,32,1024]{2,1,0:T(8,128)S(1)}, u32[]{:S(2)}, u32[]{:S(2)}) collective-permute-start(f32[1,32,1024]{2,1,0:T(8,128)} %slice_0.1), channel_id=1, source_target_pairs={{0,96},{32,0},{64,32},{96,64},{1,97},{33,1},{65,33},{97,65},{2,98}... | collective-permute-start | bytes 393224 | tf_op jit(solution)/shard_map/ppermute | solution.py:519
  6.3 0.7 pad_add_fusion.place_ref
  7.1 2.5 %shard_map.82 = (f32[32,32,128]{2,1,0:T(8,128)S(1)}, f32[2,2,32,1024]{3,2,1,0:T(8,128)S(1)}, f32[9,8,128]{2,1,0:T(8,128)S(1)}) custom-call(s32[18]{0:T(128)S(1)} %pad_add_fusion.place_ref, f32[32,1024]{1,0:T(8,128)} %illum_hbm.1, bf16[256,256]{1,0:T(8,128)(2,1)} %constant.13.clone.high_hbm.high_ref, bf16[256,256]{1,0:T(8,128)(2,1)} %constant.14.clone.low_hbm.low_ref, ...), custom_call_target="tpu_custom_call" | custom-call | tf_op jit(solution)/shard_map/pallas_call | solution.py:482
  9.7 0.0 collective-permute-done.1.slice_2
  9.7 0.4 collective-permute-done.slice_1
  10.1 0.0 collective-permute-done.2.slice_3
  10.1 0.0 copy-done
  10.1 0.0 copy-done.1
  10.1 0.0 copy-done.2
  10.1 0.0 copy-done.3
  10.1 1.3 %shard_map.83 = (f32[32,80,128]{2,1,0:T(8,128)S(1)}, f32[32,1024]{1,0:T(8,128)S(1)}, f32[2,8,2,32,128]{4,3,2,1,0:T(8,128)S(1)}) custom-call(f32[9,8,128]{2,1,0:T(8,128)S(1)} %get-tuple-element.17.constants_ref, f32[32,32,128]{2,1,0:T(8,128)S(1)} %get-tuple-element.18.launched_ref, f32[1,32,1024]{2,1,0:T(8,128)S(1)} %copy-done.2, ...), custom_call_target="tpu_custom_call" | custom-call | tf_op jit(solution)/shard_map/pallas_call | solution.py:482
  11.4 29.7 %all_to_all.25.in_ref = f32[32,80,128]{2,1,0:T(8,128)S(1)} all-to-all(f32[32,80,128]{2,1,0:T(8,128)S(1)} %get-tuple-element.20), channel_id=1, replica_groups=mesh['sec'=4,'row'=32] {'row'}, dimensions={0} | all-to-all | bytes 2621440 | tf_op jit(solution)/shard_map/all_to_all | solution.py:537
  41.2 3.6 %shard_map.84 = (f32[32,64,128]{2,1,0:T(8,128)S(1)}, f32[2,8,2,32,128]{4,3,2,1,0:T(8,128)S(1)}, f32[2,8,2,32,128]{4,3,2,1,0:T(8,128)S(1)}, f32[2,8,2,32,128]{4,3,2,1,0:T(8,128)S(1)}) custom-call(f32[9,8,128]{2,1,0:T(8,128)S(1)} %get-tuple-element.17.constants_ref, f32[32,80,128]{2,1,0:T(8,128)S(1)} %all_to_all.25.in_ref, bf16[256,256]{1,0:T(8,128)(2,1)S(1)} %copy-done.1, ...), custom_call_target="tpu_custom_call" | custom-call | tf_op jit(solution)/shard_map/pallas_call | solution.py:482
  44.7 20.4 %all_to_all.26.in_ref = f32[32,64,128]{2,1,0:T(8,128)S(1)} all-to-all(f32[32,64,128]{2,1,0:T(8,128)S(1)} %get-tuple-element.21), channel_id=1, replica_groups=mesh['sec'=4,'row'=32] {'row'}, dimensions={0} | all-to-all | bytes 2097152 | tf_op jit(solution)/shard_map/all_to_all | solution.py:540
  65.1 3.2 %shard_map.85 = (f32[32,64,128]{2,1,0:T(8,128)S(1)}, f32[32,1024]{1,0:T(8,128)S(1)}) custom-call(f32[9,8,128]{2,1,0:T(8,128)S(1)} %get-tuple-element.17.constants_ref, f32[32,64,128]{2,1,0:T(8,128)S(1)} %all_to_all.26.in_ref, bf16[256,256]{1,0:T(8,128)(2,1)S(1)} %copy-done.1, bf16[256,256]{1,0:T(8,128)(2,1)S(1)} %copy-done, ...), custom_call_target="tpu_custom_call" | custom-call | tf_op jit(solution)/shard_map/pallas_call | solution.py:482
  68.3 20.7 %all_to_all.27.in_ref = f32[32,64,128]{2,1,0:T(8,128)S(1)} all-to-all(f32[32,64,128]{2,1,0:T(8,128)S(1)} %get-tuple-element.23), channel_id=1, replica_groups=mesh['sec'=4,'row'=32] {'row'}, dimensions={0} | all-to-all | bytes 2097152 | tf_op jit(solution)/shard_map/all_to_all | solution.py:545
  89.0 2.4 %shard_map.86 = f32[32,48,128]{2,1,0:T(8,128)S(1)} custom-call(f32[9,8,128]{2,1,0:T(8,128)S(1)} %get-tuple-element.17.constants_ref, f32[32,64,128]{2,1,0:T(8,128)S(1)} %all_to_all.27.in_ref, bf16[256,256]{1,0:T(8,128)(2,1)S(1)} %copy-done.1, bf16[256,256]{1,0:T(8,128)(2,1)S(1)} %copy-done, f32[2,8,2,32,128]{4,3,2,1,0:T(8,128)S(1)} %get-tuple-element.24.field_ref, ...), custom_call_target="tpu_custom_call" | custom-call | tf_op jit(solution)/shard_map/pallas_call | solution.py:482
  91.4 18.0 %all_to_all.28.in_ref = f32[32,48,128]{2,1,0:T(8,128)S(1)} all-to-all(f32[32,48,128]{2,1,0:T(8,128)S(1)} %shard_map.86), channel_id=1, replica_groups=mesh['sec'=4,'row'=32] {'row'}, dimensions={0} | all-to-all | bytes 1572864 | tf_op jit(solution)/shard_map/all_to_all | solution.py:552
  109.4 1.0 shard_map.87
  110.5 12.9 %all_to_all.29.in_ref = f32[4,32,1024]{2,1,0:T(8,128)S(1)} all-to-all(f32[4,32,1024]{2,1,0:T(8,128)S(1)} %shard_map.87), channel_id=1, replica_groups=mesh['sec'=4,'row'=32] {'sec'}, dimensions={0} | all-to-all | bytes 1048576 | tf_op jit(solution)/shard_map/all_to_all | solution.py:556
  123.3 0.7 shard_map.88
Async XLA Ops:
  0.0 10.1 %copy-start = (bf16[256,256]{1,0:T(8,128)(2,1)S(1)}, bf16[256,256]{1,0:T(8,128)(2,1)}, u32[]{:S(2)}) copy-start(bf16[256,256]{1,0:T(8,128)(2,1)} %constant.14.clone.low_hbm.low_ref) | copy-start | bytes 393220
  0.0 10.1 %copy-start.1 = (bf16[256,256]{1,0:T(8,128)(2,1)S(1)}, bf16[256,256]{1,0:T(8,128)(2,1)}, u32[]{:S(2)}) copy-start(bf16[256,256]{1,0:T(8,128)(2,1)} %constant.13.clone.high_hbm.high_ref) | copy-start | bytes 393220
  0.0 10.1 %copy-start.2 = (f32[1,32,1024]{2,1,0:T(8,128)S(1)}, f32[1,32,1024]{2,1,0:T(8,128)}, u32[]{:S(2)}) copy-start(f32[1,32,1024]{2,1,0:T(8,128)} %slice_0.1) | copy-start | bytes 393220
  0.0 10.1 %copy-start.3 = (s32[32,1024]{1,0:T(8,128)S(1)}, s32[32,1024]{1,0:T(8,128)}, u32[]{:S(2)}) copy-start(s32[32,1024]{1,0:T(8,128)} %mask_ref.1) | copy-start | bytes 393220
  0.0 9.6 %collective-permute-start.1 = (f32[1,32,1024]{2,1,0:T(8,128)}, f32[1,32,1024]{2,1,0:T(8,128)S(1)}, u32[]{:S(2)}, u32[]{:S(2)}) collective-permute-start(f32[1,32,1024]{2,1,0:T(8,128)} %slice_0.1), channel_id=1, source_target_pairs={{0,64},{32,96},{64,0},{96,32},{1,65},{33,97},{65,1},{97,33},{2,66}... | collective-permute-start | bytes 393224 | tf_op jit(solution)/shard_map/ppermute | solution.py:519
  3.7 6.4 %collective-permute-start = (f32[1,32,1024]{2,1,0:T(8,128)}, f32[1,32,1024]{2,1,0:T(8,128)S(1)}, u32[]{:S(2)}, u32[]{:S(2)}) collective-permute-start(f32[1,32,1024]{2,1,0:T(8,128)} %slice_0.1), channel_id=1, source_target_pairs={{0,32},{32,64},{64,96},{96,0},{1,33},{33,65},{65,97},{97,1},{2,34}... | collective-permute-start | bytes 393224 | tf_op jit(solution)/shard_map/ppermute | solution.py:519
  4.0 6.1 %collective-permute-start.2 = (f32[1,32,1024]{2,1,0:T(8,128)}, f32[1,32,1024]{2,1,0:T(8,128)S(1)}, u32[]{:S(2)}, u32[]{:S(2)}) collective-permute-start(f32[1,32,1024]{2,1,0:T(8,128)} %slice_0.1), channel_id=1, source_target_pairs={{0,96},{32,0},{64,32},{96,64},{1,97},{33,1},{65,33},{97,65},{2,98}... | collective-permute-start | bytes 393224 | tf_op jit(solution)/shard_map/ppermute | solution.py:519

commit v6 on v5

--- a/solution.py
+++ b/solution.py
@@ -454,22 +454,25 @@
     store_planes(out_ref, WIDE, (gradient(target, kept(field_ref), constants), grad_2))
 
 
-def last_kernel(constants_ref, in_ref, high_ref, low_ref, screen_ref, target_ref, first_ref, out_ref):
+def last_kernel(constants_ref, in_ref, high_ref, low_ref, screen_ref, target_ref, first_ref, *out_refs):
     constants = Constants(constants_ref, high_ref, low_ref)
     field = constants.along(load_field(in_ref, 0), 1)
     field = each(times, field, kept(screen_ref))
     grad_0, grad_2 = load_planes(in_ref, WIDE)
     planes = [grad_0, planes_of(first_ref), grad_2, gradient(target_of(target_ref), field, constants)]
-    for layer, plane in enumerate(planes):
+    section = constants_ref[3 * SHARE + 2][:1]
+    for place, out_ref in enumerate(out_refs):
+        layer = section + float(place)
+        layer = jnp.where(layer > 3.0, layer - 4.0, layer)
         for group in range(GROUPS):
-            out_ref[layer, :, lanes_of(group)] = plane[group]
-
-
-def sum_kernel(in_ref, out_ref):
-    total = in_ref[0]
-    for section in range(1, in_ref.shape[0]):
-        total = total + in_ref[section]
-    out_ref[0] = total
+            value = planes[0][group]
+            for number in range(1, 4):
+                value = jnp.where(layer == float(number), planes[number][group], value)
+            out_ref[0, :, lanes_of(group)] = value
+
+
+def sum_kernel(own_ref, one_ref, two_ref, three_ref, out_ref):
+    out_ref[...] = (own_ref[...] + one_ref[...]) + (two_ref[...] + three_ref[...])
 
 
 def call(kernel, scalars, near, far, outs, scratch=(), moves=1):
@@ -546,14 +549,17 @@
         (),
         (blocks(WIDE + 16),),
     )
-    (grads,) = call(
+    grads = call(
         last_kernel,
         (),
         (constants, swap(sent, "row"), *tables, screen_3, target, grad_1),
         (),
-        (free((sec_count, *plane)),),
-    )
-    (result,) = call(sum_kernel, (), (swap(grads, "sec"),), (), (free((1, *plane)),))
+        (free((1, *plane)),) * sec_count,
+    )
+    parts = [grads[0]]
+    for on in range(1, sec_count):
+        parts.append(lax.ppermute(grads[on], "sec", [(i, (i + on) % sec_count) for i in range(sec_count)]))
+    (result,) = call(sum_kernel, (), parts, (), (free((1, *plane)),))
     return result
 
 

time: 124 us -> 122 us (0.984)
  blocking collectives: 102 us -> 88.8 us
  waiting for transfers between devices: 0.42 us -> 6.96 us
  starting transfers between devices: 6.33 us -> 10.2 us
    all_to_all x1 -> x0, blocking collectives: 12.9 us -> none  [body(): swap(grads, 'sec')]
    ppermute x0 -> x3, waiting for transfers between devices: none -> 6.54 us  [body(): lax.ppermute(grads[on], 'sec', [(i, (i + on) % sec_count) for i in range(...]
    ppermute x0 -> x3, starting transfers between devices: none -> 3.88 us  [body(): lax.ppermute(grads[on], 'sec', [(i, (i + on) % sec_count) for i in range(...]
  transfers between devices with their start and end apart: 3 -> 6, of which waited for: 1 -> 3; matrix products, arithmetic and copies ran while one was open for 1% -> 1% of each run, Pallas kernels for 2% -> 2%
where the time goes in v6:
time: 122 us
  blocking collectives  88.8 us (73%)
  Pallas kernels  14.8 us (12%)
  starting transfers between devices  10.2 us (8%)
  waiting for transfers between devices  6.96 us (6%)
    all_to_all x4, blocking collectives, body(): swap(sent, 'row')  88.8 us
    pallas_call x7, Pallas kernels, call(): pl.pallas_call(kernel, out_shape=[place(shape, jnp.float32) for shape, pl...  14.8 us
    ppermute x3, waiting for transfers between devices, body(): lax.ppermute(grads[on], 'sec', [(i, (i + on) % sec_count) for i in range(...  6.54 us
    ppermute x3, starting transfers between devices, body(): slices.append(lax.ppermute(index_slices, 'sec', pairs))  6.33 us
    ppermute x3, starting transfers between devices, body(): lax.ppermute(grads[on], 'sec', [(i, (i + on) % sec_count) for i in range(...  3.88 us
  transfers between devices with their start and end apart: 6, of which 3 were waited for; matrix products, arithmetic and copies ran while one was open for 1% of the time, Pallas kernels for 2%

profile of v6, /device:TPU:1, one launch (start us, length us, event | category | flops | bytes accessed | tf_op | source)
XLA Modules:
  0.0 121.6 jit_solution(11222605679013220409)
XLA Ops:
  0.0 0.0 copy-start
  0.0 0.0 copy-start.1
  0.0 0.0 copy-start.2
  0.0 0.0 copy-start.3
  0.0 3.7 %collective-permute-start.1 = (f32[1,32,1024]{2,1,0:T(8,128)}, f32[1,32,1024]{2,1,0:T(8,128)S(1)}, u32[]{:S(2)}, u32[]{:S(2)}) collective-permute-start(f32[1,32,1024]{2,1,0:T(8,128)} %slice_0.1), channel_id=1, source_target_pairs={{0,64},{32,96},{64,0},{96,32},{1,65},{33,97},{65,1},{97,33},{2,66}... | collective-permute-start | bytes 393224 | tf_op jit(solution)/shard_map/ppermute | solution.py:522
  3.7 0.3 collective-permute-start
  4.0 2.4 %collective-permute-start.2 = (f32[1,32,1024]{2,1,0:T(8,128)}, f32[1,32,1024]{2,1,0:T(8,128)S(1)}, u32[]{:S(2)}, u32[]{:S(2)}) collective-permute-start(f32[1,32,1024]{2,1,0:T(8,128)} %slice_0.1), channel_id=1, source_target_pairs={{0,96},{32,0},{64,32},{96,64},{1,97},{33,1},{65,33},{97,65},{2,98}... | collective-permute-start | bytes 393224 | tf_op jit(solution)/shard_map/ppermute | solution.py:522
  6.3 0.7 pad_add_fusion.place_ref
  7.1 2.5 %shard_map.82 = (f32[32,32,128]{2,1,0:T(8,128)S(1)}, f32[2,2,32,1024]{3,2,1,0:T(8,128)S(1)}, f32[9,8,128]{2,1,0:T(8,128)S(1)}) custom-call(s32[18]{0:T(128)S(1)} %pad_add_fusion.place_ref, f32[32,1024]{1,0:T(8,128)} %illum_hbm.1, bf16[256,256]{1,0:T(8,128)(2,1)} %constant.13.clone.high_hbm.high_ref, bf16[256,256]{1,0:T(8,128)(2,1)} %constant.14.clone.low_hbm.low_ref, ...), custom_call_target="tpu_custom_call" | custom-call | tf_op jit(solution)/shard_map/pallas_call | solution.py:485
  9.7 0.0 collective-permute-done.1.slice_2
  9.7 0.4 collective-permute-done.slice_1
  10.1 0.0 collective-permute-done.2.slice_3
  10.1 0.0 copy-done
  10.1 0.0 copy-done.1
  10.1 0.0 copy-done.2
  10.1 0.0 copy-done.3
  10.1 1.3 %shard_map.83 = (f32[32,80,128]{2,1,0:T(8,128)S(1)}, f32[32,1024]{1,0:T(8,128)S(1)}, f32[2,8,2,32,128]{4,3,2,1,0:T(8,128)S(1)}) custom-call(f32[9,8,128]{2,1,0:T(8,128)S(1)} %get-tuple-element.21.constants_ref, f32[32,32,128]{2,1,0:T(8,128)S(1)} %get-tuple-element.22.launched_ref, f32[1,32,1024]{2,1,0:T(8,128)S(1)} %copy-done.2, ...), custom_call_target="tpu_custom_call" | custom-call | tf_op jit(solution)/shard_map/pallas_call | solution.py:485
  11.4 29.7 %all_to_all.20.in_ref = f32[32,80,128]{2,1,0:T(8,128)S(1)} all-to-all(f32[32,80,128]{2,1,0:T(8,128)S(1)} %get-tuple-element.24), channel_id=1, replica_groups=mesh['sec'=4,'row'=32] {'row'}, dimensions={0} | all-to-all | bytes 2621440 | tf_op jit(solution)/shard_map/all_to_all | solution.py:540
  41.2 3.6 %shard_map.84 = (f32[32,64,128]{2,1,0:T(8,128)S(1)}, f32[2,8,2,32,128]{4,3,2,1,0:T(8,128)S(1)}, f32[2,8,2,32,128]{4,3,2,1,0:T(8,128)S(1)}, f32[2,8,2,32,128]{4,3,2,1,0:T(8,128)S(1)}) custom-call(f32[9,8,128]{2,1,0:T(8,128)S(1)} %get-tuple-element.21.constants_ref, f32[32,80,128]{2,1,0:T(8,128)S(1)} %all_to_all.20.in_ref, bf16[256,256]{1,0:T(8,128)(2,1)S(1)} %copy-done.1, ...), custom_call_target="tpu_custom_call" | custom-call | tf_op jit(solution)/shard_map/pallas_call | solution.py:485
  44.7 20.4 %all_to_all.21.in_ref = f32[32,64,128]{2,1,0:T(8,128)S(1)} all-to-all(f32[32,64,128]{2,1,0:T(8,128)S(1)} %get-tuple-element.25), channel_id=1, replica_groups=mesh['sec'=4,'row'=32] {'row'}, dimensions={0} | all-to-all | bytes 2097152 | tf_op jit(solution)/shard_map/all_to_all | solution.py:543
  65.1 3.2 %shard_map.85 = (f32[32,64,128]{2,1,0:T(8,128)S(1)}, f32[32,1024]{1,0:T(8,128)S(1)}) custom-call(f32[9,8,128]{2,1,0:T(8,128)S(1)} %get-tuple-element.21.constants_ref, f32[32,64,128]{2,1,0:T(8,128)S(1)} %all_to_all.21.in_ref, bf16[256,256]{1,0:T(8,128)(2,1)S(1)} %copy-done.1, bf16[256,256]{1,0:T(8,128)(2,1)S(1)} %copy-done, ...), custom_call_target="tpu_custom_call" | custom-call | tf_op jit(solution)/shard_map/pallas_call | solution.py:485
  68.3 20.7 %all_to_all.22.in_ref = f32[32,64,128]{2,1,0:T(8,128)S(1)} all-to-all(f32[32,64,128]{2,1,0:T(8,128)S(1)} %get-tuple-element.27), channel_id=1, replica_groups=mesh['sec'=4,'row'=32] {'row'}, dimensions={0} | all-to-all | bytes 2097152 | tf_op jit(solution)/shard_map/all_to_all | solution.py:548
  89.0 2.4 %shard_map.86 = f32[32,48,128]{2,1,0:T(8,128)S(1)} custom-call(f32[9,8,128]{2,1,0:T(8,128)S(1)} %get-tuple-element.21.constants_ref, f32[32,64,128]{2,1,0:T(8,128)S(1)} %all_to_all.22.in_ref, bf16[256,256]{1,0:T(8,128)(2,1)S(1)} %copy-done.1, bf16[256,256]{1,0:T(8,128)(2,1)S(1)} %copy-done, f32[2,8,2,32,128]{4,3,2,1,0:T(8,128)S(1)} %get-tuple-element.28.field_ref, ...), custom_call_target="tpu_custom_call" | custom-call | tf_op jit(solution)/shard_map/pallas_call | solution.py:485
  91.4 18.0 %all_to_all.23.in_ref = f32[32,48,128]{2,1,0:T(8,128)S(1)} all-to-all(f32[32,48,128]{2,1,0:T(8,128)S(1)} %shard_map.86), channel_id=1, replica_groups=mesh['sec'=4,'row'=32] {'row'}, dimensions={0} | all-to-all | bytes 1572864 | tf_op jit(solution)/shard_map/all_to_all | solution.py:555
  109.4 1.1 shard_map.87
  110.5 1.0 collective-permute-start.3
  111.6 2.9 %collective-permute-start.4 = (f32[1,32,1024]{2,1,0:T(8,128)S(1)}, f32[1,32,1024]{2,1,0:T(8,128)S(1)}, u32[]{:S(2)}, u32[]{:S(2)}) collective-permute-start(f32[1,32,1024]{2,1,0:T(8,128)S(1)} %get-tuple-element.35), channel_id=1, source_target_pairs={{0,64},{32,96},{64,0},{96,32},{1,65},{33,97},{65,1},{97,33},{2,66}... | collective-permute-start | bytes 393224 | tf_op jit(solution)/shard_map/ppermute | solution.py:561
  114.4 0.0 collective-permute-start.5
  114.4 2.6 %collective-permute-done.3.one_ref = f32[1,32,1024]{2,1,0:T(8,128)S(1)} collective-permute-done((f32[1,32,1024]{2,1,0:T(8,128)S(1)}, f32[1,32,1024]{2,1,0:T(8,128)S(1)}, u32[]{:S(2)}, u32[]{:S(2)}) %collective-permute-start.3) | collective-permute-done | bytes 131104 | tf_op jit(solution)/shard_map/ppermute | solution.py:561
  117.0 3.9 %collective-permute-done.4.two_ref = f32[1,32,1024]{2,1,0:T(8,128)S(1)} collective-permute-done((f32[1,32,1024]{2,1,0:T(8,128)S(1)}, f32[1,32,1024]{2,1,0:T(8,128)S(1)}, u32[]{:S(2)}, u32[]{:S(2)}) %collective-permute-start.4) | collective-permute-done | bytes 131104 | tf_op jit(solution)/shard_map/ppermute | solution.py:561
  121.0 0.0 collective-permute-done.5.three_ref
  121.0 0.7 shard_map.88
Async XLA Ops:
  0.0 10.1 %copy-start = (bf16[256,256]{1,0:T(8,128)(2,1)S(1)}, bf16[256,256]{1,0:T(8,128)(2,1)}, u32[]{:S(2)}) copy-start(bf16[256,256]{1,0:T(8,128)(2,1)} %constant.14.clone.low_hbm.low_ref) | copy-start | bytes 393220
  0.0 10.1 %copy-start.1 = (bf16[256,256]{1,0:T(8,128)(2,1)S(1)}, bf16[256,256]{1,0:T(8,128)(2,1)}, u32[]{:S(2)}) copy-start(bf16[256,256]{1,0:T(8,128)(2,1)} %constant.13.clone.high_hbm.high_ref) | copy-start | bytes 393220
  0.0 10.1 %copy-start.2 = (f32[1,32,1024]{2,1,0:T(8,128)S(1)}, f32[1,32,1024]{2,1,0:T(8,128)}, u32[]{:S(2)}) copy-start(f32[1,32,1024]{2,1,0:T(8,128)} %slice_0.1) | copy-start | bytes 393220
  0.0 10.1 %copy-start.3 = (s32[32,1024]{1,0:T(8,128)S(1)}, s32[32,1024]{1,0:T(8,128)}, u32[]{:S(2)}) copy-start(s32[32,1024]{1,0:T(8,128)} %mask_ref.1) | copy-start | bytes 393220
  0.0 9.6 %collective-permute-start.1 = (f32[1,32,1024]{2,1,0:T(8,128)}, f32[1,32,1024]{2,1,0:T(8,128)S(1)}, u32[]{:S(2)}, u32[]{:S(2)}) collective-permute-start(f32[1,32,1024]{2,1,0:T(8,128)} %slice_0.1), channel_id=1, source_target_pairs={{0,64},{32,96},{64,0},{96,32},{1,65},{33,97},{65,1},{97,33},{2,66}... | collective-permute-start | bytes 393224 | tf_op jit(solution)/shard_map/ppermute | solution.py:522
  3.7 6.4 %collective-permute-start = (f32[1,32,1024]{2,1,0:T(8,128)}, f32[1,32,1024]{2,1,0:T(8,128)S(1)}, u32[]{:S(2)}, u32[]{:S(2)}) collective-permute-start(f32[1,32,1024]{2,1,0:T(8,128)} %slice_0.1), channel_id=1, source_target_pairs={{0,32},{32,64},{64,96},{96,0},{1,33},{33,65},{65,97},{97,1},{2,34}... | collective-permute-start | bytes 393224 | tf_op jit(solution)/shard_map/ppermute | solution.py:522
  4.0 6.1 %collective-permute-start.2 = (f32[1,32,1024]{2,1,0:T(8,128)}, f32[1,32,1024]{2,1,0:T(8,128)S(1)}, u32[]{:S(2)}, u32[]{:S(2)}) collective-permute-start(f32[1,32,1024]{2,1,0:T(8,128)} %slice_0.1), channel_id=1, source_target_pairs={{0,96},{32,0},{64,32},{96,64},{1,97},{33,1},{65,33},{97,65},{2,98}... | collective-permute-start | bytes 393224 | tf_op jit(solution)/shard_map/ppermute | solution.py:522
  110.5 6.5 %collective-permute-start.3 = (f32[1,32,1024]{2,1,0:T(8,128)S(1)}, f32[1,32,1024]{2,1,0:T(8,128)S(1)}, u32[]{:S(2)}, u32[]{:S(2)}) collective-permute-start(f32[1,32,1024]{2,1,0:T(8,128)S(1)} %get-tuple-element.34), channel_id=1, source_target_pairs={{0,32},{32,64},{64,96},{96,0},{1,33},{33,65},{65,97},{97,1},{2,34}... | collective-permute-start | bytes 393224 | tf_op jit(solution)/shard_map/ppermute | solution.py:561
  111.6 9.4 %collective-permute-start.4 = (f32[1,32,1024]{2,1,0:T(8,128)S(1)}, f32[1,32,1024]{2,1,0:T(8,128)S(1)}, u32[]{:S(2)}, u32[]{:S(2)}) collective-permute-start(f32[1,32,1024]{2,1,0:T(8,128)S(1)} %get-tuple-element.35), channel_id=1, source_target_pairs={{0,64},{32,96},{64,0},{96,32},{1,65},{33,97},{65,1},{97,33},{2,66}... | collective-permute-start | bytes 393224 | tf_op jit(solution)/shard_map/ppermute | solution.py:561
  114.4 6.5 %collective-permute-start.5 = (f32[1,32,1024]{2,1,0:T(8,128)S(1)}, f32[1,32,1024]{2,1,0:T(8,128)S(1)}, u32[]{:S(2)}, u32[]{:S(2)}) collective-permute-start(f32[1,32,1024]{2,1,0:T(8,128)S(1)} %get-tuple-element.36), channel_id=1, source_target_pairs={{0,96},{32,0},{64,32},{96,64},{1,97},{33,1},{65,33},{97,65},{2,98}... | collective-permute-start | bytes 393224 | tf_op jit(solution)/shard_map/ppermute | solution.py:561

commit v7 on v6

--- a/solution.py
+++ b/solution.py
@@ -557,7 +557,7 @@
         (free((1, *plane)),) * sec_count,
     )
     parts = [grads[0]]
-    for on in range(1, sec_count):
+    for on in (2, 1, 3):
         parts.append(lax.ppermute(grads[on], "sec", [(i, (i + on) % sec_count) for i in range(sec_count)]))
     (result,) = call(sum_kernel, (), parts, (), (free((1, *plane)),))
     return result

time: 122 us -> 121 us (level)
  no operation moved by 1% of the time
where the time goes in v7:
time: 121 us
  blocking collectives  88.8 us (73%)
  Pallas kernels  14.8 us (12%)
  starting transfers between devices  10.7 us (9%)
  waiting for transfers between devices  5.95 us (5%)
    all_to_all x4, blocking collectives, body(): swap(sent, 'row')  88.8 us
    pallas_call x7, Pallas kernels, call(): pl.pallas_call(kernel, out_shape=[place(shape, jnp.float32) for shape, pl...  14.8 us
    ppermute x3, starting transfers between devices, body(): slices.append(lax.ppermute(index_slices, 'sec', pairs))  6.33 us
    ppermute x3, waiting for transfers between devices, body(): lax.ppermute(grads[on], 'sec', [(i, (i + on) % sec_count) for i in range(...  5.53 us
    ppermute x3, starting transfers between devices, body(): lax.ppermute(grads[on], 'sec', [(i, (i + on) % sec_count) for i in range(...  4.32 us
  transfers between devices with their start and end apart: 6, of which 3 were waited for; matrix products, arithmetic and copies ran while one was open for 1% of the time, Pallas kernels for 2%

profile of v7, /device:TPU:1, one launch (start us, length us, event | category | flops | bytes accessed | tf_op | source)
XLA Modules:
  0.0 121.1 jit_solution(13935467547658727076)
XLA Ops:
  0.0 0.0 copy-start
  0.0 0.0 copy-start.1
  0.0 0.0 copy-start.2
  0.0 0.0 copy-start.3
  0.0 3.7 %collective-permute-start.1 = (f32[1,32,1024]{2,1,0:T(8,128)}, f32[1,32,1024]{2,1,0:T(8,128)S(1)}, u32[]{:S(2)}, u32[]{:S(2)}) collective-permute-start(f32[1,32,1024]{2,1,0:T(8,128)} %slice_0.1), channel_id=1, source_target_pairs={{0,64},{32,96},{64,0},{96,32},{1,65},{33,97},{65,1},{97,33},{2,66}... | collective-permute-start | bytes 393224 | tf_op jit(solution)/shard_map/ppermute | solution.py:522
  3.7 0.3 collective-permute-start
  4.0 2.4 %collective-permute-start.2 = (f32[1,32,1024]{2,1,0:T(8,128)}, f32[1,32,1024]{2,1,0:T(8,128)S(1)}, u32[]{:S(2)}, u32[]{:S(2)}) collective-permute-start(f32[1,32,1024]{2,1,0:T(8,128)} %slice_0.1), channel_id=1, source_target_pairs={{0,96},{32,0},{64,32},{96,64},{1,97},{33,1},{65,33},{97,65},{2,98}... | collective-permute-start | bytes 393224 | tf_op jit(solution)/shard_map/ppermute | solution.py:522
  6.3 0.7 pad_add_fusion.place_ref
  7.1 2.5 %shard_map.82 = (f32[32,32,128]{2,1,0:T(8,128)S(1)}, f32[2,2,32,1024]{3,2,1,0:T(8,128)S(1)}, f32[9,8,128]{2,1,0:T(8,128)S(1)}) custom-call(s32[18]{0:T(128)S(1)} %pad_add_fusion.place_ref, f32[32,1024]{1,0:T(8,128)} %illum_hbm.1, bf16[256,256]{1,0:T(8,128)(2,1)} %constant.13.clone.high_hbm.high_ref, bf16[256,256]{1,0:T(8,128)(2,1)} %constant.14.clone.low_hbm.low_ref, ...), custom_call_target="tpu_custom_call" | custom-call | tf_op jit(solution)/shard_map/pallas_call | solution.py:485
  9.7 0.0 collective-permute-done.1.slice_2
  9.7 0.4 collective-permute-done.slice_1
  10.1 0.0 collective-permute-done.2.slice_3
  10.1 0.0 copy-done
  10.1 0.0 copy-done.1
  10.1 0.0 copy-done.2
  10.1 0.0 copy-done.3
  10.1 1.3 %shard_map.83 = (f32[32,80,128]{2,1,0:T(8,128)S(1)}, f32[32,1024]{1,0:T(8,128)S(1)}, f32[2,8,2,32,128]{4,3,2,1,0:T(8,128)S(1)}) custom-call(f32[9,8,128]{2,1,0:T(8,128)S(1)} %get-tuple-element.21.constants_ref, f32[32,32,128]{2,1,0:T(8,128)S(1)} %get-tuple-element.22.launched_ref, f32[1,32,1024]{2,1,0:T(8,128)S(1)} %copy-done.2, ...), custom_call_target="tpu_custom_call" | custom-call | tf_op jit(solution)/shard_map/pallas_call | solution.py:485
  11.4 29.7 %all_to_all.20.in_ref = f32[32,80,128]{2,1,0:T(8,128)S(1)} all-to-all(f32[32,80,128]{2,1,0:T(8,128)S(1)} %get-tuple-element.24), channel_id=1, replica_groups=mesh['sec'=4,'row'=32] {'row'}, dimensions={0} | all-to-all | bytes 2621440 | tf_op jit(solution)/shard_map/all_to_all | solution.py:540
  41.2 3.6 %shard_map.84 = (f32[32,64,128]{2,1,0:T(8,128)S(1)}, f32[2,8,2,32,128]{4,3,2,1,0:T(8,128)S(1)}, f32[2,8,2,32,128]{4,3,2,1,0:T(8,128)S(1)}, f32[2,8,2,32,128]{4,3,2,1,0:T(8,128)S(1)}) custom-call(f32[9,8,128]{2,1,0:T(8,128)S(1)} %get-tuple-element.21.constants_ref, f32[32,80,128]{2,1,0:T(8,128)S(1)} %all_to_all.20.in_ref, bf16[256,256]{1,0:T(8,128)(2,1)S(1)} %copy-done.1, ...), custom_call_target="tpu_custom_call" | custom-call | tf_op jit(solution)/shard_map/pallas_call | solution.py:485
  44.7 20.4 %all_to_all.21.in_ref = f32[32,64,128]{2,1,0:T(8,128)S(1)} all-to-all(f32[32,64,128]{2,1,0:T(8,128)S(1)} %get-tuple-element.25), channel_id=1, replica_groups=mesh['sec'=4,'row'=32] {'row'}, dimensions={0} | all-to-all | bytes 2097152 | tf_op jit(solution)/shard_map/all_to_all | solution.py:543
  65.1 3.2 %shard_map.85 = (f32[32,64,128]{2,1,0:T(8,128)S(1)}, f32[32,1024]{1,0:T(8,128)S(1)}) custom-call(f32[9,8,128]{2,1,0:T(8,128)S(1)} %get-tuple-element.21.constants_ref, f32[32,64,128]{2,1,0:T(8,128)S(1)} %all_to_all.21.in_ref, bf16[256,256]{1,0:T(8,128)(2,1)S(1)} %copy-done.1, bf16[256,256]{1,0:T(8,128)(2,1)S(1)} %copy-done, ...), custom_call_target="tpu_custom_call" | custom-call | tf_op jit(solution)/shard_map/pallas_call | solution.py:485
  68.3 20.7 %all_to_all.22.in_ref = f32[32,64,128]{2,1,0:T(8,128)S(1)} all-to-all(f32[32,64,128]{2,1,0:T(8,128)S(1)} %get-tuple-element.27), channel_id=1, replica_groups=mesh['sec'=4,'row'=32] {'row'}, dimensions={0} | all-to-all | bytes 2097152 | tf_op jit(solution)/shard_map/all_to_all | solution.py:548
  89.0 2.4 %shard_map.86 = f32[32,48,128]{2,1,0:T(8,128)S(1)} custom-call(f32[9,8,128]{2,1,0:T(8,128)S(1)} %get-tuple-element.21.constants_ref, f32[32,64,128]{2,1,0:T(8,128)S(1)} %all_to_all.22.in_ref, bf16[256,256]{1,0:T(8,128)(2,1)S(1)} %copy-done.1, bf16[256,256]{1,0:T(8,128)(2,1)S(1)} %copy-done, f32[2,8,2,32,128]{4,3,2,1,0:T(8,128)S(1)} %get-tuple-element.28.field_ref, ...), custom_call_target="tpu_custom_call" | custom-call | tf_op jit(solution)/shard_map/pallas_call | solution.py:485
  91.4 18.0 %all_to_all.23.in_ref = f32[32,48,128]{2,1,0:T(8,128)S(1)} all-to-all(f32[32,48,128]{2,1,0:T(8,128)S(1)} %shard_map.86), channel_id=1, replica_groups=mesh['sec'=4,'row'=32] {'row'}, dimensions={0} | all-to-all | bytes 1572864 | tf_op jit(solution)/shard_map/all_to_all | solution.py:555
  109.4 1.1 shard_map.87
  110.5 1.6 %collective-permute-start.3 = (f32[1,32,1024]{2,1,0:T(8,128)S(1)}, f32[1,32,1024]{2,1,0:T(8,128)S(1)}, u32[]{:S(2)}, u32[]{:S(2)}) collective-permute-start(f32[1,32,1024]{2,1,0:T(8,128)S(1)} %get-tuple-element.34), channel_id=1, source_target_pairs={{0,64},{32,96},{64,0},{96,32},{1,65},{33,97},{65,1},{97,33},{2,66}... | collective-permute-start | bytes 393224 | tf_op jit(solution)/shard_map/ppermute | solution.py:561
  112.2 1.6 %collective-permute-start.4 = (f32[1,32,1024]{2,1,0:T(8,128)S(1)}, f32[1,32,1024]{2,1,0:T(8,128)S(1)}, u32[]{:S(2)}, u32[]{:S(2)}) collective-permute-start(f32[1,32,1024]{2,1,0:T(8,128)S(1)} %get-tuple-element.35), channel_id=1, source_target_pairs={{0,32},{32,64},{64,96},{96,0},{1,33},{33,65},{65,97},{97,1},{2,34}... | collective-permute-start | bytes 393224 | tf_op jit(solution)/shard_map/ppermute | solution.py:561
  113.8 1.0 collective-permute-start.5
  114.9 2.5 %collective-permute-done.3.one_ref = f32[1,32,1024]{2,1,0:T(8,128)S(1)} collective-permute-done((f32[1,32,1024]{2,1,0:T(8,128)S(1)}, f32[1,32,1024]{2,1,0:T(8,128)S(1)}, u32[]{:S(2)}, u32[]{:S(2)}) %collective-permute-start.3) | collective-permute-done | bytes 131104 | tf_op jit(solution)/shard_map/ppermute | solution.py:561
  117.3 3.1 %collective-permute-done.4.two_ref = f32[1,32,1024]{2,1,0:T(8,128)S(1)} collective-permute-done((f32[1,32,1024]{2,1,0:T(8,128)S(1)}, f32[1,32,1024]{2,1,0:T(8,128)S(1)}, u32[]{:S(2)}, u32[]{:S(2)}) %collective-permute-start.4) | collective-permute-done | bytes 131104 | tf_op jit(solution)/shard_map/ppermute | solution.py:561
  120.4 0.0 collective-permute-done.5.three_ref
  120.4 0.7 shard_map.88
Async XLA Ops:
  0.0 10.1 %copy-start = (bf16[256,256]{1,0:T(8,128)(2,1)S(1)}, bf16[256,256]{1,0:T(8,128)(2,1)}, u32[]{:S(2)}) copy-start(bf16[256,256]{1,0:T(8,128)(2,1)} %constant.14.clone.low_hbm.low_ref) | copy-start | bytes 393220
  0.0 10.1 %copy-start.1 = (bf16[256,256]{1,0:T(8,128)(2,1)S(1)}, bf16[256,256]{1,0:T(8,128)(2,1)}, u32[]{:S(2)}) copy-start(bf16[256,256]{1,0:T(8,128)(2,1)} %constant.13.clone.high_hbm.high_ref) | copy-start | bytes 393220
  0.0 10.1 %copy-start.2 = (f32[1,32,1024]{2,1,0:T(8,128)S(1)}, f32[1,32,1024]{2,1,0:T(8,128)}, u32[]{:S(2)}) copy-start(f32[1,32,1024]{2,1,0:T(8,128)} %slice_0.1) | copy-start | bytes 393220
  0.0 10.1 %copy-start.3 = (s32[32,1024]{1,0:T(8,128)S(1)}, s32[32,1024]{1,0:T(8,128)}, u32[]{:S(2)}) copy-start(s32[32,1024]{1,0:T(8,128)} %mask_ref.1) | copy-start | bytes 393220
  0.0 9.6 %collective-permute-start.1 = (f32[1,32,1024]{2,1,0:T(8,128)}, f32[1,32,1024]{2,1,0:T(8,128)S(1)}, u32[]{:S(2)}, u32[]{:S(2)}) collective-permute-start(f32[1,32,1024]{2,1,0:T(8,128)} %slice_0.1), channel_id=1, source_target_pairs={{0,64},{32,96},{64,0},{96,32},{1,65},{33,97},{65,1},{97,33},{2,66}... | collective-permute-start | bytes 393224 | tf_op jit(solution)/shard_map/ppermute | solution.py:522
  3.7 6.4 %collective-permute-start = (f32[1,32,1024]{2,1,0:T(8,128)}, f32[1,32,1024]{2,1,0:T(8,128)S(1)}, u32[]{:S(2)}, u32[]{:S(2)}) collective-permute-start(f32[1,32,1024]{2,1,0:T(8,128)} %slice_0.1), channel_id=1, source_target_pairs={{0,32},{32,64},{64,96},{96,0},{1,33},{33,65},{65,97},{97,1},{2,34}... | collective-permute-start | bytes 393224 | tf_op jit(solution)/shard_map/ppermute | solution.py:522
  4.0 6.1 %collective-permute-start.2 = (f32[1,32,1024]{2,1,0:T(8,128)}, f32[1,32,1024]{2,1,0:T(8,128)S(1)}, u32[]{:S(2)}, u32[]{:S(2)}) collective-permute-start(f32[1,32,1024]{2,1,0:T(8,128)} %slice_0.1), channel_id=1, source_target_pairs={{0,96},{32,0},{64,32},{96,64},{1,97},{33,1},{65,33},{97,65},{2,98}... | collective-permute-start | bytes 393224 | tf_op jit(solution)/shard_map/ppermute | solution.py:522
  110.5 6.8 %collective-permute-start.3 = (f32[1,32,1024]{2,1,0:T(8,128)S(1)}, f32[1,32,1024]{2,1,0:T(8,128)S(1)}, u32[]{:S(2)}, u32[]{:S(2)}) collective-permute-start(f32[1,32,1024]{2,1,0:T(8,128)S(1)} %get-tuple-element.34), channel_id=1, source_target_pairs={{0,64},{32,96},{64,0},{96,32},{1,65},{33,97},{65,1},{97,33},{2,66}... | collective-permute-start | bytes 393224 | tf_op jit(solution)/shard_map/ppermute | solution.py:561
  112.2 8.2 %collective-permute-start.4 = (f32[1,32,1024]{2,1,0:T(8,128)S(1)}, f32[1,32,1024]{2,1,0:T(8,128)S(1)}, u32[]{:S(2)}, u32[]{:S(2)}) collective-permute-start(f32[1,32,1024]{2,1,0:T(8,128)S(1)} %get-tuple-element.35), channel_id=1, source_target_pairs={{0,32},{32,64},{64,96},{96,0},{1,33},{33,65},{65,97},{97,1},{2,34}... | collective-permute-start | bytes 393224 | tf_op jit(solution)/shard_map/ppermute | solution.py:561
  113.8 6.6 %collective-permute-start.5 = (f32[1,32,1024]{2,1,0:T(8,128)S(1)}, f32[1,32,1024]{2,1,0:T(8,128)S(1)}, u32[]{:S(2)}, u32[]{:S(2)}) collective-permute-start(f32[1,32,1024]{2,1,0:T(8,128)S(1)} %get-tuple-element.36), channel_id=1, source_target_pairs={{0,96},{32,0},{64,32},{96,64},{1,97},{33,1},{65,33},{97,65},{2,98}... | collective-permute-start | bytes 393224 | tf_op jit(solution)/shard_map/ppermute | solution.py:561
